TPU v7x, 512 devices: a whole 4x4x16 slice. The times are simulated.
512 devices in a mesh: seq: 64 (over z, x), tp: 8 (over y, core).
Axes of the slice: x: 4, y: 4, z: 16, core: 2. Of those that a mesh axis runs over, the one named last changes fastest.
Arguments:
- latent: bfloat16 [16384, 5120], P('seq', 'tp'), may hold values from -12 to 12
- pose_rows: bfloat16 [16384, 256], P('seq'), may hold values from -6 to 6
- dest_device: int32 [16384, 1], P('seq'), may hold values from 0 to 63; in each aligned block of 256 rows (0 to 255, 256 to 511, ...) at most 8 rows name the same one
- dest_slot: int32 [16384], P('seq'), may hold values from 0 to 255
- w_section1: bfloat16 [16, 32], replicated, may hold values from -1.5 to 1.5
- w_section2: bfloat16 [128, 128], replicated, may hold values from -0.5 to 0.5
- w_section3: bfloat16 [512, 5120], P(None, 'tp'), may hold values from -0.25 to 0.25
- shift_mod: float32 [5120], P('tp'), may hold values from -3 to 3
- scale_mod: float32 [5120], P('tp'), may hold values from -0.5 to 0.5
- w_query: bfloat16 [5120, 5120], P('seq', 'tp'), may hold values from -0.078125 to 0.078125
- bias_query: float32 [5120], P('tp'), may hold values from -3 to 3
- gain_query: float32 [5120], P('tp'), may hold values from 0.25 to 1.75
- cotangent: bfloat16 [16384, 5120], P('seq', 'tp'), may hold values from -16 to 16
Outputs:
- normed_query: bfloat16 [16384, 5120], P('seq', 'tp')
- section_three_grad: float32 [512, 5120], P('seq', 'tp')
- section_two_grad: float32 [128, 128], replicated
- section_one_grad: float32 [16, 32], replicated
Inputs may be any that keep to these rules, and one draw needn't show every extreme that they name: `dest_device`: among the rows of one device no index of seq appears more than 8 times, and some index appears exactly 8 times among some device's rows.
All inputs are finite; a program needn't handle non-finite values.
Results may differ from a plain program's by a relative error of at most 0.02.
Values may be sent and summed in bfloat16 or wider, within the bound.
No kernel may reach another device: no remote copies, remote signals or barrier semaphores. Data moves between devices by JAX's collectives and lax.ppermute only.
A program may use at most 64 MiB of HBM per device.

v0:
```python
import jax
import jax.numpy as jnp
from jax import lax
from jax.sharding import PartitionSpec as P

epsilon = 1e-06


def silu_slope(z):
    s = jax.nn.sigmoid(z)
    return s * (1.0 + z * (1.0 - s))


def run_sections(pose, w_one, w_two):
    count = pose.shape[0]
    c_one = w_one.shape[1]
    cells = pose.reshape(count * 16, 16)
    z_one = jnp.dot(cells, w_one, preferred_element_type=jnp.float32)
    feature_one = jax.nn.silu(z_one).astype(jnp.bfloat16)
    stacked_one = (
        feature_one.reshape(count, 2, 2, 2, 2, c_one)
        .transpose(0, 1, 3, 2, 4, 5)
        .reshape(count * 4, 4 * c_one)
    )
    z_two = jnp.dot(stacked_one, w_two, preferred_element_type=jnp.float32)
    stacked_two = jax.nn.silu(z_two).astype(jnp.bfloat16).reshape(count, 4 * w_two.shape[1])
    return (cells, z_one, stacked_one, z_two, stacked_two)


def section_back(cells, z_one, stacked_one, z_two, stacked_grad, w_two):
    quads = z_two.shape[0]
    count = quads // 4
    c_one = z_one.shape[1]
    two_grad = stacked_grad.reshape(quads, -1) * silu_slope(z_two)
    grad_two = lax.dot_general(
        stacked_one.astype(jnp.float32),
        two_grad,
        (((0,), (0,)), ((), ())),
        precision=lax.Precision.HIGHEST,
    )
    back_one = jnp.dot(two_grad, w_two.astype(jnp.float32).T, precision=lax.Precision.HIGHEST)
    back_one = (
        back_one.reshape(count, 2, 2, 2, 2, c_one)
        .transpose(0, 1, 3, 2, 4, 5)
        .reshape(count * 16, c_one)
    )
    one_grad = back_one * silu_slope(z_one)
    grad_one = lax.dot_general(
        cells.astype(jnp.float32),
        one_grad,
        (((0,), (0,)), ((), ())),
        precision=lax.Precision.HIGHEST,
    )
    return (grad_two, grad_one)


def body(
    latent,
    pose_rows,
    dest_device,
    dest_slot,
    w_section1,
    w_section2,
    w_section3,
    shift_mod,
    scale_mod,
    w_query,
    bias_query,
    gain_query,
    cotangent,
):
    tokens = latent.shape[0]
    seq_count = lax.axis_size("seq")
    tp_count = lax.axis_size("tp")
    full_width = latent.shape[1] * tp_count
    query_width = w_query.shape[1] * tp_count
    capacity = max(2, 2 * tokens // seq_count)
    slots_all = seq_count * capacity
    owner = dest_device[:, 0]
    marks = (owner[:, None] == jnp.arange(seq_count, dtype=jnp.int32)[None, :]).astype(jnp.int32)
    before = jnp.cumsum(marks, axis=0) - marks
    position = owner * capacity + jnp.sum(before * marks, axis=1)
    slot_send = (
        jnp.full((slots_all,), tokens, jnp.int32)
        .at[position]
        .set(dest_slot)
        .reshape(seq_count, capacity)
    )
    cells, z_one, stacked_one, z_two, stacked_two = run_sections(pose_rows, w_section1, w_section2)
    pose_tokens = jnp.dot(stacked_two, w_section3, preferred_element_type=jnp.float32).astype(
        jnp.bfloat16
    )
    outgoing = (
        jnp.zeros((slots_all, pose_tokens.shape[1]), jnp.bfloat16).at[position].set(pose_tokens)
    )
    incoming, slot_recv = (
        lax.all_to_all(
            outgoing.reshape(seq_count, capacity, -1),
            "seq",
            split_axis=0,
            concat_axis=0,
            tiled=True,
        ),
        lax.all_to_all(slot_send, "seq", split_axis=0, concat_axis=0, tiled=True),
    )
    incoming = incoming.reshape(slots_all, -1)
    select = (
        jnp.arange(tokens, dtype=jnp.int32)[:, None] == slot_recv.reshape(-1)[None, :]
    ).astype(jnp.bfloat16)
    guidance = jnp.dot(select, incoming, preferred_element_type=jnp.float32)
    summed = latent.astype(jnp.float32) + guidance
    total, squares = lax.psum((jnp.sum(summed, axis=1), jnp.sum(summed * summed, axis=1)), "tp")
    center = total / full_width
    inverse = lax.rsqrt(squares / full_width - center * center + epsilon)[:, None]
    normed = (summed - center[:, None]) * inverse
    modulated = (normed * (1.0 + scale_mod) + shift_mod).astype(jnp.bfloat16)
    whole = lax.all_gather(modulated, "tp", axis=1, tiled=True)
    weights_all = lax.all_gather(w_query, "seq", axis=0, tiled=True)
    query = jnp.dot(whole, weights_all, preferred_element_type=jnp.float32)
    query = query + bias_query
    upstream = cotangent.astype(jnp.float32) * gain_query
    sum_square, sum_along = lax.psum(
        (jnp.sum(query * query, axis=1), jnp.sum(upstream * query, axis=1)), "tp"
    )
    rinv = lax.rsqrt(sum_square / query_width + epsilon)[:, None]
    normed_query = (query * rinv * gain_query).astype(jnp.bfloat16)
    along = (sum_along / query_width)[:, None]
    query_grad = (upstream * rinv - query * along * rinv**3).astype(jnp.bfloat16)
    partial_grad = lax.dot_general(
        query_grad, weights_all, (((1,), (1,)), ((), ())), preferred_element_type=jnp.float32
    )
    modulated_grad = lax.psum_scatter(
        partial_grad.astype(jnp.bfloat16), "tp", scatter_dimension=1, tiled=True
    ).astype(jnp.float32)
    normed_grad = modulated_grad * (1.0 + scale_mod)
    grad_total, grad_cross = lax.psum(
        (jnp.sum(normed_grad, axis=1), jnp.sum(normed_grad * normed, axis=1)), "tp"
    )
    latent_grad = inverse * (
        normed_grad
        - (grad_total / full_width)[:, None]
        - normed * (grad_cross / full_width)[:, None]
    )
    latent_grad = latent_grad.astype(jnp.bfloat16)
    slot_grad = lax.dot_general(
        select, latent_grad, (((0,), (0,)), ((), ())), preferred_element_type=jnp.float32
    ).astype(jnp.bfloat16)
    returned = lax.all_to_all(
        slot_grad.reshape(seq_count, capacity, -1), "seq", split_axis=0, concat_axis=0, tiled=True
    )
    row_grad = returned.reshape(slots_all, -1)[position]
    section_three_grad = lax.psum_scatter(
        lax.dot_general(
            stacked_two, row_grad, (((0,), (0,)), ((), ())), preferred_element_type=jnp.float32
        ),
        "seq",
        scatter_dimension=0,
        tiled=True,
    )
    stacked_grad = lax.dot_general(
        row_grad, w_section3, (((1,), (1,)), ((), ())), preferred_element_type=jnp.float32
    )
    grad_two, grad_one = section_back(cells, z_one, stacked_one, z_two, stacked_grad, w_section2)
    section_two_grad, section_one_grad = lax.psum((grad_two, grad_one), ("seq", "tp"))
    return (normed_query, section_three_grad, section_two_grad, section_one_grad)


def solution(mesh):
    return jax.shard_map(
        body,
        mesh=mesh,
        in_specs=(
            P("seq", "tp"),
            P("seq", None),
            P("seq", None),
            P("seq"),
            P(),
            P(),
            P(None, "tp"),
            P("tp"),
            P("tp"),
            P("seq", "tp"),
            P("tp"),
            P("tp"),
            P("seq", "tp"),
        ),
        out_specs=(P("seq", "tp"), P("seq", "tp"), P(), P()),
        check_vma=False,
    )
```

profile of v0, /device:TPU:1, one launch (start us, length us, event | category | flops | bytes accessed | tf_op | source)
XLA Modules:
  0.0 1137.6 jit_solution(16691175735568463168)
XLA Ops:
  10.2 1.6 scatter_custom_fusion
  12.5 19.1 %all-to-all-start = ((s32[64,1,8]{2,1,0:T(1,128)}), s32[64,1,8]{2,1,0:T(1,128)S(1)}, u32[]{:S(2)}, u32[]{:S(2)}) async-start(s32[64,1,8]{2,1,0:T(1,128)} %bitcast.5), calls=%async_computation | async-start | bytes 65536 | tf_op jit(solution)/shard_map/all_to_all | solution.py:104
  31.6 1.8 reshape.78
  33.4 2.0 multiply_convert_fusion.3
  38.8 2.5 scatter_custom_fusion.1
  41.3 3.7 all-to-all-done
  45.0 10.8 all-to-all-start.1
  57.3 32.8 %all-to-all-done.1 = bf16[64,8,640]{2,1,0:T(8,128)(2,1)S(1)} async-done(((bf16[64,8,640]{2,1,0:T(8,128)(2,1)}), bf16[64,8,640]{2,1,0:T(8,128)(2,1)S(1)}, u32[]{:S(2)}, u32[]{:S(2)}) %all-to-all-start.1) | async-done | bytes 655392 | tf_op jit(solution)/shard_map/all_to_all | solution.py:97
  90.6 17.1 %all-reduce.3 = (f32[256]{0:T(256)S(1)}, f32[256]{0:T(256)S(1)}) all-reduce(f32[256]{0:T(256)S(1)} %get-tuple-element.7, f32[256]{0:T(256)S(1)} %get-tuple-element.6), channel_id=1, replica_groups=mesh['seq'=64,'tp'=8] {'tp'}, use_global_device_ids=true, to_apply=%region_8.9 | all-reduce | flops 512 | bytes 4096 | tf_op jit(solution)/shard_map/psum | solution.py:112
  109.4 24.1 %all-gather.3.cloned.1.call-done = bf16[256,5120]{1,0:T(8,128)(2,1)} async-done(((bf16[256,640]{1,0:T(8,128)(2,1)}), bf16[256,5120]{1,0:T(8,128)(2,1)}) %all-gather.3.cloned.1.call-update) | async-done | bytes 2621456 | tf_op jit(solution)/shard_map/all_gather | solution.py:117
  133.6 147.6 %all-gather.5.cloned.1.call-done = bf16[5120,640]{1,0:T(8,128)(2,1)} async-done(((bf16[80,640]{1,0:T(8,128)(2,1)}), bf16[5120,640]{1,0:T(8,128)(2,1)}) %all-gather.5.cloned.1.call-update) | async-done | bytes 6553616 | tf_op jit(solution)/shard_map/all_gather | solution.py:118
  281.2 6.7 multiply_reduce_fusion.1
  288.0 20.8 %all-reduce.2 = (f32[256]{0:T(256)S(1)}, f32[256]{0:T(256)S(1)}) all-reduce(f32[256]{0:T(256)S(1)} %get-tuple-element.5, f32[256]{0:T(256)S(1)} %get-tuple-element.4), channel_id=1, replica_groups=mesh['seq'=64,'tp'=8] {'tp'}, use_global_device_ids=true, to_apply=%region_10.11 | all-reduce | flops 512 | bytes 4096 | tf_op jit(solution)/shard_map/psum | solution.py:122
  309.4 5.5 convolution_convert_fusion
  314.9 2.6 copy.29
  317.5 32.9 %reduce-scatter.4.cloned.1.call-done = bf16[640,256]{1,0:T(8,128)(2,1)} async-done(((bf16[5120,256]{1,0:T(8,128)(2,1)}), bf16[640,256]{1,0:T(8,128)(2,1)}) %reduce-scatter.4.cloned.1.call-update) | async-done | bytes 327696
  351.8 14.3 %all-reduce.1 = (f32[256]{0:T(256)S(1)}, f32[256]{0:T(256)S(1)}) all-reduce(f32[256]{0:T(256)S(1)} %get-tuple-element.9, f32[256]{0:T(256)S(1)} %get-tuple-element.8), channel_id=1, replica_groups=mesh['seq'=64,'tp'=8] {'tp'}, use_global_device_ids=true, to_apply=%region_17.18 | all-reduce | flops 512 | bytes 4096 | tf_op jit(solution)/shard_map/psum | solution.py:136
  366.1 1.5 fusion
  367.6 15.3 %all-to-all-start.2 = ((bf16[64,8,640]{2,1,0:T(8,128)(2,1)}), bf16[64,8,640]{2,1,0:T(8,128)(2,1)S(1)}, u32[]{:S(2)}, u32[]{:S(2)}) async-start(bf16[64,8,640]{2,1,0:T(8,128)(2,1)} %fusion), calls=%async_computation.2 | async-start | bytes 1310720 | tf_op jit(solution)/shard_map/all_to_all | solution.py:148
  383.0 1.3 dynamic-slice
  384.9 32.4 %all-to-all-done.2 = bf16[64,8,640]{2,1,0:T(8,128)(2,1)S(1)} async-done(((bf16[64,8,640]{2,1,0:T(8,128)(2,1)}), bf16[64,8,640]{2,1,0:T(8,128)(2,1)S(1)}, u32[]{:S(2)}, u32[]{:S(2)}) %all-to-all-start.2) | async-done | bytes 655392 | tf_op jit(solution)/shard_map/all_to_all | solution.py:148
  417.4 1.2 gather_fusion
  418.6 1.5 fusion.30
  421.7 1.2 fusion.33
  422.8 3.0 reshape.87
  425.8 2.1 copy.27
  427.9 2.3 copy.28
  431.2 104.6 %psum.63 = f32[16,32]{1,0:T(8,128)} all-reduce(f32[16,32]{1,0:T(8,128)S(1)} %convolution_bitcast_fusion), channel_id=1, replica_groups=mesh['seq'=64,'tp'=8] {'seq','tp'}, use_global_device_ids=true, to_apply=%region_20.21 | all-reduce | flops 512 | bytes 4096 | tf_op jit(solution)/shard_map/psum | solution.py:164
  537.0 142.3 %all-reduce.9.cloned.1.call-done = f32[512,640]{1,0:T(8,128)} async-done(((f32[512,640]{1,0:T(8,128)}), f32[512,640]{1,0:T(8,128)}) %all-reduce.9.cloned.1.call-update) | async-done | bytes 1310736
  679.2 1.3 constant_dynamic-slice_fusion
  680.6 449.1 %all-reduce.7.cloned.1.call-done = f32[128,128]{1,0:T(8,128)} async-done(((f32[128,128]{1,0:T(8,128)}), f32[128,128]{1,0:T(8,128)}) %all-reduce.7.cloned.1.call-update) | async-done | bytes 65552 | tf_op jit(solution)/shard_map/psum | solution.py:164
  1129.6 1.5 copy.35
  (91 shorter events, 16.4 us)
Async XLA Ops:
  7.2 31.2 %copy-start = (bf16[512,640]{1,0:T(8,128)(2,1)S(1)}, bf16[512,640]{1,0:T(8,128)(2,1)}, u32[]{:S(2)}) copy-start(bf16[512,640]{1,0:T(8,128)(2,1)} %param.19) | copy-start | bytes 1966084
  10.2 28.5 %copy-start.15 = (s32[256,1]{0,1:T(1,128)}, s32[256,1]{0,1:T(1,128)S(1)}, u32[]{:S(2)}) copy-start(s32[256,1]{0,1:T(1,128)S(1)} %compare_select_fusion) | copy-start | bytes 3076
  12.5 32.5 %all-to-all-start = ((s32[64,1,8]{2,1,0:T(1,128)}), s32[64,1,8]{2,1,0:T(1,128)S(1)}, u32[]{:S(2)}, u32[]{:S(2)}) async-start(s32[64,1,8]{2,1,0:T(1,128)} %bitcast.5), calls=%async_computation | async-start | bytes 65536 | tf_op jit(solution)/shard_map/all_to_all | solution.py:104
  33.4 2.0 copy-start.5
  35.4 1.7 copy-start.9
  37.1 1.1 copy-start.3
  37.2 18.8 %copy-start.17 = (f32[640]{0:T(1024)S(1)}, f32[640]{0:T(1024)}, u32[]{:S(2)}) copy-start(f32[640]{0:T(1024)} %param.21) | copy-start | bytes 7684
  37.2 52.9 %copy-start.20 = (bf16[256,640]{1,0:T(8,128)(2,1)S(1)}, bf16[256,640]{1,0:T(8,128)(2,1)}, u32[]{:S(2)}) copy-start(bf16[256,640]{1,0:T(8,128)(2,1)} %param.13) | copy-start | bytes 983044
  38.4 69.3 %copy-start.11 = (f32[640]{0:T(1024)S(1)}, f32[640]{0:T(1024)}, u32[]{:S(2)}) copy-start(f32[640]{0:T(1024)} %param.20) | copy-start | bytes 7684
  38.8 242.5 %copy-start.12 = (f32[640]{0:T(1024)S(1)}, f32[640]{0:T(1024)}, u32[]{:S(2)}) copy-start(f32[640]{0:T(1024)} %param.24) | copy-start | bytes 7684
  38.8 242.5 %copy-start.21 = (bf16[256,640]{1,0:T(8,128)(2,1)S(1)}, bf16[256,640]{1,0:T(8,128)(2,1)}, u32[]{:S(2)}) copy-start(bf16[256,640]{1,0:T(8,128)(2,1)} %param.25) | copy-start | bytes 983044
  38.8 242.4 %copy-start.22 = (f32[640]{0:T(1024)S(1)}, f32[640]{0:T(1024)}, u32[]{:S(2)}) copy-start(f32[640]{0:T(1024)} %param.23) | copy-start | bytes 7684
  45.0 45.0 %all-to-all-start.1 = ((bf16[64,8,640]{2,1,0:T(8,128)(2,1)}), bf16[64,8,640]{2,1,0:T(8,128)(2,1)S(1)}, u32[]{:S(2)}, u32[]{:S(2)}) async-start(bf16[64,8,640]{2,1,0:T(8,128)(2,1)} %bitcast.8), calls=%async_computation.1 | async-start | bytes 1310720 | tf_op jit(solution)/shard_map/all_to_all | solution.py:97
  55.9 77.7 %all-gather.3.cloned.1.call-start = ((), (), s32[]{:S(2)}) async-start(), calls=%async_computation.4 | async-start | bytes 2949120 | tf_op jit(solution)/shard_map/all_gather | solution.py:117
  57.3 50.4 %copy-start.18 = (s32[512]{0:T(512)}, s32[512]{0:T(512)S(1)}, u32[]{:S(2)}) copy-start(s32[512]{0:T(512)S(1)} %eq.49) | copy-start | bytes 6148
  90.6 197.4 %copy-start.1 = (f32[256,640]{1,0:T(8,128)}, f32[256,640]{1,0:T(8,128)S(1)}, u32[]{:S(2)}) copy-start(f32[256,640]{1,0:T(8,128)S(1)} %get-tuple-element.24) | copy-start | bytes 1966084
  108.6 172.6 %all-gather.5.cloned.1.call-start = ((), (), s32[]{:S(2)}) async-start(), calls=%async_computation.5 | async-start | bytes 6656000 | tf_op jit(solution)/shard_map/all_gather | solution.py:118
  109.4 241.0 %reduce-scatter.4.cloned.1.call-start = ((), (), s32[]{:S(2)}) async-start(), calls=%async_computation.7 | async-start | bytes 2949120
  308.8 0.6 copy-start.13
  317.5 34.1 %copy-start.2 = (f32[256,640]{1,0:T(8,128)S(1)}, f32[256,640]{1,0:T(8,128)}, u32[]{:S(2)}) copy-start(f32[256,640]{1,0:T(8,128)} %copy-done.1) | copy-start | bytes 1966084
  317.5 48.7 %copy-start.19 = (s32[512]{0:T(512)S(1)}, s32[512]{0:T(512)}, u32[]{:S(2)}) copy-start(s32[512]{0:T(512)} %copy-done.18) | copy-start | bytes 6148
  317.5 67.4 %copy-start.16 = (s32[256,1]{0,1:T(1,128)S(1)}, s32[256,1]{0,1:T(1,128)}, u32[]{:S(2)}) copy-start(s32[256,1]{0,1:T(1,128)} %copy-done.15) | copy-start | bytes 3076
  367.6 49.8 %all-to-all-start.2 = ((bf16[64,8,640]{2,1,0:T(8,128)(2,1)}), bf16[64,8,640]{2,1,0:T(8,128)(2,1)S(1)}, u32[]{:S(2)}, u32[]{:S(2)}) async-start(bf16[64,8,640]{2,1,0:T(8,128)(2,1)} %fusion), calls=%async_computation.2 | async-start | bytes 1310720 | tf_op jit(solution)/shard_map/all_to_all | solution.py:148
  382.9 296.3 %all-reduce.9.cloned.1.call-start = ((), (), s32[]{:S(2)}) async-start(), calls=%async_computation.8 | async-start | bytes 2621440
  417.4 2.8 copy-start.7
  417.4 2.8 copy-start.14
  420.0 1.4 copy-start.8
  420.1 1.6 copy-start.10
  420.1 709.6 %all-reduce.7.cloned.1.call-start = ((), (), s32[]{:S(2)}) async-start(), calls=%async_computation.6 | async-start | bytes 131072 | tf_op jit(solution)/shard_map/psum | solution.py:164
  427.9 2.3 copy-start.6
  427.9 2.3 copy-start.23
  427.9 108.0 %copy-start.4 = (bf16[1024,128]{1,0:T(8,128)(2,1)S(1)}, bf16[1024,128]{1,0:T(8,128)(2,1)}, u32[]{:S(2)}) copy-start(bf16[1024,128]{1,0:T(8,128)(2,1)} %copy-done.3) | copy-start | bytes 786436
Sparse Core Ops, SparseCore 0:
  108.8 24.7 all-gather.2
  136.5 144.6 all-gather.4
  317.6 32.7 reduce-scatter.3
  420.2 259.0 all-reduce.8
  685.1 444.4 all-reduce.6
where the time goes:
time: 1140 us
  waiting for transfers between devices  866 us (76%)
  blocking collectives  157 us (14%)
  starting transfers between devices  45.5 us (4%)
  local copies, waits for them, and re-layouts  26.3 us (2%)
  matrix products  22.7 us (2%)
  between operations  14.8 us (1%)
    psum x1, waiting for transfers between devices, body(): lax.psum((grad_two, grad_one), ('seq', 'tp'))  449 us
    unnamed x7, waiting for transfers between devices  176 us
    all_gather x1, waiting for transfers between devices, body(): weights_all = lax.all_gather(w_query, 'seq', axis=0, tiled=True)  148 us
    psum x1, blocking collectives, body(): lax.psum((grad_two, grad_one), ('seq', 'tp'))  105 us
    all_to_all x1, waiting for transfers between devices, body(): lax.all_to_all(outgoing.reshape(seq_count, capacity, -1), 'seq', split_ax...  32.8 us
    all_to_all x1, waiting for transfers between devices, body(): lax.all_to_all(slot_grad.reshape(seq_count, capacity, -1), 'seq', split_a...  32.4 us
    all_gather x1, waiting for transfers between devices, body(): whole = lax.all_gather(modulated, 'tp', axis=1, tiled=True)  24.1 us
  transfers between devices with their start and end apart: 8, of which 8 were waited for; matrix products, arithmetic and copies ran while one was open for 2% of the time, Pallas kernels for 0%

commit v1 on v0

v1 whole, which is shorter than its diff:
```python
import jax
import jax.numpy as jnp
from jax import lax
from jax.experimental import pallas as pl
from jax.experimental.pallas import tpu as pltpu
from jax.sharding import Mesh, PartitionSpec as P

epsilon = 1e-06
bf16 = jnp.bfloat16
f32 = jnp.float32
SEQ = ("z", "x")
TP = ("y", "c")
N_Z, N_X, N_Y, N_C = 16, 4, 4, 2
N_SEQ, N_TP = N_Z * N_X, N_Y * N_C
CAP = 8


def silu_slope(z):
    s = jax.nn.sigmoid(z)
    return s * (1.0 + z * (1.0 - s))


def dot(a, b, dims, precision=None):
    return lax.dot_general(a, b, (dims, ((), ())), precision=precision, preferred_element_type=f32)


def exchange(x, axis):
    return lax.all_to_all(x, axis, split_axis=0, concat_axis=0, tiled=True)


def copies(x, axis, count):
    return exchange(jnp.broadcast_to(x[None], (count,) + x.shape), axis)


def query_kernel(core_ref, own_ref, other_ref, w_own_ref, w_other_ref, out_ref):
    @pl.when(pl.program_id(0) == 0)
    def _():
        out_ref[...] = jnp.zeros_like(out_ref)

    out_ref[...] += jnp.dot(
        own_ref[0], w_own_ref[0], preferred_element_type=f32
    ) + jnp.dot(other_ref[0], w_other_ref[0], preferred_element_type=f32)


def query_matmul(core, own, other, weights):
    groups, tokens, width = own.shape
    cols = weights.shape[2]
    return pl.pallas_call(
        query_kernel,
        out_shape=jax.ShapeDtypeStruct((tokens, cols), f32),
        grid_spec=pltpu.PrefetchScalarGridSpec(
            num_scalar_prefetch=1,
            grid=(groups,),
            in_specs=[
                pl.BlockSpec((1, tokens, width), lambda i, core: (i, 0, 0)),
                pl.BlockSpec((1, tokens, width), lambda i, core: (i, 0, 0)),
                pl.BlockSpec((1, width, cols), lambda i, core: (2 * i + core[0], 0, 0)),
                pl.BlockSpec((1, width, cols), lambda i, core: (2 * i + 1 - core[0], 0, 0)),
            ],
            out_specs=pl.BlockSpec((tokens, cols), lambda i, core: (0, 0)),
        ),
    )(core, own, other, weights, weights)


def partial_kernel(core_ref, grad_ref, w_ref, out_ref):
    out_ref[0] = dot(grad_ref[...], w_ref[0], ((1,), (1,))).astype(out_ref.dtype)


def partial_matmul(core, grad, weights):
    tokens, cols = grad.shape
    width = weights.shape[1]
    groups = weights.shape[0] // 2
    return pl.pallas_call(
        partial_kernel,
        out_shape=jax.ShapeDtypeStruct((groups, tokens, width), bf16),
        grid_spec=pltpu.PrefetchScalarGridSpec(
            num_scalar_prefetch=1,
            grid=(groups,),
            in_specs=[
                pl.BlockSpec((tokens, cols), lambda i, core: (0, 0)),
                pl.BlockSpec((1, width, cols), lambda i, core: (2 * i + core[0], 0, 0)),
            ],
            out_specs=pl.BlockSpec((1, tokens, width), lambda i, core: (i, 0, 0)),
        ),
    )(core, grad, weights)


def swap_cores(x):
    return lax.ppermute(x, "c", [(0, 1), (1, 0)])


def body(
    latent,
    pose_rows,
    dest_device,
    dest_slot,
    w_section1,
    w_section2,
    w_section3,
    shift_mod,
    scale_mod,
    w_query,
    bias_query,
    gain_query,
    cotangent,
):
    tokens, width = latent.shape
    rows = pose_rows.shape[0]
    cols = w_query.shape[1]
    full_width = width * N_TP
    query_width = cols * N_TP
    slots = N_SEQ * CAP
    c = lax.axis_index("c")
    core = c.astype(jnp.int32).reshape(1)

    w_rows = lax.all_gather(w_query, "x", axis=0, tiled=True)

    owner = dest_device[:, 0]
    marks = owner[:, None] == jnp.arange(N_SEQ, dtype=jnp.int32)[None, :]
    earlier = jnp.arange(rows)[:, None] > jnp.arange(rows)[None, :]
    before = dot(earlier.astype(bf16), marks.astype(bf16), ((1,), (0,)))
    rank = jnp.sum(jnp.where(marks, before, 0.0), axis=1).astype(jnp.int32)
    position = owner * CAP + rank
    place = (jnp.arange(slots, dtype=jnp.int32)[:, None] == position[None, :]).astype(bf16)
    half = pose_rows.shape[1] // 2
    pose_half = lax.dynamic_slice_in_dim(pose_rows, c * half, half, axis=1)
    label = jnp.broadcast_to((dest_slot + 1).astype(bf16)[:, None], (rows, half))
    packed = dot(place, jnp.concatenate([pose_half, label], axis=1), ((1,), (0,))).astype(bf16)
    outgoing = jnp.concatenate(
        [packed[:, :half].reshape(N_SEQ, CAP, half), packed[:, half:].reshape(N_SEQ, CAP, half)],
        axis=1,
    )
    w_rows, outgoing = lax.optimization_barrier((w_rows, outgoing))
    weights = lax.all_gather(w_rows, "z", axis=0, tiled=True).reshape(N_TP, width, cols)
    incoming = exchange(outgoing, SEQ)
    pose = lax.all_gather(incoming[:, :CAP].reshape(slots, half), "c", axis=1, tiled=True)
    slot = incoming[:, CAP:, :1].reshape(slots, 1).astype(jnp.int32) - 1
    select = (slot == jnp.arange(tokens, dtype=jnp.int32)[None, :]).astype(bf16)

    cell_in, c_one = w_section1.shape
    c_two = w_section2.shape[1]
    in_cell = jnp.arange(16 * cell_in) // cell_in
    out_cell = jnp.arange(16 * c_one) // c_one
    big_i, big_j, a, b = out_cell // 8, (out_cell // 4) % 2, (out_cell // 2) % 2, out_cell % 2
    from_cell = 4 * (2 * big_i + a) + 2 * big_j + b
    cell_mask = in_cell[:, None] == from_cell[None, :]
    w_one = jnp.where(cell_mask, jnp.tile(w_section1, (16, 16)), jnp.zeros((), bf16))
    quad = jnp.arange(4 * c_two) // c_two
    w_two = jnp.where(
        quad[:, None] == quad[None, :], jnp.tile(w_section2, (4, 4)), jnp.zeros((), bf16)
    )
    z_one = dot(pose, w_one, ((1,), (0,)))
    stacked_one = jax.nn.silu(z_one).astype(bf16)
    z_two = dot(stacked_one, w_two, ((1,), (0,)))
    stacked_two = jax.nn.silu(z_two).astype(bf16)
    pose_tokens = dot(stacked_two, w_section3, ((1,), (0,))).astype(bf16)
    guidance = dot(select, pose_tokens, ((0,), (0,)))
    summed = latent.astype(f32) + guidance

    local_mean = jnp.mean(summed, axis=1)
    local_square = jnp.sum((summed - local_mean[:, None]) ** 2, axis=1)
    stats = copies(jnp.stack([local_mean, local_square]), TP, N_TP)
    center = jnp.mean(stats[:, 0], axis=0)
    spread = (
        jnp.sum(stats[:, 1], axis=0) + width * jnp.sum((stats[:, 0] - center) ** 2, axis=0)
    ) / full_width
    inverse = lax.rsqrt(spread + epsilon)[:, None]
    normed = (summed - center[:, None]) * inverse
    modulated = (normed * (1.0 + scale_mod) + shift_mod).astype(bf16)
    own = copies(modulated, "y", N_Y)
    other = swap_cores(own)

    query = query_matmul(core, own, other, weights) + bias_query
    upstream = cotangent.astype(f32) * gain_query
    sums = copies(
        jnp.stack([jnp.sum(query * query, axis=1), jnp.sum(upstream * query, axis=1)]), TP, N_TP
    )
    sums = jnp.sum(sums, axis=0)
    rinv = lax.rsqrt(sums[0] / query_width + epsilon)[:, None]
    along = (sums[1] / query_width)[:, None]
    normed_query = (query * rinv * gain_query).astype(bf16)
    query_grad = (upstream * rinv - query * along * rinv**3).astype(bf16)

    theirs = swap_cores(partial_matmul(1 - core, query_grad, weights))
    mine = partial_matmul(core, query_grad, weights)
    pair = (mine.astype(f32) + theirs.astype(f32)).astype(bf16)
    modulated_grad = jnp.sum(exchange(pair, "y").astype(f32), axis=0)
    normed_grad = modulated_grad * (1.0 + scale_mod)
    sums = copies(
        jnp.stack([jnp.sum(normed_grad, axis=1), jnp.sum(normed_grad * normed, axis=1)]), TP, N_TP
    )
    sums = jnp.sum(sums, axis=0) / full_width
    latent_grad = inverse * (normed_grad - sums[0][:, None] - normed * sums[1][:, None])
    latent_grad = latent_grad.astype(bf16)

    slot_grad = dot(select, latent_grad, ((1,), (0,))).astype(bf16)
    grad_three = dot(stacked_two, slot_grad, ((0,), (0,)))
    two_grad = dot(slot_grad, w_section3, ((1,), (1,))) * silu_slope(z_two)
    grad_two = sum(
        dot(
            stacked_one[:, k * c_two : (k + 1) * c_two].astype(f32),
            two_grad[:, k * c_two : (k + 1) * c_two],
            ((0,), (0,)),
            lax.Precision.HIGHEST,
        )
        for k in range(4)
    )
    one_grad = dot(
        two_grad, w_two.astype(f32), ((1,), (1,)), lax.Precision.HIGHEST
    ) * silu_slope(z_one)
    cross = dot(pose.astype(f32), one_grad, ((0,), (0,)), lax.Precision.HIGHEST)
    cross = jnp.where(cell_mask, cross, 0.0)
    cross = jnp.sum(cross.reshape(16, cell_in, 16 * c_one), axis=0)
    grad_one = sum(cross[:, k * c_one : (k + 1) * c_one] for k in range(16))

    per = grad_three.shape[0] // N_SEQ
    two_rows = c_two // N_SEQ
    small = jnp.concatenate(
        [
            grad_two.reshape(N_SEQ, two_rows, c_two),
            jnp.pad(
                grad_one.reshape(N_SEQ, 1, -1),
                ((0, 0), (0, 0), (0, c_two - grad_one.size // N_SEQ)),
            ),
            jnp.zeros((N_SEQ, per - two_rows - 1, c_two), f32),
        ],
        axis=1,
    )
    shares = jnp.concatenate([grad_three.reshape(N_SEQ, per, width), small], axis=2).astype(bf16)
    mine = jnp.sum(exchange(shares, SEQ).astype(f32), axis=0)
    section_three_grad = mine[:, :width]
    small = mine[: two_rows + 1, width:].reshape(1, (two_rows + 1) * c_two)
    small = jnp.sum(copies(small, TP, N_TP), axis=0)
    small = copies(small, SEQ, N_SEQ).reshape(N_SEQ, two_rows + 1, c_two)
    section_two_grad = small[:, :two_rows].reshape(grad_two.shape)
    section_one_grad = small[:, two_rows, : grad_one.size // N_SEQ].reshape(grad_one.shape)
    return (normed_query, section_three_grad, section_two_grad, section_one_grad)


def solution(mesh):
    fine = Mesh(mesh.devices.reshape(N_Z, N_X, N_Y, N_C), ("z", "x", "y", "c"))
    return jax.shard_map(
        body,
        mesh=fine,
        in_specs=(
            P(SEQ, TP),
            P(SEQ, None),
            P(SEQ, None),
            P(SEQ),
            P(),
            P(),
            P(None, TP),
            P(TP),
            P(TP),
            P(SEQ, TP),
            P(TP),
            P(TP),
            P(SEQ, TP),
        ),
        out_specs=(P(SEQ, TP), P(SEQ, TP), P(), P()),
        check_vma=False,
    )
```

time: 1140 us -> 289 us (0.25)
  waiting for transfers between devices: 866 us -> 58.1 us
  blocking collectives: 157 us -> 126 us
  local copies, waits for them, and re-layouts: 26.3 us -> 8.47 us
  Pallas kernels: 0 us -> 16.2 us
  matrix products: 22.7 us -> 9.54 us
    psum x1 -> x0, waiting for transfers between devices: 449 us -> none  [body(): lax.psum((grad_two, grad_one), ('seq', 'tp'))]
    unnamed x7 -> x1, waiting for transfers between devices: 176 us -> 0.02 us
    all_gather x2 -> x1, waiting for transfers between devices: 172 us -> 11.2 us  [body(): lax.all_gather(w_rows, 'z', axis=0, tiled=True).reshape(N_TP, width, cols)]
    psum x4 -> x0, blocking collectives: 157 us -> none  [the longest x1 105 us: body(): lax.psum((grad_two, grad_one), ('seq', 'tp'))]
    all_to_all x0 -> x4, blocking collectives: none -> 103 us  [exchange(): return lax.all_to_all(x, axis, split_axis=0, concat_axis=0, tiled=True)]
    all_to_all x3 -> x5, waiting for transfers between devices: 68.9 us -> 44.2 us  [exchange(): return lax.all_to_all(x, axis, split_axis=0, concat_axis=0, tiled=True)]
    all_gather x0 -> x2, blocking collectives: none -> 23 us  [the longest x1 13 us: body(): w_rows = lax.all_gather(w_query, 'x', axis=0, tiled=True)]
    pallas_call x0 -> x3, Pallas kernels: none -> 16.2 us  [the longest x2 9.64 us: partial_matmul(): pl.pallas_call(partial_kernel, out_shape=jax.ShapeDtypeStruct((groups, to...]
  transfers between devices with their start and end apart: 8 -> 8, of which waited for: 8 -> 7; matrix products, arithmetic and copies ran while one was open for 2% -> 3% of each run, Pallas kernels for 0% -> 2%
where the time goes in v1:
time: 289 us; the launch traced here: 287 us
  blocking collectives  126 us (44%)
  waiting for transfers between devices  58.1 us (20%)
  starting transfers between devices  44.2 us (15%)
  Pallas kernels  16.2 us (6%)
  between operations  14.4 us (5%)
  other arithmetic  10.3 us (4%)
  matrix products  9.54 us (3%)
  local copies, waits for them, and re-layouts  8.47 us (3%)
    all_to_all x4, blocking collectives, exchange(): return lax.all_to_all(x, axis, split_axis=0, concat_axis=0, tiled=True)  103 us
    all_to_all x5, waiting for transfers between devices, exchange(): return lax.all_to_all(x, axis, split_axis=0, concat_axis=0, tiled=True)  44.2 us
    all_to_all x5, starting transfers between devices, exchange(): return lax.all_to_all(x, axis, split_axis=0, concat_axis=0, tiled=True)  37.9 us
    all_gather x1, blocking collectives, body(): w_rows = lax.all_gather(w_query, 'x', axis=0, tiled=True)  13 us
    all_gather x1, waiting for transfers between devices, body(): lax.all_gather(w_rows, 'z', axis=0, tiled=True).reshape(N_TP, width, cols)  11.2 us
    all_gather x1, blocking collectives, body(): lax.all_gather(incoming[:, :CAP].reshape(slots, half), 'c', axis=1, tiled...  10 us
    pallas_call x2, Pallas kernels, partial_matmul(): pl.pallas_call(partial_kernel, out_shape=jax.ShapeDtypeStruct((groups, to...  9.64 us
    dot_general x14, matrix products, dot(): lax.dot_general(a, b, (dims, ((), ())), precision=precision, preferred_el...  9.54 us
  transfers between devices with their start and end apart: 8, of which 7 were waited for; matrix products, arithmetic and copies ran while one was open for 3% of the time, Pallas kernels for 2%

profile of v1, /device:TPU:1, one launch (start us, length us, event | category | flops | bytes accessed | tf_op | source)
XLA Modules:
  0.0 287.2 jit_solution(1779908323939460863)
XLA Ops:
  7.2 1.0 fusion.8
  10.8 13.0 %all_gather.9 = bf16[320,640]{1,0:T(8,128)(2,1)} all-gather(bf16[80,640]{1,0:T(8,128)(2,1)} %param.22), channel_id=1, replica_groups=mesh['z'=16,'x'=4,'y'=4,'c'=2] {'x'}, dimensions={0}, use_global_device_ids=true | all-gather | bytes 512000 | tf_op jit(solution)/shard_map/all_gather | solution.py:116
  24.6 16.5 %all-to-all-start = ((bf16[64,16,128]{2,1,0:T(8,128)(2,1)}), bf16[64,16,128]{2,1,0:T(8,128)(2,1)S(1)}, u32[]{:S(2)}, u32[]{:S(2)}) async-start(bf16[64,16,128]{2,1,0:T(8,128)(2,1)} %pad_maximum_fusion), calls=%async_computation | async-start | bytes 524288 | tf_op jit(solution)/shard_map/all_to_all | solution.py:28
  41.3 1.0 tile.9
  42.4 16.3 %all-to-all-done = bf16[64,16,128]{2,1,0:T(8,128)(2,1)S(1)} async-done(((bf16[64,16,128]{2,1,0:T(8,128)(2,1)}), bf16[64,16,128]{2,1,0:T(8,128)(2,1)S(1)}, u32[]{:S(2)}, u32[]{:S(2)}) %all-to-all-start) | async-done | bytes 262176 | tf_op jit(solution)/shard_map/all_to_all | solution.py:28
  58.6 1.2 add_reduce_fusion
  59.9 10.0 %all_gather.10 = bf16[512,256]{1,0:T(8,128)(2,1)S(1)} all-gather(bf16[512,128]{1,0:T(8,128)(2,1)S(1)} %slice_bitcast_fusion), channel_id=1, replica_groups=mesh['z'=16,'x'=4,'y'=4,'c'=2] {'c'}, dimensions={1}, use_global_device_ids=true | all-gather | bytes 393216 | tf_op jit(solution)/shard_map/all_gather | solution.py:136
  69.9 1.4 multiply_convert_fusion.1
  72.9 1.0 fusion.65
  74.8 4.8 %all-to-all-start.1 = ((f32[8,2,256]{2,1,0:T(2,128)}), f32[8,2,256]{2,1,0:T(2,128)S(1)}, u32[]{:S(2)}, u32[]{:S(2)}) async-start(f32[8,2,256]{2,1,0:T(2,128)} %broadcast_in_dim.37), calls=%async_computation.1 | async-start | bytes 32768 | tf_op jit(solution)/shard_map/all_to_all | solution.py:28
  79.7 4.7 %all-to-all-done.1 = f32[8,2,256]{2,1,0:T(2,128)S(1)} async-done(((f32[8,2,256]{2,1,0:T(2,128)}), f32[8,2,256]{2,1,0:T(2,128)S(1)}, u32[]{:S(2)}, u32[]{:S(2)}) %all-to-all-start.1) | async-done | bytes 16416 | tf_op jit(solution)/shard_map/all_to_all | solution.py:28
  84.7 19.5 %all_to_all.45.own_ref = bf16[4,256,640]{2,1,0:T(8,128)(2,1)S(1)} all-to-all(bf16[4,256,640]{2,1,0:T(8,128)(2,1)S(1)} %broadcast_in_dim.38), channel_id=1, replica_groups=mesh['z'=16,'x'=4,'y'=4,'c'=2] {'y'}, dimensions={0} | all-to-all | bytes 2621440 | tf_op jit(solution)/shard_map/all_to_all | solution.py:28
  104.3 3.7 %collective-permute-start = (bf16[4,256,640]{2,1,0:T(8,128)(2,1)S(1)}, bf16[4,256,640]{2,1,0:T(8,128)(2,1)}, u32[]{:S(2)}, u32[]{:S(2)}) collective-permute-start(bf16[4,256,640]{2,1,0:T(8,128)(2,1)S(1)} %all_to_all.45.own_ref), channel_id=1, source_target_pairs={{0,1},{1,0},{2,3},{3,2},{4,5},{5,4},{6,7},{7,6},{8,9},{9,8},{10,11... | collective-permute-start | bytes 3932168 | tf_op jit(solution)/shard_map/ppermute | solution.py:89
  107.9 2.8 collective-permute-done.other_ref
  110.7 11.2 %all-gather.2.cloned.1.call-done = bf16[5120,640]{1,0:T(8,128)(2,1)} async-done(((bf16[320,640]{1,0:T(8,128)(2,1)}), bf16[5120,640]{1,0:T(8,128)(2,1)}) %all-gather.2.cloned.1.call-update) | async-done | bytes 6553616 | tf_op jit(solution)/shard_map/all_gather | solution.py:134
  121.9 6.6 %shard_map.156 = f32[256,640]{1,0:T(8,128)} custom-call(s32[1]{0:T(128)} %bitcast.core_ref, bf16[4,256,640]{2,1,0:T(8,128)(2,1)} %copy-done.1, bf16[4,256,640]{2,1,0:T(8,128)(2,1)} %collective-permute-done.other_ref, bf16[8,640,640]{2,1,0:T(8,128)(2,1)} %bitcast.49, bf16[8,640,640]{2,1,0:T(8,128)(2,1)} %bitcast.50), custom_call_target="tpu_custom_call" | custom-call | tf_op jit(solution)/shard_map/pallas_call | solution.py:48
  128.5 1.3 multiply_reduce_fusion.2
  130.4 6.7 %all-to-all-start.3 = ((f32[8,2,256]{2,1,0:T(2,128)}), f32[8,2,256]{2,1,0:T(2,128)S(1)}, u32[]{:S(2)}, u32[]{:S(2)}) async-start(f32[8,2,256]{2,1,0:T(2,128)} %broadcast_in_dim.39), calls=%async_computation.3 | async-start | bytes 32768 | tf_op jit(solution)/shard_map/all_to_all | solution.py:28
  137.2 4.7 %all-to-all-done.3 = f32[8,2,256]{2,1,0:T(2,128)S(1)} async-done(((f32[8,2,256]{2,1,0:T(2,128)}), f32[8,2,256]{2,1,0:T(2,128)S(1)}, u32[]{:S(2)}, u32[]{:S(2)}) %all-to-all-start.3) | async-done | bytes 16416 | tf_op jit(solution)/shard_map/all_to_all | solution.py:28
  141.8 2.2 subtract_convert_fusion
  144.0 4.8 %shard_map.158 = bf16[4,256,640]{2,1,0:T(8,128)(2,1)} custom-call(s32[1]{0:T(128)S(6)} %sub.108.core_ref, bf16[256,640]{1,0:T(8,128)(2,1)} %get-tuple-element.14.grad_ref, bf16[8,640,640]{2,1,0:T(8,128)(2,1)} %bitcast.51), custom_call_target="tpu_custom_call" | custom-call | tf_op jit(solution)/shard_map/pallas_call | solution.py:73
  148.8 2.6 collective-permute-start.1
  151.4 4.9 %shard_map.157 = bf16[4,256,640]{2,1,0:T(8,128)(2,1)} custom-call(s32[1]{0:T(128)} %bitcast.core_ref, bf16[256,640]{1,0:T(8,128)(2,1)} %get-tuple-element.14.grad_ref, bf16[8,640,640]{2,1,0:T(8,128)(2,1)} %bitcast.52), custom_call_target="tpu_custom_call" | custom-call | tf_op jit(solution)/shard_map/pallas_call | solution.py:73
  156.3 1.7 add_convert_fusion
  158.0 20.2 %all_to_all.46 = bf16[4,256,640]{2,1,0:T(8,128)(2,1)S(1)} all-to-all(bf16[4,256,640]{2,1,0:T(8,128)(2,1)S(1)} %add_convert_fusion), channel_id=1, replica_groups=mesh['z'=16,'x'=4,'y'=4,'c'=2] {'y'}, dimensions={0} | all-to-all | bytes 2621440 | tf_op jit(solution)/shard_map/all_to_all | solution.py:28
  179.3 4.3 %all-to-all-start.5 = ((f32[8,2,256]{2,1,0:T(2,128)}), f32[8,2,256]{2,1,0:T(2,128)S(1)}, u32[]{:S(2)}, u32[]{:S(2)}) async-start(f32[8,2,256]{2,1,0:T(2,128)} %broadcast_in_dim.40), calls=%async_computation.5 | async-start | bytes 32768 | tf_op jit(solution)/shard_map/all_to_all | solution.py:28
  183.6 4.7 %all-to-all-done.5 = f32[8,2,256]{2,1,0:T(2,128)S(1)} async-done(((f32[8,2,256]{2,1,0:T(2,128)}), f32[8,2,256]{2,1,0:T(2,128)S(1)}, u32[]{:S(2)}, u32[]{:S(2)}) %all-to-all-start.5) | async-done | bytes 16416 | tf_op jit(solution)/shard_map/all_to_all | solution.py:28
  192.0 1.4 convolution_multiply_fusion
  194.6 51.7 %all_to_all.47 = bf16[64,8,768]{2,1,0:T(8,128)(2,1)S(1)} all-to-all(bf16[64,8,768]{2,1,0:T(8,128)(2,1)S(1)} %maximum_maximum_fusion), channel_id=1, replica_groups=mesh['z'=16,'x'=4,'y'=4,'c'=2] {'z','x'}, dimensions={0} | all-to-all | bytes 1572864 | tf_op jit(solution)/shard_map/all_to_all | solution.py:28
  246.5 11.4 %all_to_all.48 = f32[8,1,384]{2,1,0:T(1,128)S(1)} all-to-all(f32[8,1,384]{2,1,0:T(1,128)S(1)} %broadcast_in_dim.44), channel_id=1, replica_groups=mesh['z'=16,'x'=4,'y'=4,'c'=2] {'y','c'}, dimensions={0} | all-to-all | bytes 24576 | tf_op jit(solution)/shard_map/all_to_all | solution.py:28
  258.5 5.6 %all-to-all-start.8 = ((f32[64,1,384]{2,1,0:T(1,128)}), f32[64,1,384]{2,1,0:T(1,128)S(1)}, u32[]{:S(2)}, u32[]{:S(2)}) async-start(f32[64,1,384]{2,1,0:T(1,128)} %broadcast_in_dim.45), calls=%async_computation.8 | async-start | bytes 196608 | tf_op jit(solution)/shard_map/all_to_all | solution.py:28
  264.7 13.9 %all-to-all-done.8 = f32[64,1,384]{2,1,0:T(1,128)S(1)} async-done(((f32[64,1,384]{2,1,0:T(1,128)}), f32[64,1,384]{2,1,0:T(1,128)S(1)}, u32[]{:S(2)}, u32[]{:S(2)}) %all-to-all-start.8) | async-done | bytes 98336 | tf_op jit(solution)/shard_map/all_to_all | solution.py:28
  (100 shorter events, 16.2 us)
Async XLA Ops:
  7.2 65.7 %copy-start = (bf16[512,640]{1,0:T(8,128)(2,1)S(1)}, bf16[512,640]{1,0:T(8,128)(2,1)}, u32[]{:S(2)}) copy-start(bf16[512,640]{1,0:T(8,128)(2,1)} %param.19) | copy-start | bytes 1966084
  7.2 114.7 %all-gather.2.cloned.1.call-start = ((), (), s32[]{:S(2)}) async-start(), calls=%async_computation.9 | async-start | bytes 6963200 | tf_op jit(solution)/shard_map/all_gather | solution.py:134
  9.6 31.5 %copy-start.10 = (bf16[16,32]{1,0:T(8,128)(2,1)S(1)}, bf16[16,32]{1,0:T(8,128)(2,1)}, u32[]{:S(2)}) copy-start(bf16[16,32]{1,0:T(8,128)(2,1)} %param.17) | copy-start | bytes 3076
  24.6 34.0 %all-to-all-start = ((bf16[64,16,128]{2,1,0:T(8,128)(2,1)}), bf16[64,16,128]{2,1,0:T(8,128)(2,1)S(1)}, u32[]{:S(2)}, u32[]{:S(2)}) async-start(bf16[64,16,128]{2,1,0:T(8,128)(2,1)} %pad_maximum_fusion), calls=%async_computation | async-start | bytes 524288 | tf_op jit(solution)/shard_map/all_to_all | solution.py:28
  69.9 1.4 copy-start.7
  71.3 0.8 copy-start.5
  71.3 1.6 copy-start.13
  71.5 0.8 copy-start.3
  72.9 1.1 copy-start.14
  72.9 6.7 %copy-start.12 = (f32[640]{0:T(1024)S(1)}, f32[640]{0:T(1024)}, u32[]{:S(2)}) copy-start(f32[640]{0:T(1024)} %param.21) | copy-start | bytes 7684
  72.9 11.5 %copy-start.11 = (f32[640]{0:T(1024)S(1)}, f32[640]{0:T(1024)}, u32[]{:S(2)}) copy-start(f32[640]{0:T(1024)} %param.20) | copy-start | bytes 7684
  74.8 9.5 %all-to-all-start.1 = ((f32[8,2,256]{2,1,0:T(2,128)}), f32[8,2,256]{2,1,0:T(2,128)S(1)}, u32[]{:S(2)}, u32[]{:S(2)}) async-start(f32[8,2,256]{2,1,0:T(2,128)} %broadcast_in_dim.37), calls=%async_computation.1 | async-start | bytes 32768 | tf_op jit(solution)/shard_map/all_to_all | solution.py:28
  104.3 17.6 %copy-start.1 = (bf16[4,256,640]{2,1,0:T(8,128)(2,1)}, bf16[4,256,640]{2,1,0:T(8,128)(2,1)S(1)}, u32[]{:S(2)}) copy-start(bf16[4,256,640]{2,1,0:T(8,128)(2,1)S(1)} %all_to_all.45.own_ref) | copy-start | bytes 3932164
  104.3 6.4 %collective-permute-start = (bf16[4,256,640]{2,1,0:T(8,128)(2,1)S(1)}, bf16[4,256,640]{2,1,0:T(8,128)(2,1)}, u32[]{:S(2)}, u32[]{:S(2)}) collective-permute-start(bf16[4,256,640]{2,1,0:T(8,128)(2,1)S(1)} %all_to_all.45.own_ref), channel_id=1, source_target_pairs={{0,1},{1,0},{2,3},{3,2},{4,5},{5,4},{6,7},{7,6},{8,9},{9,8},{10,11... | collective-permute-start | bytes 3932168 | tf_op jit(solution)/shard_map/ppermute | solution.py:89
  121.9 6.6 %copy-start.2 = (bf16[256,640]{1,0:T(8,128)(2,1)S(1)}, bf16[256,640]{1,0:T(8,128)(2,1)}, u32[]{:S(2)}) copy-start(bf16[256,640]{1,0:T(8,128)(2,1)} %param.25) | copy-start | bytes 983044
  121.9 6.6 %copy-start.8 = (f32[640]{0:T(1024)S(1)}, f32[640]{0:T(1024)}, u32[]{:S(2)}) copy-start(f32[640]{0:T(1024)} %param.23) | copy-start | bytes 7684
  121.9 6.6 %copy-start.9 = (f32[640]{0:T(1024)S(1)}, f32[640]{0:T(1024)}, u32[]{:S(2)}) copy-start(f32[640]{0:T(1024)} %param.24) | copy-start | bytes 7684
  130.4 11.4 %all-to-all-start.3 = ((f32[8,2,256]{2,1,0:T(2,128)}), f32[8,2,256]{2,1,0:T(2,128)S(1)}, u32[]{:S(2)}, u32[]{:S(2)}) async-start(f32[8,2,256]{2,1,0:T(2,128)} %broadcast_in_dim.39), calls=%async_computation.3 | async-start | bytes 32768 | tf_op jit(solution)/shard_map/all_to_all | solution.py:28
  148.8 7.5 %collective-permute-start.1 = (bf16[4,256,640]{2,1,0:T(8,128)(2,1)}, bf16[4,256,640]{2,1,0:T(8,128)(2,1)S(1)}, u32[]{:S(2)}, u32[]{:S(2)}) collective-permute-start(bf16[4,256,640]{2,1,0:T(8,128)(2,1)} %shard_map.158), channel_id=1, source_target_pairs={{0,1},{1,0},{2,3},{3,2},{4,5},{5,4},{6,7},{7,6},{8,9},{9,8},{10,11... | collective-permute-start | bytes 3932168 | tf_op jit(solution)/shard_map/ppermute | solution.py:89
  178.4 10.5 %copy-start.15 = (f32[512,512]{1,0:T(8,128)S(1)}, f32[512,512]{1,0:T(8,128)}, u32[]{:S(2)}) copy-start(f32[512,512]{1,0:T(8,128)} %copy-done.14) | copy-start | bytes 3145732
  179.3 9.0 %all-to-all-start.5 = ((f32[8,2,256]{2,1,0:T(2,128)}), f32[8,2,256]{2,1,0:T(2,128)S(1)}, u32[]{:S(2)}, u32[]{:S(2)}) async-start(f32[8,2,256]{2,1,0:T(2,128)} %broadcast_in_dim.40), calls=%async_computation.5 | async-start | bytes 32768 | tf_op jit(solution)/shard_map/all_to_all | solution.py:28
  189.6 1.0 copy-start.6
  190.6 1.3 copy-start.4
  190.6 1.4 copy-start.16
  258.5 20.1 %all-to-all-start.8 = ((f32[64,1,384]{2,1,0:T(1,128)}), f32[64,1,384]{2,1,0:T(1,128)S(1)}, u32[]{:S(2)}, u32[]{:S(2)}) async-start(f32[64,1,384]{2,1,0:T(1,128)} %broadcast_in_dim.45), calls=%async_computation.8 | async-start | bytes 196608 | tf_op jit(solution)/shard_map/all_to_all | solution.py:28
Sparse Core Ops, SparseCore 0:
  24.7 97.1 all-gather.1

commit v2 on v1

--- a/solution.py
+++ b/solution.py
@@ -10,8 +10,9 @@
 f32 = jnp.float32
 SEQ = ("z", "x")
 TP = ("y", "c")
+PLANE = ("x", "y", "c")
 N_Z, N_X, N_Y, N_C = 16, 4, 4, 2
-N_SEQ, N_TP = N_Z * N_X, N_Y * N_C
+N_SEQ, N_TP, N_PLANE = N_Z * N_X, N_Y * N_C, N_X * N_Y * N_C
 CAP = 8
 
 
@@ -63,7 +64,7 @@
 
 
 def partial_kernel(core_ref, grad_ref, w_ref, out_ref):
-    out_ref[0] = dot(grad_ref[...], w_ref[0], ((1,), (1,))).astype(out_ref.dtype)
+    out_ref[0] = dot(w_ref[0], grad_ref[...], ((1,), (1,))).astype(out_ref.dtype)
 
 
 def partial_matmul(core, grad, weights):
@@ -72,7 +73,7 @@
     groups = weights.shape[0] // 2
     return pl.pallas_call(
         partial_kernel,
-        out_shape=jax.ShapeDtypeStruct((groups, tokens, width), bf16),
+        out_shape=jax.ShapeDtypeStruct((groups, width, tokens), bf16),
         grid_spec=pltpu.PrefetchScalarGridSpec(
             num_scalar_prefetch=1,
             grid=(groups,),
@@ -80,9 +81,14 @@
                 pl.BlockSpec((tokens, cols), lambda i, core: (0, 0)),
                 pl.BlockSpec((1, width, cols), lambda i, core: (2 * i + core[0], 0, 0)),
             ],
-            out_specs=pl.BlockSpec((1, tokens, width), lambda i, core: (i, 0, 0)),
+            out_specs=pl.BlockSpec((1, width, tokens), lambda i, core: (i, 0, 0)),
         ),
     )(core, grad, weights)
+
+
+def halves(x):
+    high = lax.reduce_precision(x, 8, 7)
+    return jnp.stack([high, x - high]).astype(bf16)
 
 
 def swap_cores(x):
@@ -114,6 +120,10 @@
     core = c.astype(jnp.int32).reshape(1)
 
     w_rows = lax.all_gather(w_query, "x", axis=0, tiled=True)
+    w_rows, pose_rows, dest_device, dest_slot = lax.optimization_barrier(
+        (w_rows, pose_rows, dest_device, dest_slot)
+    )
+    weights = lax.all_gather(w_rows, "z", axis=0, tiled=True).reshape(N_TP, width, cols)
 
     owner = dest_device[:, 0]
     marks = owner[:, None] == jnp.arange(N_SEQ, dtype=jnp.int32)[None, :]
@@ -130,8 +140,6 @@
         [packed[:, :half].reshape(N_SEQ, CAP, half), packed[:, half:].reshape(N_SEQ, CAP, half)],
         axis=1,
     )
-    w_rows, outgoing = lax.optimization_barrier((w_rows, outgoing))
-    weights = lax.all_gather(w_rows, "z", axis=0, tiled=True).reshape(N_TP, width, cols)
     incoming = exchange(outgoing, SEQ)
     pose = lax.all_gather(incoming[:, :CAP].reshape(slots, half), "c", axis=1, tiled=True)
     slot = incoming[:, CAP:, :1].reshape(slots, 1).astype(jnp.int32) - 1
@@ -167,35 +175,61 @@
     inverse = lax.rsqrt(spread + epsilon)[:, None]
     normed = (summed - center[:, None]) * inverse
     modulated = (normed * (1.0 + scale_mod) + shift_mod).astype(bf16)
-    own = copies(modulated, "y", N_Y)
+    extra = jnp.concatenate([halves(1.0 + scale_mod), halves(shift_mod)])
+    extra = jnp.pad(extra, ((0, 12), (0, 0)))
+    own = copies(jnp.concatenate([modulated, extra]), "y", N_Y)
     other = swap_cores(own)
-
-    query = query_matmul(core, own, other, weights) + bias_query
+    normed_t, slope_one, slope_two, other = lax.optimization_barrier(
+        (normed.T, silu_slope(z_one), silu_slope(z_two), other)
+    )
+
+    products = query_matmul(core, own, other, weights)
+    query = products[:tokens] + bias_query
+    scale_w = products[tokens] + products[tokens + 1]
+    shift_w = products[tokens + 2] + products[tokens + 3] + bias_query
     upstream = cotangent.astype(f32) * gain_query
     sums = copies(
-        jnp.stack([jnp.sum(query * query, axis=1), jnp.sum(upstream * query, axis=1)]), TP, N_TP
+        jnp.stack(
+            [
+                jnp.sum(query * query, axis=1),
+                jnp.sum(upstream * query, axis=1),
+                jnp.sum(query * scale_w, axis=1),
+                jnp.sum(upstream * scale_w, axis=1),
+                jnp.sum(query * shift_w, axis=1),
+                jnp.sum(upstream * shift_w, axis=1),
+            ]
+        ),
+        TP,
+        N_TP,
     )
     sums = jnp.sum(sums, axis=0)
-    rinv = lax.rsqrt(sums[0] / query_width + epsilon)[:, None]
-    along = (sums[1] / query_width)[:, None]
+    rinv = lax.rsqrt(sums[0] / query_width + epsilon)
+    along = sums[1] / query_width
+    pull = along * rinv**3
+    grad_mean = (sums[3] * rinv - sums[2] * pull) / full_width
+    grad_cross = ((sums[1] - sums[5]) * rinv - (sums[0] - sums[4]) * pull) / full_width
+    rinv, pull = rinv[:, None], pull[:, None]
     normed_query = (query * rinv * gain_query).astype(bf16)
-    query_grad = (upstream * rinv - query * along * rinv**3).astype(bf16)
+    query_grad = (upstream * rinv - query * pull).astype(bf16)
 
     theirs = swap_cores(partial_matmul(1 - core, query_grad, weights))
     mine = partial_matmul(core, query_grad, weights)
     pair = (mine.astype(f32) + theirs.astype(f32)).astype(bf16)
     modulated_grad = jnp.sum(exchange(pair, "y").astype(f32), axis=0)
-    normed_grad = modulated_grad * (1.0 + scale_mod)
-    sums = copies(
-        jnp.stack([jnp.sum(normed_grad, axis=1), jnp.sum(normed_grad * normed, axis=1)]), TP, N_TP
-    )
-    sums = jnp.sum(sums, axis=0) / full_width
-    latent_grad = inverse * (normed_grad - sums[0][:, None] - normed * sums[1][:, None])
-    latent_grad = latent_grad.astype(bf16)
-
-    slot_grad = dot(select, latent_grad, ((1,), (0,))).astype(bf16)
-    grad_three = dot(stacked_two, slot_grad, ((0,), (0,)))
-    two_grad = dot(slot_grad, w_section3, ((1,), (1,))) * silu_slope(z_two)
+    normed_grad = modulated_grad * (1.0 + scale_mod)[:, None]
+    latent_grad = (
+        inverse.reshape(1, tokens)
+        * (normed_grad - grad_mean[None, :] - normed_t * grad_cross[None, :])
+    ).astype(bf16)
+
+    slot_grad = dot(select, latent_grad, ((1,), (1,))).astype(bf16)
+    grad_three = dot(stacked_two, slot_grad, ((0,), (0,))).astype(bf16)
+    per = grad_three.shape[0] // N_SEQ
+    grad_three = grad_three.reshape(N_Z, N_X, per, width).transpose(1, 0, 2, 3)
+    grad_three, slot_grad = lax.optimization_barrier((grad_three, slot_grad))
+    grad_three = exchange(grad_three, "x")
+
+    two_grad = dot(slot_grad, w_section3, ((1,), (1,))) * slope_two
     grad_two = sum(
         dot(
             stacked_one[:, k * c_two : (k + 1) * c_two].astype(f32),
@@ -205,35 +239,31 @@
         )
         for k in range(4)
     )
-    one_grad = dot(
-        two_grad, w_two.astype(f32), ((1,), (1,)), lax.Precision.HIGHEST
-    ) * silu_slope(z_one)
+    one_grad = dot(two_grad, w_two.astype(f32), ((1,), (1,)), lax.Precision.HIGHEST) * slope_one
     cross = dot(pose.astype(f32), one_grad, ((0,), (0,)), lax.Precision.HIGHEST)
     cross = jnp.where(cell_mask, cross, 0.0)
     cross = jnp.sum(cross.reshape(16, cell_in, 16 * c_one), axis=0)
     grad_one = sum(cross[:, k * c_one : (k + 1) * c_one] for k in range(16))
 
-    per = grad_three.shape[0] // N_SEQ
-    two_rows = c_two // N_SEQ
+    rows_two = c_two // N_PLANE
+    left = grad_one.size // N_PLANE
     small = jnp.concatenate(
         [
-            grad_two.reshape(N_SEQ, two_rows, c_two),
-            jnp.pad(
-                grad_one.reshape(N_SEQ, 1, -1),
-                ((0, 0), (0, 0), (0, c_two - grad_one.size // N_SEQ)),
-            ),
-            jnp.zeros((N_SEQ, per - two_rows - 1, c_two), f32),
+            grad_two.reshape(N_PLANE, rows_two, c_two),
+            jnp.pad(grad_one.reshape(N_PLANE, 1, left), ((0, 0), (0, 0), (0, c_two - left))),
         ],
         axis=1,
     )
-    shares = jnp.concatenate([grad_three.reshape(N_SEQ, per, width), small], axis=2).astype(bf16)
-    mine = jnp.sum(exchange(shares, SEQ).astype(f32), axis=0)
-    section_three_grad = mine[:, :width]
-    small = mine[: two_rows + 1, width:].reshape(1, (two_rows + 1) * c_two)
-    small = jnp.sum(copies(small, TP, N_TP), axis=0)
-    small = copies(small, SEQ, N_SEQ).reshape(N_SEQ, two_rows + 1, c_two)
-    section_two_grad = small[:, :two_rows].reshape(grad_two.shape)
-    section_one_grad = small[:, two_rows, : grad_one.size // N_SEQ].reshape(grad_one.shape)
+    small, grad_three = lax.optimization_barrier((small, grad_three))
+    small = jnp.sum(exchange(small, PLANE), axis=0)
+    grad_three = jnp.sum(grad_three.astype(f32), axis=0).astype(bf16)
+    small = jnp.broadcast_to(small.reshape(1, 1, width).astype(bf16), (N_Z, 1, width))
+    total = exchange(jnp.concatenate([grad_three, small], axis=1), "z")
+    total = jnp.sum(total.astype(f32), axis=0)
+    section_three_grad = total[:per]
+    small = copies(total[per:], PLANE, N_PLANE).reshape(N_PLANE, rows_two + 1, c_two)
+    section_two_grad = small[:, :rows_two].reshape(grad_two.shape)
+    section_one_grad = small[:, rows_two, :left].reshape(grad_one.shape)
     return (normed_query, section_three_grad, section_two_grad, section_one_grad)
 
 

time: 289 us -> 266 us (0.920)
  blocking collectives: 126 us -> 86.5 us
  starting transfers between devices: 44.2 us -> 53.9 us
  local copies, waits for them, and re-layouts: 8.47 us -> 11.5 us
    all_to_all x4 -> x3, blocking collectives: 103 us -> 64.7 us  [exchange(): return lax.all_to_all(x, axis, split_axis=0, concat_axis=0, tiled=True)]
    all_to_all x5 -> x6, starting transfers between devices: 37.9 us -> 47.7 us  [exchange(): return lax.all_to_all(x, axis, split_axis=0, concat_axis=0, tiled=True)]
    all_to_all x5 -> x6, waiting for transfers between devices: 44.2 us -> 50.5 us  [exchange(): return lax.all_to_all(x, axis, split_axis=0, concat_axis=0, tiled=True)]
    all_gather x1, waiting for transfers between devices: 11.2 us -> 5.42 us  [body(): lax.all_gather(w_rows, 'z', axis=0, tiled=True).reshape(N_TP, width, cols)]
  transfers between devices with their start and end apart: 8 -> 9, of which waited for: 7 -> 8; matrix products, arithmetic and copies ran while one was open for 3% -> 6% of each run, Pallas kernels for 2% -> 2%
where the time goes in v2:
time: 266 us; the launch traced here: 265 us
  blocking collectives  86.5 us (33%)
  waiting for transfers between devices  58.7 us (22%)
  starting transfers between devices  53.9 us (20%)
  Pallas kernels  16.5 us (6%)
  between operations  14.7 us (6%)
  matrix products  12 us (5%)
  local copies, waits for them, and re-layouts  11.5 us (4%)
  other arithmetic  11.4 us (4%)
    all_to_all x3, blocking collectives, exchange(): return lax.all_to_all(x, axis, split_axis=0, concat_axis=0, tiled=True)  64.7 us
    all_to_all x6, waiting for transfers between devices, exchange(): return lax.all_to_all(x, axis, split_axis=0, concat_axis=0, tiled=True)  50.5 us
    all_to_all x6, starting transfers between devices, exchange(): return lax.all_to_all(x, axis, split_axis=0, concat_axis=0, tiled=True)  47.7 us
    all_gather x1, blocking collectives, body(): w_rows = lax.all_gather(w_query, 'x', axis=0, tiled=True)  13.2 us
    dot_general x14, matrix products, dot(): lax.dot_general(a, b, (dims, ((), ())), precision=precision, preferred_el...  12 us
    pallas_call x2, Pallas kernels, partial_matmul(): pl.pallas_call(partial_kernel, out_shape=jax.ShapeDtypeStruct((groups, wi...  9.63 us
    all_gather x1, blocking collectives, body(): lax.all_gather(incoming[:, :CAP].reshape(slots, half), 'c', axis=1, tiled...  8.69 us
    pallas_call x1, Pallas kernels, query_matmul(): pl.pallas_call(query_kernel, out_shape=jax.ShapeDtypeStruct((tokens, cols...  6.86 us
  transfers between devices with their start and end apart: 9, of which 8 were waited for; matrix products, arithmetic and copies ran while one was open for 6% of the time, Pallas kernels for 2%

profile of v2, /device:TPU:1, one launch (start us, length us, event | category | flops | bytes accessed | tf_op | source)
XLA Modules:
  0.0 265.2 jit_solution(11597190307003632251)
XLA Ops:
  7.2 13.2 %all_gather.9 = bf16[320,640]{1,0:T(8,128)(2,1)} all-gather(bf16[80,640]{1,0:T(8,128)(2,1)} %param.22), channel_id=1, replica_groups=mesh['z'=16,'x'=4,'y'=4,'c'=2] {'x'}, dimensions={0}, use_global_device_ids=true | all-gather | bytes 512000 | tf_op jit(solution)/shard_map/all_gather | solution.py:122
  24.7 16.5 %all-to-all-start = ((bf16[64,16,128]{2,1,0:T(8,128)(2,1)}), bf16[64,16,128]{2,1,0:T(8,128)(2,1)S(1)}, u32[]{:S(2)}, u32[]{:S(2)}) async-start(bf16[64,16,128]{2,1,0:T(8,128)(2,1)} %pad_maximum_fusion.2), calls=%async_computation | async-start | bytes 524288 | tf_op jit(solution)/shard_map/all_to_all | solution.py:29
  42.7 18.5 %all-to-all-done = bf16[64,16,128]{2,1,0:T(8,128)(2,1)S(1)} async-done(((bf16[64,16,128]{2,1,0:T(8,128)(2,1)}), bf16[64,16,128]{2,1,0:T(8,128)(2,1)S(1)}, u32[]{:S(2)}, u32[]{:S(2)}) %all-to-all-start) | async-done | bytes 262176 | tf_op jit(solution)/shard_map/all_to_all | solution.py:29
  61.1 1.2 add_reduce_fusion
  62.4 8.7 %all_gather.10 = bf16[512,256]{1,0:T(8,128)(2,1)S(1)} all-gather(bf16[512,128]{1,0:T(8,128)(2,1)S(1)} %slice_bitcast_fusion), channel_id=1, replica_groups=mesh['z'=16,'x'=4,'y'=4,'c'=2] {'c'}, dimensions={1}, use_global_device_ids=true | all-gather | bytes 393216 | tf_op jit(solution)/shard_map/all_gather | solution.py:144
  71.1 1.7 add_multiply_fusion.1
  73.0 2.0 add_multiply_fusion
  75.0 2.3 fusion.73
  78.1 5.0 %all-to-all-start.1 = ((f32[8,2,256]{2,1,0:T(2,128)}), f32[8,2,256]{2,1,0:T(2,128)S(1)}, u32[]{:S(2)}, u32[]{:S(2)}) async-start(f32[8,2,256]{2,1,0:T(2,128)} %broadcast_in_dim.33), calls=%async_computation.1 | async-start | bytes 32768 | tf_op jit(solution)/shard_map/all_to_all | solution.py:29
  83.1 4.7 %all-to-all-done.1 = f32[8,2,256]{2,1,0:T(2,128)S(1)} async-done(((f32[8,2,256]{2,1,0:T(2,128)}), f32[8,2,256]{2,1,0:T(2,128)S(1)}, u32[]{:S(2)}, u32[]{:S(2)}) %all-to-all-start.1) | async-done | bytes 16416 | tf_op jit(solution)/shard_map/all_to_all | solution.py:29
  88.6 20.6 %all_to_all.45.own_ref = bf16[4,272,640]{2,1,0:T(8,128)(2,1)S(1)} all-to-all(bf16[4,272,640]{2,1,0:T(8,128)(2,1)S(1)} %broadcast_in_dim.34), channel_id=1, replica_groups=mesh['z'=16,'x'=4,'y'=4,'c'=2] {'y'}, dimensions={0} | all-to-all | bytes 2785280 | tf_op jit(solution)/shard_map/all_to_all | solution.py:29
  109.2 3.4 %collective-permute-start = (bf16[4,272,640]{2,1,0:T(8,128)(2,1)S(1)}, bf16[4,272,640]{2,1,0:T(8,128)(2,1)S(1)}, u32[]{:S(2)}, u32[]{:S(2)}) collective-permute-start(bf16[4,272,640]{2,1,0:T(8,128)(2,1)S(1)} %all_to_all.45.own_ref), channel_id=1, source_target_pairs={{0,1},{1,0},{2,3},{3,2},{4,5},{5,4},{6,7},{7,6},{8,9},{9,8},{10,11... | collective-permute-start | bytes 4177928 | tf_op jit(solution)/shard_map/ppermute | solution.py:95
  112.7 2.8 %collective-permute-done.other_ref = bf16[4,272,640]{2,1,0:T(8,128)(2,1)S(1)} collective-permute-done((bf16[4,272,640]{2,1,0:T(8,128)(2,1)S(1)}, bf16[4,272,640]{2,1,0:T(8,128)(2,1)S(1)}, u32[]{:S(2)}, u32[]{:S(2)}) %collective-permute-start) | collective-permute-done | bytes 1392672 | tf_op jit(solution)/shard_map/ppermute | solution.py:95
  115.4 1.2 copy-done.3
  116.6 5.4 %all-gather.2.cloned.1.call-done = bf16[5120,640]{1,0:T(8,128)(2,1)} async-done(((bf16[320,640]{1,0:T(8,128)(2,1)}), bf16[5120,640]{1,0:T(8,128)(2,1)}) %all-gather.2.cloned.1.call-update) | async-done | bytes 6553616 | tf_op jit(solution)/shard_map/all_gather | solution.py:126
  122.0 6.9 %shard_map.156 = f32[272,640]{1,0:T(8,128)} custom-call(s32[1]{0:T(128)} %bitcast.core_ref, bf16[4,272,640]{2,1,0:T(8,128)(2,1)} %copy-done.2, bf16[4,272,640]{2,1,0:T(8,128)(2,1)} %copy-done.3, bf16[8,640,640]{2,1,0:T(8,128)(2,1)} %bitcast.59, bf16[8,640,640]{2,1,0:T(8,128)(2,1)} %bitcast.60), custom_call_target="tpu_custom_call" | custom-call | tf_op jit(solution)/shard_map/pallas_call | solution.py:49
  130.5 1.5 multiply_reduce_fusion.1
  132.7 6.2 %all-to-all-start.3 = ((f32[8,6,256]{2,1,0:T(8,128)}), f32[8,6,256]{2,1,0:T(8,128)S(1)}, u32[]{:S(2)}, u32[]{:S(2)}) async-start(f32[8,6,256]{2,1,0:T(8,128)} %broadcast_in_dim.35), calls=%async_computation.3 | async-start | bytes 131072 | tf_op jit(solution)/shard_map/all_to_all | solution.py:29
  138.9 4.9 %all-to-all-done.3 = f32[8,6,256]{2,1,0:T(8,128)S(1)} async-done(((f32[8,6,256]{2,1,0:T(8,128)}), f32[8,6,256]{2,1,0:T(8,128)S(1)}, u32[]{:S(2)}, u32[]{:S(2)}) %all-to-all-start.3) | async-done | bytes 49184 | tf_op jit(solution)/shard_map/all_to_all | solution.py:29
  145.0 4.8 %shard_map.158 = bf16[4,640,256]{2,1,0:T(8,128)(2,1)} custom-call(s32[1]{0:T(128)S(6)} %sub.134.core_ref, bf16[256,640]{1,0:T(8,128)(2,1)} %get-tuple-element.40.grad_ref, bf16[8,640,640]{2,1,0:T(8,128)(2,1)} %bitcast.61), custom_call_target="tpu_custom_call" | custom-call | tf_op jit(solution)/shard_map/pallas_call | solution.py:74
  149.7 2.7 %collective-permute-start.1 = (bf16[4,640,256]{2,1,0:T(8,128)(2,1)}, bf16[4,640,256]{2,1,0:T(8,128)(2,1)S(1)}, u32[]{:S(2)}, u32[]{:S(2)}) collective-permute-start(bf16[4,640,256]{2,1,0:T(8,128)(2,1)} %shard_map.158), channel_id=1, source_target_pairs={{0,1},{1,0},{2,3},{3,2},{4,5},{5,4},{6,7},{7,6},{8,9},{9,8},{10,11... | collective-permute-start | bytes 3932168 | tf_op jit(solution)/shard_map/ppermute | solution.py:95
  152.4 4.8 %shard_map.157 = bf16[4,640,256]{2,1,0:T(8,128)(2,1)} custom-call(s32[1]{0:T(128)} %bitcast.core_ref, bf16[256,640]{1,0:T(8,128)(2,1)} %get-tuple-element.40.grad_ref, bf16[8,640,640]{2,1,0:T(8,128)(2,1)} %bitcast.62), custom_call_target="tpu_custom_call" | custom-call | tf_op jit(solution)/shard_map/pallas_call | solution.py:74
  157.3 1.6 add_convert_fusion
  158.9 20.2 %all_to_all.46 = bf16[4,640,256]{2,1,0:T(8,128)(2,1)S(1)} all-to-all(bf16[4,640,256]{2,1,0:T(8,128)(2,1)S(1)} %add_convert_fusion), channel_id=1, replica_groups=mesh['z'=16,'x'=4,'y'=4,'c'=2] {'y'}, dimensions={0} | all-to-all | bytes 2621440 | tf_op jit(solution)/shard_map/all_to_all | solution.py:29
  185.2 1.2 convolution_multiply_fusion
  187.4 3.7 %all-to-all-start.5 = ((bf16[4,16,8,640]{3,2,1,0:T(8,128)(2,1)}), bf16[4,16,8,640]{3,2,1,0:T(8,128)(2,1)S(1)}, u32[]{:S(2)}, u32[]{:S(2)}) async-start(bf16[4,16,8,640]{3,2,1,0:T(8,128)(2,1)} %bitcast.58), calls=%async_computation.5 | async-start | bytes 1310720 | tf_op jit(solution)/shard_map/all_to_all | solution.py:29
  192.4 7.9 %all-to-all-done.5 = bf16[4,16,8,640]{3,2,1,0:T(8,128)(2,1)S(1)} async-done(((bf16[4,16,8,640]{3,2,1,0:T(8,128)(2,1)}), bf16[4,16,8,640]{3,2,1,0:T(8,128)(2,1)S(1)}, u32[]{:S(2)}, u32[]{:S(2)}) %all-to-all-start.5) | async-done | bytes 655392 | tf_op jit(solution)/shard_map/all_to_all | solution.py:29
  200.3 6.1 %all-to-all-start.6 = ((f32[32,5,128]{2,1,0:T(8,128)}), f32[32,5,128]{2,1,0:T(8,128)S(1)}, u32[]{:S(2)}, u32[]{:S(2)}) async-start(f32[32,5,128]{2,1,0:T(8,128)} %pad_maximum_fusion.3), calls=%async_computation.6 | async-start | bytes 262144 | tf_op jit(solution)/shard_map/all_to_all | solution.py:29
  206.5 7.7 %all-to-all-done.6 = f32[32,5,128]{2,1,0:T(8,128)S(1)} async-done(((f32[32,5,128]{2,1,0:T(8,128)}), f32[32,5,128]{2,1,0:T(8,128)S(1)}, u32[]{:S(2)}, u32[]{:S(2)}) %all-to-all-start.6) | async-done | bytes 81952 | tf_op jit(solution)/shard_map/all_to_all | solution.py:29
  214.3 23.9 %all_to_all.47 = bf16[16,9,640]{2,1,0:T(8,128)(2,1)S(1)} all-to-all(bf16[16,9,640]{2,1,0:T(8,128)(2,1)S(1)} %pad_maximum_fusion.1), channel_id=1, replica_groups=mesh['z'=16,'x'=4,'y'=4,'c'=2] {'z'}, dimensions={0} | all-to-all | bytes 368640 | tf_op jit(solution)/shard_map/all_to_all | solution.py:29
  239.0 10.2 %all-to-all-start.8 = ((f32[32,1,640]{2,1,0:T(1,128)}), f32[32,1,640]{2,1,0:T(1,128)S(1)}, u32[]{:S(2)}, u32[]{:S(2)}) async-start(f32[32,1,640]{2,1,0:T(1,128)} %broadcast_in_dim.39), calls=%async_computation.8 | async-start | bytes 163840 | tf_op jit(solution)/shard_map/all_to_all | solution.py:29
  249.8 6.9 %all-to-all-done.8 = f32[32,1,640]{2,1,0:T(1,128)S(1)} async-done(((f32[32,1,640]{2,1,0:T(1,128)}), f32[32,1,640]{2,1,0:T(1,128)S(1)}, u32[]{:S(2)}, u32[]{:S(2)}) %all-to-all-start.8) | async-done | bytes 81952 | tf_op jit(solution)/shard_map/all_to_all | solution.py:29
  (136 shorter events, 22.4 us)
Async XLA Ops:
  7.2 67.8 %copy-start = (bf16[512,640]{1,0:T(8,128)(2,1)S(1)}, bf16[512,640]{1,0:T(8,128)(2,1)}, u32[]{:S(2)}) copy-start(bf16[512,640]{1,0:T(8,128)(2,1)} %param.19) | copy-start | bytes 1966084
  7.2 114.8 %all-gather.2.cloned.1.call-start = ((), (), s32[]{:S(2)}) async-start(), calls=%async_computation.9 | async-start | bytes 6963200 | tf_op jit(solution)/shard_map/all_gather | solution.py:126
  20.4 20.8 %copy-start.25 = (bf16[16,32]{1,0:T(8,128)(2,1)S(1)}, bf16[16,32]{1,0:T(8,128)(2,1)}, u32[]{:S(2)}) copy-start(bf16[16,32]{1,0:T(8,128)(2,1)} %param.17) | copy-start | bytes 3076
  24.7 36.4 %all-to-all-start = ((bf16[64,16,128]{2,1,0:T(8,128)(2,1)}), bf16[64,16,128]{2,1,0:T(8,128)(2,1)S(1)}, u32[]{:S(2)}, u32[]{:S(2)}) async-start(bf16[64,16,128]{2,1,0:T(8,128)(2,1)} %pad_maximum_fusion.2), calls=%async_computation | async-start | bytes 524288 | tf_op jit(solution)/shard_map/all_to_all | solution.py:29
  41.2 1.2 copy-start.26
  41.2 1.3 copy-start.18
  42.5 45.4 %copy-start.12 = (f32[640]{0:T(1024)}, f32[640]{0:T(1024)S(1)}, u32[]{:S(2)}) copy-start(f32[640]{0:T(1024)S(1)} %get-tuple-element.51) | copy-start | bytes 7684
  42.6 30.2 %copy-start.27 = (s32[256]{0:T(256)}, s32[256]{0:T(256)S(1)}, u32[]{:S(2)}) copy-start(s32[256]{0:T(256)S(1)} %and_select_fusion) | copy-start | bytes 3076
  42.6 30.1 %copy-start.23 = (s32[512]{0:T(512)}, s32[512]{0:T(512)S(1)}, u32[]{:S(2)}) copy-start(s32[512]{0:T(512)S(1)} %fusion.47) | copy-start | bytes 6148
  42.6 30.3 %copy-start.15 = (s32[512]{0:T(512)}, s32[512]{0:T(512)S(1)}, u32[]{:S(2)}) copy-start(s32[512]{0:T(512)S(1)} %add_select_fusion) | copy-start | bytes 6148
  62.4 12.6 %copy-start.21 = (s32[512]{0:T(512)}, s32[512]{0:T(512)S(1)}, u32[]{:S(2)}) copy-start(s32[512]{0:T(512)S(1)} %sub.116) | copy-start | bytes 6148
  71.1 1.7 copy-start.6
  71.1 1.7 copy-start.14
  72.8 2.2 copy-start.9
  72.9 2.0 copy-start.29
  78.1 9.7 %all-to-all-start.1 = ((f32[8,2,256]{2,1,0:T(2,128)}), f32[8,2,256]{2,1,0:T(2,128)S(1)}, u32[]{:S(2)}, u32[]{:S(2)}) async-start(f32[8,2,256]{2,1,0:T(2,128)} %broadcast_in_dim.33), calls=%async_computation.1 | async-start | bytes 32768 | tf_op jit(solution)/shard_map/all_to_all | solution.py:29
  109.2 12.8 %copy-start.2 = (bf16[4,272,640]{2,1,0:T(8,128)(2,1)}, bf16[4,272,640]{2,1,0:T(8,128)(2,1)S(1)}, u32[]{:S(2)}) copy-start(bf16[4,272,640]{2,1,0:T(8,128)(2,1)S(1)} %all_to_all.45.own_ref) | copy-start | bytes 4177924
  109.2 6.2 %collective-permute-start = (bf16[4,272,640]{2,1,0:T(8,128)(2,1)S(1)}, bf16[4,272,640]{2,1,0:T(8,128)(2,1)S(1)}, u32[]{:S(2)}, u32[]{:S(2)}) collective-permute-start(bf16[4,272,640]{2,1,0:T(8,128)(2,1)S(1)} %all_to_all.45.own_ref), channel_id=1, source_target_pairs={{0,1},{1,0},{2,3},{3,2},{4,5},{5,4},{6,7},{7,6},{8,9},{9,8},{10,11... | collective-permute-start | bytes 4177928 | tf_op jit(solution)/shard_map/ppermute | solution.py:95
  122.0 8.5 %copy-start.4 = (bf16[256,640]{1,0:T(8,128)(2,1)S(1)}, bf16[256,640]{1,0:T(8,128)(2,1)}, u32[]{:S(2)}) copy-start(bf16[256,640]{1,0:T(8,128)(2,1)} %param.25) | copy-start | bytes 983044
  128.8 15.0 %copy-start.1 = (f32[272,640]{1,0:T(8,128)S(1)}, f32[272,640]{1,0:T(8,128)}, u32[]{:S(2)}) copy-start(f32[272,640]{1,0:T(8,128)} %shard_map.156) | copy-start | bytes 2088964
  128.9 15.0 %copy-start.11 = (f32[640]{0:T(1024)S(1)}, f32[640]{0:T(1024)}, u32[]{:S(2)}) copy-start(f32[640]{0:T(1024)} %param.23) | copy-start | bytes 7684
  128.9 15.0 %copy-start.17 = (f32[640]{0:T(1024)S(1)}, f32[640]{0:T(1024)}, u32[]{:S(2)}) copy-start(f32[640]{0:T(1024)} %param.24) | copy-start | bytes 7684
  132.7 11.1 %all-to-all-start.3 = ((f32[8,6,256]{2,1,0:T(8,128)}), f32[8,6,256]{2,1,0:T(8,128)S(1)}, u32[]{:S(2)}, u32[]{:S(2)}) async-start(f32[8,6,256]{2,1,0:T(8,128)} %broadcast_in_dim.35), calls=%async_computation.3 | async-start | bytes 131072 | tf_op jit(solution)/shard_map/all_to_all | solution.py:29
  149.7 7.5 %collective-permute-start.1 = (bf16[4,640,256]{2,1,0:T(8,128)(2,1)}, bf16[4,640,256]{2,1,0:T(8,128)(2,1)S(1)}, u32[]{:S(2)}, u32[]{:S(2)}) collective-permute-start(bf16[4,640,256]{2,1,0:T(8,128)(2,1)} %shard_map.158), channel_id=1, source_target_pairs={{0,1},{1,0},{2,3},{3,2},{4,5},{5,4},{6,7},{7,6},{8,9},{9,8},{10,11... | collective-permute-start | bytes 3932168 | tf_op jit(solution)/shard_map/ppermute | solution.py:95
  179.5 1.2 copy-start.30
  182.3 1.2 copy-start.5
  183.5 1.7 copy-start.8
  183.5 1.7 copy-start.16
  185.2 1.2 copy-start.7
  187.4 12.9 %all-to-all-start.5 = ((bf16[4,16,8,640]{3,2,1,0:T(8,128)(2,1)}), bf16[4,16,8,640]{3,2,1,0:T(8,128)(2,1)S(1)}, u32[]{:S(2)}, u32[]{:S(2)}) async-start(bf16[4,16,8,640]{3,2,1,0:T(8,128)(2,1)} %bitcast.58), calls=%async_computation.5 | async-start | bytes 1310720 | tf_op jit(solution)/shard_map/all_to_all | solution.py:29
  200.3 13.9 %all-to-all-start.6 = ((f32[32,5,128]{2,1,0:T(8,128)}), f32[32,5,128]{2,1,0:T(8,128)S(1)}, u32[]{:S(2)}, u32[]{:S(2)}) async-start(f32[32,5,128]{2,1,0:T(8,128)} %pad_maximum_fusion.3), calls=%async_computation.6 | async-start | bytes 262144 | tf_op jit(solution)/shard_map/all_to_all | solution.py:29
  239.0 17.7 %all-to-all-start.8 = ((f32[32,1,640]{2,1,0:T(1,128)}), f32[32,1,640]{2,1,0:T(1,128)S(1)}, u32[]{:S(2)}, u32[]{:S(2)}) async-start(f32[32,1,640]{2,1,0:T(1,128)} %broadcast_in_dim.39), calls=%async_computation.8 | async-start | bytes 163840 | tf_op jit(solution)/shard_map/all_to_all | solution.py:29
  (8 other events, 7.3 us)
Sparse Core Ops, SparseCore 0:
  20.5 101.4 all-gather.1

commit v3 on v2

--- a/solution.py
+++ b/solution.py
@@ -10,9 +10,8 @@
 f32 = jnp.float32
 SEQ = ("z", "x")
 TP = ("y", "c")
-PLANE = ("x", "y", "c")
 N_Z, N_X, N_Y, N_C = 16, 4, 4, 2
-N_SEQ, N_TP, N_PLANE = N_Z * N_X, N_Y * N_C, N_X * N_Y * N_C
+N_SEQ, N_TP = N_Z * N_X, N_Y * N_C
 CAP = 8
 
 
@@ -119,7 +118,7 @@
     c = lax.axis_index("c")
     core = c.astype(jnp.int32).reshape(1)
 
-    w_rows = lax.all_gather(w_query, "x", axis=0, tiled=True)
+    w_rows = copies(w_query, "x", N_X).reshape(N_X * w_query.shape[0], cols)
     w_rows, pose_rows, dest_device, dest_slot = lax.optimization_barrier(
         (w_rows, pose_rows, dest_device, dest_slot)
     )
@@ -226,8 +225,6 @@
     grad_three = dot(stacked_two, slot_grad, ((0,), (0,))).astype(bf16)
     per = grad_three.shape[0] // N_SEQ
     grad_three = grad_three.reshape(N_Z, N_X, per, width).transpose(1, 0, 2, 3)
-    grad_three, slot_grad = lax.optimization_barrier((grad_three, slot_grad))
-    grad_three = exchange(grad_three, "x")
 
     two_grad = dot(slot_grad, w_section3, ((1,), (1,))) * slope_two
     grad_two = sum(
@@ -245,23 +242,35 @@
     cross = jnp.sum(cross.reshape(16, cell_in, 16 * c_one), axis=0)
     grad_one = sum(cross[:, k * c_one : (k + 1) * c_one] for k in range(16))
 
-    rows_two = c_two // N_PLANE
-    left = grad_one.size // N_PLANE
+    rows_two = c_two // N_TP
+    left = grad_one.size // N_TP
+    lines = 4
     small = jnp.concatenate(
         [
-            grad_two.reshape(N_PLANE, rows_two, c_two),
-            jnp.pad(grad_one.reshape(N_PLANE, 1, left), ((0, 0), (0, 0), (0, c_two - left))),
+            grad_two.reshape(N_TP, rows_two, c_two),
+            jnp.pad(grad_one.reshape(N_TP, 1, left), ((0, 0), (0, 3), (0, c_two - left))),
         ],
         axis=1,
     )
-    small, grad_three = lax.optimization_barrier((small, grad_three))
-    small = jnp.sum(exchange(small, PLANE), axis=0)
-    grad_three = jnp.sum(grad_three.astype(f32), axis=0).astype(bf16)
-    small = jnp.broadcast_to(small.reshape(1, 1, width).astype(bf16), (N_Z, 1, width))
-    total = exchange(jnp.concatenate([grad_three, small], axis=1), "z")
-    total = jnp.sum(total.astype(f32), axis=0)
+    small = jnp.sum(exchange(small, TP), axis=0).astype(bf16).reshape(1, lines, width)
+    shares = jnp.concatenate(
+        [
+            grad_three.reshape(N_X, N_Z * per, width),
+            jnp.broadcast_to(small, (N_X, lines, width)),
+        ],
+        axis=1,
+    )
+    shares = jnp.sum(exchange(shares, "x").astype(f32), axis=0).astype(bf16)
+    shares = jnp.concatenate(
+        [
+            shares[: N_Z * per].reshape(N_Z, per, width),
+            jnp.broadcast_to(shares[None, N_Z * per :], (N_Z, lines, width)),
+        ],
+        axis=1,
+    )
+    total = jnp.sum(exchange(shares, "z").astype(f32), axis=0)
     section_three_grad = total[:per]
-    small = copies(total[per:], PLANE, N_PLANE).reshape(N_PLANE, rows_two + 1, c_two)
+    small = copies(total[per:].reshape(lines * width // c_two, c_two), TP, N_TP)
     section_two_grad = small[:, :rows_two].reshape(grad_two.shape)
     section_one_grad = small[:, rows_two, :left].reshape(grad_one.shape)
     return (normed_query, section_three_grad, section_two_grad, section_one_grad)

time: 266 us -> 256 us (0.962)
  waiting for transfers between devices: 58.7 us -> 44.5 us
  blocking collectives: 86.5 us -> 96.8 us
  starting transfers between devices: 53.9 us -> 50.8 us
    all_to_all x3 -> x5, blocking collectives: 64.7 us -> 87.9 us  [exchange(): return lax.all_to_all(x, axis, split_axis=0, concat_axis=0, tiled=True)]
    all_to_all x6 -> x5, waiting for transfers between devices: 50.5 us -> 35.7 us  [exchange(): return lax.all_to_all(x, axis, split_axis=0, concat_axis=0, tiled=True)]
    all_gather x1 -> x0, blocking collectives: 13.2 us -> none  [body(): w_rows = lax.all_gather(w_query, 'x', axis=0, tiled=True)]
    all_to_all x6 -> x5, starting transfers between devices: 47.7 us -> 44.7 us  [exchange(): return lax.all_to_all(x, axis, split_axis=0, concat_axis=0, tiled=True)]
  transfers between devices with their start and end apart: 9 -> 8, of which waited for: 8 -> 7; matrix products, arithmetic and copies ran while one was open for 6% -> 5% of each run, Pallas kernels for 2% -> 2%
where the time goes in v3:
time: 256 us; the launch traced here: 255 us
  blocking collectives  96.8 us (38%)
  starting transfers between devices  50.8 us (20%)
  waiting for transfers between devices  44.5 us (17%)
  Pallas kernels  16.5 us (6%)
  between operations  14.8 us (6%)
  matrix products  11.2 us (4%)
  local copies, waits for them, and re-layouts  10.4 us (4%)
  other arithmetic  9.88 us (4%)
    all_to_all x5, blocking collectives, exchange(): return lax.all_to_all(x, axis, split_axis=0, concat_axis=0, tiled=True)  87.9 us
    all_to_all x5, starting transfers between devices, exchange(): return lax.all_to_all(x, axis, split_axis=0, concat_axis=0, tiled=True)  44.7 us
    all_to_all x5, waiting for transfers between devices, exchange(): return lax.all_to_all(x, axis, split_axis=0, concat_axis=0, tiled=True)  35.7 us
    dot_general x14, matrix products, dot(): lax.dot_general(a, b, (dims, ((), ())), precision=precision, preferred_el...  11.2 us
    pallas_call x2, Pallas kernels, partial_matmul(): pl.pallas_call(partial_kernel, out_shape=jax.ShapeDtypeStruct((groups, wi...  9.63 us
    all_gather x1, blocking collectives, body(): lax.all_gather(incoming[:, :CAP].reshape(slots, half), 'c', axis=1, tiled...  8.91 us
    pallas_call x1, Pallas kernels, query_matmul(): pl.pallas_call(query_kernel, out_shape=jax.ShapeDtypeStruct((tokens, cols...  6.86 us
    ppermute x2, starting transfers between devices, swap_cores(): return lax.ppermute(x, 'c', [(0, 1), (1, 0)])  6.13 us
  transfers between devices with their start and end apart: 8, of which 7 were waited for; matrix products, arithmetic and copies ran while one was open for 5% of the time, Pallas kernels for 2%

profile of v3, /device:TPU:1, one launch (start us, length us, event | category | flops | bytes accessed | tf_op | source)
XLA Modules:
  0.0 254.8 jit_solution(10672129093383150725)
XLA Ops:
  8.3 11.1 %all_to_all.50 = bf16[4,80,640]{2,1,0:T(8,128)(2,1)} all-to-all(bf16[4,80,640]{2,1,0:T(8,128)(2,1)S(1)} %broadcast_in_dim.33), channel_id=1, replica_groups=mesh['z'=16,'x'=4,'y'=4,'c'=2] {'x'}, dimensions={0} | all-to-all | bytes 819200 | tf_op jit(solution)/shard_map/all_to_all | solution.py:28
  20.8 17.4 %all-to-all-start.1 = ((bf16[64,16,128]{2,1,0:T(8,128)(2,1)}), bf16[64,16,128]{2,1,0:T(8,128)(2,1)S(1)}, u32[]{:S(2)}, u32[]{:S(2)}) async-start(bf16[64,16,128]{2,1,0:T(8,128)(2,1)} %pad_maximum_fusion.3), calls=%async_computation.1 | async-start | bytes 524288 | tf_op jit(solution)/shard_map/all_to_all | solution.py:28
  39.6 17.4 %all-to-all-done.1 = bf16[64,16,128]{2,1,0:T(8,128)(2,1)S(1)} async-done(((bf16[64,16,128]{2,1,0:T(8,128)(2,1)}), bf16[64,16,128]{2,1,0:T(8,128)(2,1)S(1)}, u32[]{:S(2)}, u32[]{:S(2)}) %all-to-all-start.1) | async-done | bytes 262176 | tf_op jit(solution)/shard_map/all_to_all | solution.py:28
  57.1 1.2 add_reduce_fusion
  58.3 8.9 %all_gather.6 = bf16[512,256]{1,0:T(8,128)(2,1)S(1)} all-gather(bf16[512,128]{1,0:T(8,128)(2,1)S(1)} %slice_bitcast_fusion.1), channel_id=1, replica_groups=mesh['z'=16,'x'=4,'y'=4,'c'=2] {'c'}, dimensions={1}, use_global_device_ids=true | all-gather | bytes 393216 | tf_op jit(solution)/shard_map/all_gather | solution.py:143
  67.3 1.7 add_multiply_fusion.1
  69.1 2.0 add_multiply_fusion
  71.1 2.3 fusion.73
  74.2 4.9 %all-to-all-start.2 = ((f32[8,2,256]{2,1,0:T(2,128)}), f32[8,2,256]{2,1,0:T(2,128)S(1)}, u32[]{:S(2)}, u32[]{:S(2)}) async-start(f32[8,2,256]{2,1,0:T(2,128)} %broadcast_in_dim.38), calls=%async_computation.2 | async-start | bytes 32768 | tf_op jit(solution)/shard_map/all_to_all | solution.py:28
  79.2 4.7 %all-to-all-done.2 = f32[8,2,256]{2,1,0:T(2,128)S(1)} async-done(((f32[8,2,256]{2,1,0:T(2,128)}), f32[8,2,256]{2,1,0:T(2,128)S(1)}, u32[]{:S(2)}, u32[]{:S(2)}) %all-to-all-start.2) | async-done | bytes 16416 | tf_op jit(solution)/shard_map/all_to_all | solution.py:28
  84.7 20.6 %all_to_all.51.own_ref = bf16[4,272,640]{2,1,0:T(8,128)(2,1)S(1)} all-to-all(bf16[4,272,640]{2,1,0:T(8,128)(2,1)S(1)} %broadcast_in_dim.39), channel_id=1, replica_groups=mesh['z'=16,'x'=4,'y'=4,'c'=2] {'y'}, dimensions={0} | all-to-all | bytes 2785280 | tf_op jit(solution)/shard_map/all_to_all | solution.py:28
  105.3 3.5 %collective-permute-start = (bf16[4,272,640]{2,1,0:T(8,128)(2,1)S(1)}, bf16[4,272,640]{2,1,0:T(8,128)(2,1)S(1)}, u32[]{:S(2)}, u32[]{:S(2)}) collective-permute-start(bf16[4,272,640]{2,1,0:T(8,128)(2,1)S(1)} %all_to_all.51.own_ref), channel_id=1, source_target_pairs={{0,1},{1,0},{2,3},{3,2},{4,5},{5,4},{6,7},{7,6},{8,9},{9,8},{10,11... | collective-permute-start | bytes 4177928 | tf_op jit(solution)/shard_map/ppermute | solution.py:94
  108.8 2.8 %collective-permute-done.other_ref = bf16[4,272,640]{2,1,0:T(8,128)(2,1)S(1)} collective-permute-done((bf16[4,272,640]{2,1,0:T(8,128)(2,1)S(1)}, bf16[4,272,640]{2,1,0:T(8,128)(2,1)S(1)}, u32[]{:S(2)}, u32[]{:S(2)}) %collective-permute-start) | collective-permute-done | bytes 1392672 | tf_op jit(solution)/shard_map/ppermute | solution.py:94
  111.5 1.2 copy-done.3
  112.7 6.1 %all-gather.2.cloned.1.call-done = bf16[5120,640]{1,0:T(8,128)(2,1)} async-done(((bf16[320,640]{1,0:T(8,128)(2,1)}), bf16[5120,640]{1,0:T(8,128)(2,1)}) %all-gather.2.cloned.1.call-update) | async-done | bytes 6553616 | tf_op jit(solution)/shard_map/all_gather | solution.py:125
  118.7 6.9 %shard_map.156 = f32[272,640]{1,0:T(8,128)} custom-call(s32[1]{0:T(128)} %bitcast.core_ref, bf16[4,272,640]{2,1,0:T(8,128)(2,1)} %copy-done.2, bf16[4,272,640]{2,1,0:T(8,128)(2,1)} %copy-done.3, bf16[8,640,640]{2,1,0:T(8,128)(2,1)} %bitcast.60, bf16[8,640,640]{2,1,0:T(8,128)(2,1)} %bitcast.61), custom_call_target="tpu_custom_call" | custom-call | tf_op jit(solution)/shard_map/pallas_call | solution.py:48
  127.3 1.5 multiply_reduce_fusion.1
  129.5 6.4 %all-to-all-start.4 = ((f32[8,6,256]{2,1,0:T(8,128)}), f32[8,6,256]{2,1,0:T(8,128)S(1)}, u32[]{:S(2)}, u32[]{:S(2)}) async-start(f32[8,6,256]{2,1,0:T(8,128)} %broadcast_in_dim.40), calls=%async_computation.4 | async-start | bytes 131072 | tf_op jit(solution)/shard_map/all_to_all | solution.py:28
  135.9 4.9 %all-to-all-done.4 = f32[8,6,256]{2,1,0:T(8,128)S(1)} async-done(((f32[8,6,256]{2,1,0:T(8,128)}), f32[8,6,256]{2,1,0:T(8,128)S(1)}, u32[]{:S(2)}, u32[]{:S(2)}) %all-to-all-start.4) | async-done | bytes 49184 | tf_op jit(solution)/shard_map/all_to_all | solution.py:28
  140.8 1.1 subtract_convert_fusion
  141.9 4.8 %shard_map.158 = bf16[4,640,256]{2,1,0:T(8,128)(2,1)} custom-call(s32[1]{0:T(128)S(6)} %sub.134.core_ref, bf16[256,640]{1,0:T(8,128)(2,1)} %get-tuple-element.32.grad_ref, bf16[8,640,640]{2,1,0:T(8,128)(2,1)} %bitcast.62), custom_call_target="tpu_custom_call" | custom-call | tf_op jit(solution)/shard_map/pallas_call | solution.py:73
  146.6 2.7 %collective-permute-start.1 = (bf16[4,640,256]{2,1,0:T(8,128)(2,1)}, bf16[4,640,256]{2,1,0:T(8,128)(2,1)S(1)}, u32[]{:S(2)}, u32[]{:S(2)}) collective-permute-start(bf16[4,640,256]{2,1,0:T(8,128)(2,1)} %shard_map.158), channel_id=1, source_target_pairs={{0,1},{1,0},{2,3},{3,2},{4,5},{5,4},{6,7},{7,6},{8,9},{9,8},{10,11... | collective-permute-start | bytes 3932168 | tf_op jit(solution)/shard_map/ppermute | solution.py:94
  149.3 4.8 %shard_map.157 = bf16[4,640,256]{2,1,0:T(8,128)(2,1)} custom-call(s32[1]{0:T(128)} %bitcast.core_ref, bf16[256,640]{1,0:T(8,128)(2,1)} %get-tuple-element.32.grad_ref, bf16[8,640,640]{2,1,0:T(8,128)(2,1)} %bitcast.63), custom_call_target="tpu_custom_call" | custom-call | tf_op jit(solution)/shard_map/pallas_call | solution.py:73
  154.2 1.6 add_convert_fusion
  155.8 20.2 %all_to_all.52 = bf16[4,640,256]{2,1,0:T(8,128)(2,1)S(1)} all-to-all(bf16[4,640,256]{2,1,0:T(8,128)(2,1)S(1)} %add_convert_fusion), channel_id=1, replica_groups=mesh['z'=16,'x'=4,'y'=4,'c'=2] {'y'}, dimensions={0} | all-to-all | bytes 2621440 | tf_op jit(solution)/shard_map/all_to_all | solution.py:28
  180.8 1.2 convolution_multiply_fusion
  183.6 4.4 %all-to-all-start.6 = ((f32[8,20,128]{2,1,0:T(8,128)}), f32[8,20,128]{2,1,0:T(8,128)S(1)}, u32[]{:S(2)}, u32[]{:S(2)}) async-start(f32[8,20,128]{2,1,0:T(8,128)} %select_maximum_fusion), calls=%async_computation.6 | async-start | bytes 196608 | tf_op jit(solution)/shard_map/all_to_all | solution.py:28
  188.7 4.3 %all-to-all-done.6 = f32[8,20,128]{2,1,0:T(8,128)S(1)} async-done(((f32[8,20,128]{2,1,0:T(8,128)}), f32[8,20,128]{2,1,0:T(8,128)S(1)}, u32[]{:S(2)}, u32[]{:S(2)}) %all-to-all-start.6) | async-done | bytes 81952 | tf_op jit(solution)/shard_map/all_to_all | solution.py:28
  193.1 13.9 %all_to_all.53 = bf16[4,132,640]{2,1,0:T(8,128)(2,1)S(1)} all-to-all(bf16[4,132,640]{2,1,0:T(8,128)(2,1)S(1)} %pad_maximum_fusion), channel_id=1, replica_groups=mesh['z'=16,'x'=4,'y'=4,'c'=2] {'x'}, dimensions={0} | all-to-all | bytes 1351680 | tf_op jit(solution)/shard_map/all_to_all | solution.py:28
  207.2 22.1 %all_to_all.54 = bf16[16,12,640]{2,1,0:T(8,128)(2,1)S(1)} all-to-all(bf16[16,12,640]{2,1,0:T(8,128)(2,1)S(1)} %pad_maximum_fusion.2), channel_id=1, replica_groups=mesh['z'=16,'x'=4,'y'=4,'c'=2] {'z'}, dimensions={0} | all-to-all | bytes 491520 | tf_op jit(solution)/shard_map/all_to_all | solution.py:28
  230.1 11.6 %all-to-all-start.9 = ((f32[8,20,128]{2,1,0:T(8,128)}), f32[8,20,128]{2,1,0:T(8,128)S(1)}, u32[]{:S(2)}, u32[]{:S(2)}) async-start(f32[8,20,128]{2,1,0:T(8,128)} %broadcast_in_dim.45), calls=%async_computation.9 | async-start | bytes 196608 | tf_op jit(solution)/shard_map/all_to_all | solution.py:28
  242.3 4.4 %all-to-all-done.9 = f32[8,20,128]{2,1,0:T(8,128)S(1)} async-done(((f32[8,20,128]{2,1,0:T(8,128)}), f32[8,20,128]{2,1,0:T(8,128)S(1)}, u32[]{:S(2)}, u32[]{:S(2)}) %all-to-all-start.9) | async-done | bytes 81952 | tf_op jit(solution)/shard_map/all_to_all | solution.py:28
  (145 shorter events, 17.9 us)
Async XLA Ops:
  7.2 63.9 %copy-start = (bf16[512,640]{1,0:T(8,128)(2,1)S(1)}, bf16[512,640]{1,0:T(8,128)(2,1)}, u32[]{:S(2)}) copy-start(bf16[512,640]{1,0:T(8,128)(2,1)} %param.19) | copy-start | bytes 1966084
  7.2 12.2 %copy-start.15 = (bf16[256,256]{1,0:T(8,128)(2,1)S(1)}, bf16[256,256]{1,0:T(8,128)(2,1)}, u32[]{:S(2)}) copy-start(bf16[256,256]{1,0:T(8,128)(2,1)} %param.14) | copy-start | bytes 393220
  7.2 12.2 %copy-start.30 = (s32[256,1]{0,1:T(1,128)S(1)}, s32[256,1]{0,1:T(1,128)}, u32[]{:S(2)}) copy-start(s32[256,1]{0,1:T(1,128)} %param.15) | copy-start | bytes 3076
  7.2 12.4 %copy-start.32 = (s32[256]{0:T(256)S(1)}, s32[256]{0:T(256)}, u32[]{:S(2)}) copy-start(s32[256]{0:T(256)} %param.16) | copy-start | bytes 3076
  7.2 111.5 %all-gather.2.cloned.1.call-start = ((), (), s32[]{:S(2)}) async-start(), calls=%async_computation.10 | async-start | bytes 6963200 | tf_op jit(solution)/shard_map/all_gather | solution.py:125
  19.4 18.8 %copy-start.26 = (bf16[16,32]{1,0:T(8,128)(2,1)S(1)}, bf16[16,32]{1,0:T(8,128)(2,1)}, u32[]{:S(2)}) copy-start(bf16[16,32]{1,0:T(8,128)(2,1)} %param.17) | copy-start | bytes 3076
  20.8 36.3 %all-to-all-start.1 = ((bf16[64,16,128]{2,1,0:T(8,128)(2,1)}), bf16[64,16,128]{2,1,0:T(8,128)(2,1)S(1)}, u32[]{:S(2)}, u32[]{:S(2)}) async-start(bf16[64,16,128]{2,1,0:T(8,128)(2,1)} %pad_maximum_fusion.3), calls=%async_computation.1 | async-start | bytes 524288 | tf_op jit(solution)/shard_map/all_to_all | solution.py:28
  38.2 1.2 copy-start.27
  38.2 1.3 copy-start.19
  39.5 44.5 %copy-start.12 = (f32[640]{0:T(1024)}, f32[640]{0:T(1024)S(1)}, u32[]{:S(2)}) copy-start(f32[640]{0:T(1024)S(1)} %get-tuple-element.43) | copy-start | bytes 7684
  39.6 29.4 %copy-start.28 = (s32[256]{0:T(256)}, s32[256]{0:T(256)S(1)}, u32[]{:S(2)}) copy-start(s32[256]{0:T(256)S(1)} %and_select_fusion) | copy-start | bytes 3076
  39.6 29.3 %copy-start.24 = (s32[512]{0:T(512)}, s32[512]{0:T(512)S(1)}, u32[]{:S(2)}) copy-start(s32[512]{0:T(512)S(1)} %fusion.47) | copy-start | bytes 6148
  39.6 29.5 %copy-start.16 = (s32[512]{0:T(512)}, s32[512]{0:T(512)S(1)}, u32[]{:S(2)}) copy-start(s32[512]{0:T(512)S(1)} %add_select_fusion) | copy-start | bytes 6148
  58.3 12.8 %copy-start.22 = (s32[512]{0:T(512)}, s32[512]{0:T(512)S(1)}, u32[]{:S(2)}) copy-start(s32[512]{0:T(512)S(1)} %sub.116) | copy-start | bytes 6148
  67.3 1.7 copy-start.6
  67.3 1.7 copy-start.14
  68.9 2.2 copy-start.9
  69.1 2.0 copy-start.31
  74.2 9.6 %all-to-all-start.2 = ((f32[8,2,256]{2,1,0:T(2,128)}), f32[8,2,256]{2,1,0:T(2,128)S(1)}, u32[]{:S(2)}, u32[]{:S(2)}) async-start(f32[8,2,256]{2,1,0:T(2,128)} %broadcast_in_dim.38), calls=%async_computation.2 | async-start | bytes 32768 | tf_op jit(solution)/shard_map/all_to_all | solution.py:28
  105.3 13.5 %copy-start.2 = (bf16[4,272,640]{2,1,0:T(8,128)(2,1)}, bf16[4,272,640]{2,1,0:T(8,128)(2,1)S(1)}, u32[]{:S(2)}) copy-start(bf16[4,272,640]{2,1,0:T(8,128)(2,1)S(1)} %all_to_all.51.own_ref) | copy-start | bytes 4177924
  105.3 6.2 %collective-permute-start = (bf16[4,272,640]{2,1,0:T(8,128)(2,1)S(1)}, bf16[4,272,640]{2,1,0:T(8,128)(2,1)S(1)}, u32[]{:S(2)}, u32[]{:S(2)}) collective-permute-start(bf16[4,272,640]{2,1,0:T(8,128)(2,1)S(1)} %all_to_all.51.own_ref), channel_id=1, source_target_pairs={{0,1},{1,0},{2,3},{3,2},{4,5},{5,4},{6,7},{7,6},{8,9},{9,8},{10,11... | collective-permute-start | bytes 4177928 | tf_op jit(solution)/shard_map/ppermute | solution.py:94
  118.7 8.5 %copy-start.4 = (bf16[256,640]{1,0:T(8,128)(2,1)S(1)}, bf16[256,640]{1,0:T(8,128)(2,1)}, u32[]{:S(2)}) copy-start(bf16[256,640]{1,0:T(8,128)(2,1)} %param.25) | copy-start | bytes 983044
  125.6 15.2 %copy-start.1 = (f32[272,640]{1,0:T(8,128)S(1)}, f32[272,640]{1,0:T(8,128)}, u32[]{:S(2)}) copy-start(f32[272,640]{1,0:T(8,128)} %shard_map.156) | copy-start | bytes 2088964
  125.6 15.2 %copy-start.11 = (f32[640]{0:T(1024)S(1)}, f32[640]{0:T(1024)}, u32[]{:S(2)}) copy-start(f32[640]{0:T(1024)} %param.23) | copy-start | bytes 7684
  125.6 15.2 %copy-start.18 = (f32[640]{0:T(1024)S(1)}, f32[640]{0:T(1024)}, u32[]{:S(2)}) copy-start(f32[640]{0:T(1024)} %param.24) | copy-start | bytes 7684
  129.5 11.3 %all-to-all-start.4 = ((f32[8,6,256]{2,1,0:T(8,128)}), f32[8,6,256]{2,1,0:T(8,128)S(1)}, u32[]{:S(2)}, u32[]{:S(2)}) async-start(f32[8,6,256]{2,1,0:T(8,128)} %broadcast_in_dim.40), calls=%async_computation.4 | async-start | bytes 131072 | tf_op jit(solution)/shard_map/all_to_all | solution.py:28
  146.6 7.5 %collective-permute-start.1 = (bf16[4,640,256]{2,1,0:T(8,128)(2,1)}, bf16[4,640,256]{2,1,0:T(8,128)(2,1)S(1)}, u32[]{:S(2)}, u32[]{:S(2)}) collective-permute-start(bf16[4,640,256]{2,1,0:T(8,128)(2,1)} %shard_map.158), channel_id=1, source_target_pairs={{0,1},{1,0},{2,3},{3,2},{4,5},{5,4},{6,7},{7,6},{8,9},{9,8},{10,11... | collective-permute-start | bytes 3932168 | tf_op jit(solution)/shard_map/ppermute | solution.py:94
  179.5 1.3 copy-start.8
  179.5 1.3 copy-start.17
  182.0 5.9 %copy-start.33 = (f32[512,512]{1,0:T(8,128)S(1)}, f32[512,512]{1,0:T(8,128)}, u32[]{:S(2)}) copy-start(f32[512,512]{1,0:T(8,128)} %get-tuple-element.51) | copy-start | bytes 3145732
  183.6 9.4 %all-to-all-start.6 = ((f32[8,20,128]{2,1,0:T(8,128)}), f32[8,20,128]{2,1,0:T(8,128)S(1)}, u32[]{:S(2)}, u32[]{:S(2)}) async-start(f32[8,20,128]{2,1,0:T(8,128)} %select_maximum_fusion), calls=%async_computation.6 | async-start | bytes 196608 | tf_op jit(solution)/shard_map/all_to_all | solution.py:28
  230.1 16.6 %all-to-all-start.9 = ((f32[8,20,128]{2,1,0:T(8,128)}), f32[8,20,128]{2,1,0:T(8,128)S(1)}, u32[]{:S(2)}, u32[]{:S(2)}) async-start(f32[8,20,128]{2,1,0:T(8,128)} %broadcast_in_dim.45), calls=%async_computation.9 | async-start | bytes 196608 | tf_op jit(solution)/shard_map/all_to_all | solution.py:28
  (10 other events, 9.7 us)
Sparse Core Ops, SparseCore 0:
  19.5 99.2 all-gather.1

commit v4 on v3

--- a/solution.py
+++ b/solution.py
@@ -32,57 +32,150 @@
     return exchange(jnp.broadcast_to(x[None], (count,) + x.shape), axis)
 
 
-def query_kernel(core_ref, own_ref, other_ref, w_own_ref, w_other_ref, out_ref):
-    @pl.when(pl.program_id(0) == 0)
-    def _():
-        out_ref[...] = jnp.zeros_like(out_ref)
-
-    out_ref[...] += jnp.dot(
-        own_ref[0], w_own_ref[0], preferred_element_type=f32
-    ) + jnp.dot(other_ref[0], w_other_ref[0], preferred_element_type=f32)
-
-
-def query_matmul(core, own, other, weights):
-    groups, tokens, width = own.shape
-    cols = weights.shape[2]
+VMEM_LIMIT = 32 * 1024 * 1024
+QUERY_VMEM_LIMIT = 52 * 1024 * 1024
+
+
+def in_vmem(count):
+    return [pl.BlockSpec(memory_space=pltpu.VMEM)] * count
+
+
+def across(column, width):
+    block = jnp.transpose(jnp.broadcast_to(column, (128, column.shape[1])))
+    return jnp.concatenate([block] * (width // 128), axis=1)
+
+
+def query_kernel(
+    bias_ref, gain_ref, cot_ref, own_ref, other_ref, w_ref, out_ref, sums_ref, left, held, sems
+):
+    core = lax.axis_index("c")
+    groups, _, width = own_ref.shape
+    tokens, cols = out_ref.shape
+    fetches = []
+    for i in range(groups):
+        for k, (source, which) in enumerate(
+            ((own_ref, 2 * i + core), (other_ref, 2 * i + 1 - core))
+        ):
+            place = 2 * i + k
+            fetches.append(pltpu.make_async_copy(source.at[i], left.at[place], sems.at[0, place]))
+            fetches.append(
+                pltpu.make_async_copy(
+                    w_ref.at[which], held.at[pl.ds(place * width, width)], sems.at[1, place]
+                )
+            )
+    for fetch in fetches:
+        fetch.start()
+    total = None
+    for i in range(groups):
+        for fetch in fetches[4 * i : 4 * (i + 1)]:
+            fetch.wait()
+        both = jnp.concatenate([left[2 * i], left[2 * i + 1]], axis=1)
+        term = jnp.dot(
+            both, held[2 * i * width : 2 * (i + 1) * width], preferred_element_type=f32
+        )
+        total = term if total is None else total + term
+    query = total[:tokens] + bias_ref[...]
+    out_ref[...] = query
+    scale_w = total[tokens : tokens + 1] + total[tokens + 1 : tokens + 2]
+    shift_w = total[tokens + 2 : tokens + 3] + total[tokens + 3 : tokens + 4] + bias_ref[...]
+    upstream = cot_ref[...].astype(f32) * gain_ref[...]
+    terms = (
+        query * query,
+        upstream * query,
+        query * scale_w,
+        upstream * scale_w,
+        query * shift_w,
+        upstream * shift_w,
+    )
+    rows = []
+    for term in terms:
+        lanes = sum(term[:, k : k + 128] for k in range(0, cols, 128))
+        rows.append(jnp.sum(jnp.transpose(lanes), axis=0, keepdims=True))
+    rows.append(jnp.zeros((8 - len(rows), tokens), f32))
+    sums_ref[...] = jnp.broadcast_to(jnp.concatenate(rows, axis=0)[None], sums_ref.shape)
+
+
+def query_matmul(own, other, bias, gain, cotangent, weights):
+    tokens, cols = cotangent.shape
     return pl.pallas_call(
         query_kernel,
-        out_shape=jax.ShapeDtypeStruct((tokens, cols), f32),
-        grid_spec=pltpu.PrefetchScalarGridSpec(
-            num_scalar_prefetch=1,
-            grid=(groups,),
-            in_specs=[
-                pl.BlockSpec((1, tokens, width), lambda i, core: (i, 0, 0)),
-                pl.BlockSpec((1, tokens, width), lambda i, core: (i, 0, 0)),
-                pl.BlockSpec((1, width, cols), lambda i, core: (2 * i + core[0], 0, 0)),
-                pl.BlockSpec((1, width, cols), lambda i, core: (2 * i + 1 - core[0], 0, 0)),
-            ],
-            out_specs=pl.BlockSpec((tokens, cols), lambda i, core: (0, 0)),
+        name="query",
+        out_shape=(
+            jax.ShapeDtypeStruct((tokens, cols), f32),
+            jax.ShapeDtypeStruct((N_TP, 8, tokens), f32),
         ),
-    )(core, own, other, weights, weights)
-
-
-def partial_kernel(core_ref, grad_ref, w_ref, out_ref):
-    out_ref[0] = dot(w_ref[0], grad_ref[...], ((1,), (1,))).astype(out_ref.dtype)
-
-
-def partial_matmul(core, grad, weights):
-    tokens, cols = grad.shape
-    width = weights.shape[1]
-    groups = weights.shape[0] // 2
+        in_specs=in_vmem(3) + [pl.BlockSpec(memory_space=pl.ANY)] * 3,
+        out_specs=tuple(in_vmem(2)),
+        scratch_shapes=[
+            pltpu.VMEM((2 * own.shape[0],) + own.shape[1:], bf16),
+            pltpu.VMEM((weights.shape[0] * weights.shape[1], cols), bf16),
+            pltpu.SemaphoreType.DMA((2, weights.shape[0])),
+        ],
+        compiler_params=pltpu.CompilerParams(vmem_limit_bytes=QUERY_VMEM_LIMIT),
+    )(bias[None], gain[None], cotangent, own, other, weights)
+
+
+def fetch_blocks(w_ref, held, sems, core):
+    fetches = [
+        pltpu.make_async_copy(w_ref.at[2 * i + core], held.at[i], sems.at[i])
+        for i in range(held.shape[0])
+    ]
+    for fetch in fetches:
+        fetch.start()
+    return fetches
+
+
+def token_scales(sums_ref, query_width, width):
+    sums = jnp.sum(sums_ref[...], axis=0)
+    rinv = lax.rsqrt(sums[0:1] / query_width + epsilon)
+    pull = sums[1:2] / query_width * rinv * rinv * rinv
+    return across(rinv, width), across(pull, width)
+
+
+def theirs_kernel(sums_ref, query_ref, gain_ref, cot_ref, w_ref, out_ref, grad_ref, held, sems):
+    fetches = fetch_blocks(w_ref, held, sems, 1 - lax.axis_index("c"))
+    cols = query_ref.shape[1]
+    rinv, pull = token_scales(sums_ref, N_TP * cols, cols)
+    upstream = cot_ref[...].astype(f32) * gain_ref[...]
+    grad_ref[...] = (upstream * rinv - query_ref[...] * pull).astype(bf16)
+    for i, fetch in enumerate(fetches):
+        fetch.wait()
+        out_ref[i] = dot(grad_ref[...], held[i], ((1,), (1,))).astype(bf16)
+
+
+def mine_kernel(sums_ref, query_ref, gain_ref, grad_ref, w_ref, out_ref, normed_ref, held, sems):
+    fetches = fetch_blocks(w_ref, held, sems, lax.axis_index("c"))
+    cols = query_ref.shape[1]
+    for i, fetch in enumerate(fetches):
+        fetch.wait()
+        out_ref[i] = dot(grad_ref[...], held[i], ((1,), (1,))).astype(bf16)
+    rinv, _ = token_scales(sums_ref, N_TP * cols, cols)
+    normed_ref[...] = (query_ref[...] * rinv * gain_ref[...]).astype(bf16)
+
+
+def partial_matmul(kernel, name, sums, query, gain, last, weights):
+    tokens, cols = query.shape
+    groups, width = weights.shape[0] // 2, weights.shape[1]
     return pl.pallas_call(
-        partial_kernel,
-        out_shape=jax.ShapeDtypeStruct((groups, width, tokens), bf16),
-        grid_spec=pltpu.PrefetchScalarGridSpec(
-            num_scalar_prefetch=1,
-            grid=(groups,),
-            in_specs=[
-                pl.BlockSpec((tokens, cols), lambda i, core: (0, 0)),
-                pl.BlockSpec((1, width, cols), lambda i, core: (2 * i + core[0], 0, 0)),
-            ],
-            out_specs=pl.BlockSpec((1, width, tokens), lambda i, core: (i, 0, 0)),
+        kernel,
+        name=name,
+        out_shape=(
+            jax.ShapeDtypeStruct((groups, tokens, width), bf16),
+            jax.ShapeDtypeStruct((tokens, cols), bf16),
         ),
-    )(core, grad, weights)
+        in_specs=in_vmem(4) + [pl.BlockSpec(memory_space=pl.ANY)],
+        out_specs=tuple(in_vmem(2)),
+        scratch_shapes=[
+            pltpu.VMEM((groups, width, cols), bf16),
+            pltpu.SemaphoreType.DMA((groups,)),
+        ],
+        compiler_params=pltpu.CompilerParams(vmem_limit_bytes=VMEM_LIMIT),
+        cost_estimate=pl.CostEstimate(
+            flops=2 * groups * tokens * cols * width,
+            bytes_accessed=2 * groups * width * cols,
+            transcendentals=0,
+        ),
+    )(sums, query, gain[None], last, weights)
 
 
 def halves(x):
@@ -116,7 +209,6 @@
     query_width = cols * N_TP
     slots = N_SEQ * CAP
     c = lax.axis_index("c")
-    core = c.astype(jnp.int32).reshape(1)
 
     w_rows = copies(w_query, "x", N_X).reshape(N_X * w_query.shape[0], cols)
     w_rows, pose_rows, dest_device, dest_slot = lax.optimization_barrier(
@@ -178,50 +270,30 @@
     extra = jnp.pad(extra, ((0, 12), (0, 0)))
     own = copies(jnp.concatenate([modulated, extra]), "y", N_Y)
     other = swap_cores(own)
-    normed_t, slope_one, slope_two, other = lax.optimization_barrier(
-        (normed.T, silu_slope(z_one), silu_slope(z_two), other)
-    )
-
-    products = query_matmul(core, own, other, weights)
-    query = products[:tokens] + bias_query
-    scale_w = products[tokens] + products[tokens + 1]
-    shift_w = products[tokens + 2] + products[tokens + 3] + bias_query
-    upstream = cotangent.astype(f32) * gain_query
-    sums = copies(
-        jnp.stack(
-            [
-                jnp.sum(query * query, axis=1),
-                jnp.sum(upstream * query, axis=1),
-                jnp.sum(query * scale_w, axis=1),
-                jnp.sum(upstream * scale_w, axis=1),
-                jnp.sum(query * shift_w, axis=1),
-                jnp.sum(upstream * shift_w, axis=1),
-            ]
-        ),
-        TP,
-        N_TP,
+    normed, slope_one, slope_two, other = lax.optimization_barrier(
+        (normed, silu_slope(z_one), silu_slope(z_two), other)
+    )
+
+    query, sums = query_matmul(own, other, bias_query, gain_query, cotangent, weights)
+    sums = exchange(sums, TP)
+    theirs, query_grad = partial_matmul(
+        theirs_kernel, "theirs", sums, query, gain_query, cotangent, weights
+    )
+    theirs = swap_cores(theirs)
+    mine, normed_query = partial_matmul(
+        mine_kernel, "mine", sums, query, gain_query, query_grad, weights
     )
     sums = jnp.sum(sums, axis=0)
     rinv = lax.rsqrt(sums[0] / query_width + epsilon)
-    along = sums[1] / query_width
-    pull = along * rinv**3
-    grad_mean = (sums[3] * rinv - sums[2] * pull) / full_width
-    grad_cross = ((sums[1] - sums[5]) * rinv - (sums[0] - sums[4]) * pull) / full_width
-    rinv, pull = rinv[:, None], pull[:, None]
-    normed_query = (query * rinv * gain_query).astype(bf16)
-    query_grad = (upstream * rinv - query * pull).astype(bf16)
-
-    theirs = swap_cores(partial_matmul(1 - core, query_grad, weights))
-    mine = partial_matmul(core, query_grad, weights)
+    pull = sums[1] / query_width * rinv**3
+    grad_mean = ((sums[3] * rinv - sums[2] * pull) / full_width)[:, None]
+    grad_cross = (((sums[1] - sums[5]) * rinv - (sums[0] - sums[4]) * pull) / full_width)[:, None]
     pair = (mine.astype(f32) + theirs.astype(f32)).astype(bf16)
     modulated_grad = jnp.sum(exchange(pair, "y").astype(f32), axis=0)
-    normed_grad = modulated_grad * (1.0 + scale_mod)[:, None]
-    latent_grad = (
-        inverse.reshape(1, tokens)
-        * (normed_grad - grad_mean[None, :] - normed_t * grad_cross[None, :])
-    ).astype(bf16)
-
-    slot_grad = dot(select, latent_grad, ((1,), (1,))).astype(bf16)
+    normed_grad = modulated_grad * (1.0 + scale_mod)
+    latent_grad = (inverse * (normed_grad - grad_mean - normed * grad_cross)).astype(bf16)
+
+    slot_grad = dot(select, latent_grad, ((1,), (0,))).astype(bf16)
     grad_three = dot(stacked_two, slot_grad, ((0,), (0,))).astype(bf16)
     per = grad_three.shape[0] // N_SEQ
     grad_three = grad_three.reshape(N_Z, N_X, per, width).transpose(1, 0, 2, 3)

time: 256 us -> 249 us (0.973)
  waiting for transfers between devices: 44.5 us -> 58.1 us
  blocking collectives: 96.8 us -> 87.8 us
  other arithmetic: 9.88 us -> 5.43 us
  Pallas kernels: 16.5 us -> 12.1 us
  matrix products: 11.2 us -> 14.8 us
  starting transfers between devices: 50.8 us -> 47.7 us
    all_to_all x5, waiting for transfers between devices: 35.7 us -> 47.7 us  [exchange(): return lax.all_to_all(x, axis, split_axis=0, concat_axis=0, tiled=True)]
    all_to_all x5, blocking collectives: 87.9 us -> 78.9 us  [exchange(): return lax.all_to_all(x, axis, split_axis=0, concat_axis=0, tiled=True)]
    pallas_call x3, Pallas kernels: 16.5 us -> 12.1 us  [the longest x1 6.11 us: query_matmul(): pl.pallas_call(query_kernel, name='query', out_shape=(jax.ShapeDtypeStruc...]
    dot_general x14, matrix products: 11.2 us -> 14.8 us  [dot(): lax.dot_general(a, b, (dims, ((), ())), precision=precision, preferred_el...]
    all_to_all x5, starting transfers between devices: 44.7 us -> 41.6 us  [exchange(): return lax.all_to_all(x, axis, split_axis=0, concat_axis=0, tiled=True)]
  transfers between devices with their start and end apart: 8 -> 8, of which waited for: 7 -> 7; matrix products, arithmetic and copies ran while one was open for 5% -> 5% of each run, Pallas kernels for 2% -> 1%
where the time goes in v4:
time: 249 us
  blocking collectives  87.8 us (35%)
  waiting for transfers between devices  58.1 us (23%)
  starting transfers between devices  47.7 us (19%)
  matrix products  14.8 us (6%)
  between operations  14.7 us (6%)
  Pallas kernels  12.1 us (5%)
  local copies, waits for them, and re-layouts  7.99 us (3%)
  other arithmetic  5.43 us (2%)
    all_to_all x5, blocking collectives, exchange(): return lax.all_to_all(x, axis, split_axis=0, concat_axis=0, tiled=True)  78.9 us
    all_to_all x5, waiting for transfers between devices, exchange(): return lax.all_to_all(x, axis, split_axis=0, concat_axis=0, tiled=True)  47.7 us
    all_to_all x5, starting transfers between devices, exchange(): return lax.all_to_all(x, axis, split_axis=0, concat_axis=0, tiled=True)  41.6 us
    dot_general x14, matrix products, dot(): lax.dot_general(a, b, (dims, ((), ())), precision=precision, preferred_el...  14.8 us
    all_gather x1, blocking collectives, body(): lax.all_gather(incoming[:, :CAP].reshape(slots, half), 'c', axis=1, tiled...  8.86 us
    all_gather x1, waiting for transfers between devices, body(): lax.all_gather(w_rows, 'z', axis=0, tiled=True).reshape(N_TP, width, cols)  7.65 us
    ppermute x2, starting transfers between devices, swap_cores(): return lax.ppermute(x, 'c', [(0, 1), (1, 0)])  6.14 us
    pallas_call x1, Pallas kernels, query_matmul(): pl.pallas_call(query_kernel, name='query', out_shape=(jax.ShapeDtypeStruc...  6.11 us
  transfers between devices with their start and end apart: 8, of which 7 were waited for; matrix products, arithmetic and copies ran while one was open for 5% of the time, Pallas kernels for 1%

profile of v4, /device:TPU:1, one launch (start us, length us, event | category | flops | bytes accessed | tf_op | source)
XLA Modules:
  0.0 248.6 jit_solution(12113880902756311923)
XLA Ops:
  8.3 11.1 %all_to_all.50 = bf16[4,80,640]{2,1,0:T(8,128)(2,1)} all-to-all(bf16[4,80,640]{2,1,0:T(8,128)(2,1)S(1)} %broadcast_in_dim.37), channel_id=1, replica_groups=mesh['z'=16,'x'=4,'y'=4,'c'=2] {'x'}, dimensions={0} | all-to-all | bytes 819200 | tf_op jit(solution)/shard_map/all_to_all | solution.py:28
  20.8 17.4 %all-to-all-start.1 = ((bf16[64,16,128]{2,1,0:T(8,128)(2,1)}), bf16[64,16,128]{2,1,0:T(8,128)(2,1)S(1)}, u32[]{:S(2)}, u32[]{:S(2)}) async-start(bf16[64,16,128]{2,1,0:T(8,128)(2,1)} %pad_maximum_fusion.3), calls=%async_computation.1 | async-start | bytes 524288 | tf_op jit(solution)/shard_map/all_to_all | solution.py:28
  39.6 17.6 %all-to-all-done.1 = bf16[64,16,128]{2,1,0:T(8,128)(2,1)S(1)} async-done(((bf16[64,16,128]{2,1,0:T(8,128)(2,1)}), bf16[64,16,128]{2,1,0:T(8,128)(2,1)S(1)}, u32[]{:S(2)}, u32[]{:S(2)}) %all-to-all-start.1) | async-done | bytes 262176 | tf_op jit(solution)/shard_map/all_to_all | solution.py:28
  58.4 8.9 %all_gather.6 = bf16[512,256]{1,0:T(8,128)(2,1)S(1)} all-gather(bf16[512,128]{1,0:T(8,128)(2,1)S(1)} %slice_bitcast_fusion.1), channel_id=1, replica_groups=mesh['z'=16,'x'=4,'y'=4,'c'=2] {'c'}, dimensions={1}, use_global_device_ids=true | all-gather | bytes 393216 | tf_op jit(solution)/shard_map/all_gather | solution.py:235
  67.3 1.7 add_multiply_fusion.1
  69.1 1.8 add_multiply_fusion
  72.8 5.0 %all-to-all-start.2 = ((f32[8,2,256]{2,1,0:T(2,128)}), f32[8,2,256]{2,1,0:T(2,128)S(1)}, u32[]{:S(2)}, u32[]{:S(2)}) async-start(f32[8,2,256]{2,1,0:T(2,128)} %broadcast_in_dim.42), calls=%async_computation.2 | async-start | bytes 32768 | tf_op jit(solution)/shard_map/all_to_all | solution.py:28
  77.8 4.7 %all-to-all-done.2 = f32[8,2,256]{2,1,0:T(2,128)S(1)} async-done(((f32[8,2,256]{2,1,0:T(2,128)}), f32[8,2,256]{2,1,0:T(2,128)S(1)}, u32[]{:S(2)}, u32[]{:S(2)}) %all-to-all-start.2) | async-done | bytes 16416 | tf_op jit(solution)/shard_map/all_to_all | solution.py:28
  83.0 20.7 %all_to_all.51.own_ref = bf16[4,272,640]{2,1,0:T(8,128)(2,1)S(1)} all-to-all(bf16[4,272,640]{2,1,0:T(8,128)(2,1)S(1)} %broadcast_in_dim.43), channel_id=1, replica_groups=mesh['z'=16,'x'=4,'y'=4,'c'=2] {'y'}, dimensions={0} | all-to-all | bytes 2785280 | tf_op jit(solution)/shard_map/all_to_all | solution.py:28
  103.7 3.5 %collective-permute-start = (bf16[4,272,640]{2,1,0:T(8,128)(2,1)S(1)}, bf16[4,272,640]{2,1,0:T(8,128)(2,1)S(1)}, u32[]{:S(2)}, u32[]{:S(2)}) collective-permute-start(bf16[4,272,640]{2,1,0:T(8,128)(2,1)S(1)} %all_to_all.51.own_ref), channel_id=1, source_target_pairs={{0,1},{1,0},{2,3},{3,2},{4,5},{5,4},{6,7},{7,6},{8,9},{9,8},{10,11... | collective-permute-start | bytes 4177928 | tf_op jit(solution)/shard_map/ppermute | solution.py:187
  107.2 2.7 %collective-permute-done.other_ref = bf16[4,272,640]{2,1,0:T(8,128)(2,1)S(1)} collective-permute-done((bf16[4,272,640]{2,1,0:T(8,128)(2,1)S(1)}, bf16[4,272,640]{2,1,0:T(8,128)(2,1)S(1)}, u32[]{:S(2)}, u32[]{:S(2)}) %collective-permute-start) | collective-permute-done | bytes 1392672 | tf_op jit(solution)/shard_map/ppermute | solution.py:187
  109.9 1.2 copy-done.6
  111.1 7.6 %all-gather.2.cloned.1.call-done = bf16[5120,640]{1,0:T(8,128)(2,1)} async-done(((bf16[320,640]{1,0:T(8,128)(2,1)}), bf16[5120,640]{1,0:T(8,128)(2,1)}) %all-gather.2.cloned.1.call-update) | async-done | bytes 6553616 | tf_op jit(solution)/shard_map/all_gather | solution.py:217
  118.7 6.1 %query.1 = (f32[256,640]{1,0:T(8,128)S(1)}, f32[8,8,256]{2,1,0:T(8,128)S(1)}) custom-call(f32[1,640]{1,0:T(1,128)S(1)} %broadcast_in_dim.35.bias_ref, f32[1,640]{1,0:T(1,128)S(1)} %broadcast_in_dim.36.gain_ref, bf16[256,640]{1,0:T(8,128)(2,1)S(1)} %copy-done.2, bf16[4,272,640]{2,1,0:T(8,128)(2,1)} %copy-done.3, bf16[4,272,640]{2,1,0:T(8,128)(2,1)} %copy-done.6, ...), custom_call_target="tpu_custom_call" | custom-call | tf_op jit(solution)/shard_map/query/pallas_call | solution.py:100
  124.8 11.1 %all_to_all.52.sums_ref = f32[8,8,256]{2,1,0:T(8,128)S(1)} all-to-all(f32[8,8,256]{2,1,0:T(8,128)S(1)} %get-tuple-element.23), channel_id=1, replica_groups=mesh['z'=16,'x'=4,'y'=4,'c'=2] {'y','c'}, dimensions={0} | all-to-all | bytes 131072 | tf_op jit(solution)/shard_map/all_to_all | solution.py:28
  136.0 2.8 %theirs.1 = (bf16[4,256,640]{2,1,0:T(8,128)(2,1)S(1)}, bf16[256,640]{1,0:T(8,128)(2,1)S(1)}) custom-call(f32[8,8,256]{2,1,0:T(8,128)S(1)} %all_to_all.52.sums_ref, f32[256,640]{1,0:T(8,128)S(1)} %get-tuple-element.24.query_ref, f32[1,640]{1,0:T(1,128)S(1)} %broadcast_in_dim.36.gain_ref, bf16[256,640]{1,0:T(8,128)(2,1)S(1)} %copy-done.2, ...), custom_call_target="tpu_custom_call" | custom-call | flops 838860800 | bytes 3276800 | tf_op jit(solution)/shard_map/theirs/pallas_call | solution.py:159
  138.7 2.7 %collective-permute-start.1 = (bf16[4,256,640]{2,1,0:T(8,128)(2,1)S(1)}, bf16[4,256,640]{2,1,0:T(8,128)(2,1)S(1)}, u32[]{:S(2)}, u32[]{:S(2)}) collective-permute-start(bf16[4,256,640]{2,1,0:T(8,128)(2,1)S(1)} %get-tuple-element.28), channel_id=1, source_target_pairs={{0,1},{1,0},{2,3},{3,2},{4,5},{5,4},{6,7},{7,6},{8,9},{9,8},{10,11... | collective-permute-start | bytes 3932168 | tf_op jit(solution)/shard_map/ppermute | solution.py:187
  141.4 3.3 %mine.1 = (bf16[4,256,640]{2,1,0:T(8,128)(2,1)S(1)}, bf16[256,640]{1,0:T(8,128)(2,1)}) custom-call(f32[8,8,256]{2,1,0:T(8,128)S(1)} %all_to_all.52.sums_ref, f32[256,640]{1,0:T(8,128)S(1)} %get-tuple-element.24.query_ref, f32[1,640]{1,0:T(1,128)S(1)} %broadcast_in_dim.36.gain_ref, bf16[256,640]{1,0:T(8,128)(2,1)S(1)} %get-tuple-element.25.grad_ref, ...), custom_call_target="tpu_custom_call" | custom-call | flops 838860800 | bytes 3276800 | tf_op jit(solution)/shard_map/mine/pallas_call | solution.py:159
  144.7 1.4 add_convert_fusion
  146.1 3.5 %all-to-all-start.5 = ((bf16[4,256,640]{2,1,0:T(8,128)(2,1)}), bf16[4,256,640]{2,1,0:T(8,128)(2,1)S(1)}, u32[]{:S(2)}, u32[]{:S(2)}) async-start(bf16[4,256,640]{2,1,0:T(8,128)(2,1)} %add_convert_fusion), calls=%async_computation.5 | async-start | bytes 2621440 | tf_op jit(solution)/shard_map/all_to_all | solution.py:28
  149.7 18.0 %all-to-all-done.5 = bf16[4,256,640]{2,1,0:T(8,128)(2,1)S(1)} async-done(((bf16[4,256,640]{2,1,0:T(8,128)(2,1)}), bf16[4,256,640]{2,1,0:T(8,128)(2,1)S(1)}, u32[]{:S(2)}, u32[]{:S(2)}) %all-to-all-start.5) | async-done | bytes 1310752 | tf_op jit(solution)/shard_map/all_to_all | solution.py:28
  169.9 1.3 fusion.11
  173.3 1.2 convolution_add_fusion.2
  174.5 1.2 convolution_add_fusion.1
  175.7 1.2 convolution_add_fusion
  177.6 4.1 %all-to-all-start.6 = ((f32[8,20,128]{2,1,0:T(8,128)}), f32[8,20,128]{2,1,0:T(8,128)S(1)}, u32[]{:S(2)}, u32[]{:S(2)}) async-start(f32[8,20,128]{2,1,0:T(8,128)} %select_maximum_fusion), calls=%async_computation.6 | async-start | bytes 196608 | tf_op jit(solution)/shard_map/all_to_all | solution.py:28
  181.7 1.9 convolution_convert_fusion.1
  183.6 3.0 %all-to-all-done.6 = f32[8,20,128]{2,1,0:T(8,128)S(1)} async-done(((f32[8,20,128]{2,1,0:T(8,128)}), f32[8,20,128]{2,1,0:T(8,128)S(1)}, u32[]{:S(2)}, u32[]{:S(2)}) %all-to-all-start.6) | async-done | bytes 81952 | tf_op jit(solution)/shard_map/all_to_all | solution.py:28
  186.8 13.9 %all_to_all.53 = bf16[4,132,640]{2,1,0:T(8,128)(2,1)S(1)} all-to-all(bf16[4,132,640]{2,1,0:T(8,128)(2,1)S(1)} %pad_maximum_fusion), channel_id=1, replica_groups=mesh['z'=16,'x'=4,'y'=4,'c'=2] {'x'}, dimensions={0} | all-to-all | bytes 1351680 | tf_op jit(solution)/shard_map/all_to_all | solution.py:28
  200.9 22.2 %all_to_all.54 = bf16[16,12,640]{2,1,0:T(8,128)(2,1)S(1)} all-to-all(bf16[16,12,640]{2,1,0:T(8,128)(2,1)S(1)} %pad_maximum_fusion.2), channel_id=1, replica_groups=mesh['z'=16,'x'=4,'y'=4,'c'=2] {'z'}, dimensions={0} | all-to-all | bytes 491520 | tf_op jit(solution)/shard_map/all_to_all | solution.py:28
  223.8 11.6 %all-to-all-start.9 = ((f32[8,20,128]{2,1,0:T(8,128)}), f32[8,20,128]{2,1,0:T(8,128)S(1)}, u32[]{:S(2)}, u32[]{:S(2)}) async-start(f32[8,20,128]{2,1,0:T(8,128)} %broadcast_in_dim.49), calls=%async_computation.9 | async-start | bytes 196608 | tf_op jit(solution)/shard_map/all_to_all | solution.py:28
  236.0 4.4 %all-to-all-done.9 = f32[8,20,128]{2,1,0:T(8,128)S(1)} async-done(((f32[8,20,128]{2,1,0:T(8,128)}), f32[8,20,128]{2,1,0:T(8,128)S(1)}, u32[]{:S(2)}, u32[]{:S(2)}) %all-to-all-start.9) | async-done | bytes 81952 | tf_op jit(solution)/shard_map/all_to_all | solution.py:28
  (114 shorter events, 15.4 us)
Async XLA Ops:
  7.2 63.7 %copy-start = (bf16[512,640]{1,0:T(8,128)(2,1)S(1)}, bf16[512,640]{1,0:T(8,128)(2,1)}, u32[]{:S(2)}) copy-start(bf16[512,640]{1,0:T(8,128)(2,1)} %param.19) | copy-start | bytes 1966084
  7.2 12.2 %copy-start.11 = (bf16[256,256]{1,0:T(8,128)(2,1)S(1)}, bf16[256,256]{1,0:T(8,128)(2,1)}, u32[]{:S(2)}) copy-start(bf16[256,256]{1,0:T(8,128)(2,1)} %param.14) | copy-start | bytes 393220
  7.2 12.2 %copy-start.17 = (s32[256,1]{0,1:T(1,128)S(1)}, s32[256,1]{0,1:T(1,128)}, u32[]{:S(2)}) copy-start(s32[256,1]{0,1:T(1,128)} %param.15) | copy-start | bytes 3076
  7.2 12.5 %copy-start.19 = (s32[256]{0:T(256)S(1)}, s32[256]{0:T(256)}, u32[]{:S(2)}) copy-start(s32[256]{0:T(256)} %param.16) | copy-start | bytes 3076
  7.2 111.5 %all-gather.2.cloned.1.call-start = ((), (), s32[]{:S(2)}) async-start(), calls=%async_computation.10 | async-start | bytes 6963200 | tf_op jit(solution)/shard_map/all_gather | solution.py:217
  19.4 18.9 %copy-start.12 = (f32[640]{0:T(1024)S(1)}, f32[640]{0:T(1024)}, u32[]{:S(2)}) copy-start(f32[640]{0:T(1024)} %param.20) | copy-start | bytes 7684
  19.4 18.9 %copy-start.14 = (f32[640]{0:T(1024)S(1)}, f32[640]{0:T(1024)}, u32[]{:S(2)}) copy-start(f32[640]{0:T(1024)} %param.21) | copy-start | bytes 7684
  19.4 18.9 %copy-start.13 = (bf16[16,32]{1,0:T(8,128)(2,1)S(1)}, bf16[16,32]{1,0:T(8,128)(2,1)}, u32[]{:S(2)}) copy-start(bf16[16,32]{1,0:T(8,128)(2,1)} %param.17) | copy-start | bytes 3076
  20.8 36.3 %all-to-all-start.1 = ((bf16[64,16,128]{2,1,0:T(8,128)(2,1)}), bf16[64,16,128]{2,1,0:T(8,128)(2,1)S(1)}, u32[]{:S(2)}, u32[]{:S(2)}) async-start(bf16[64,16,128]{2,1,0:T(8,128)(2,1)} %pad_maximum_fusion.3), calls=%async_computation.1 | async-start | bytes 524288 | tf_op jit(solution)/shard_map/all_to_all | solution.py:28
  67.3 1.7 copy-start.10
  69.0 1.9 copy-start.9
  69.1 1.8 copy-start.4
  69.1 1.8 copy-start.18
  70.9 1.1 copy-start.20
  72.8 9.7 %all-to-all-start.2 = ((f32[8,2,256]{2,1,0:T(2,128)}), f32[8,2,256]{2,1,0:T(2,128)S(1)}, u32[]{:S(2)}, u32[]{:S(2)}) async-start(f32[8,2,256]{2,1,0:T(2,128)} %broadcast_in_dim.42), calls=%async_computation.2 | async-start | bytes 32768 | tf_op jit(solution)/shard_map/all_to_all | solution.py:28
  82.9 24.2 %copy-start.15 = (f32[640]{0:T(1024)S(1)}, f32[640]{0:T(1024)}, u32[]{:S(2)}) copy-start(f32[640]{0:T(1024)} %param.23) | copy-start | bytes 7684
  82.9 24.2 %copy-start.16 = (f32[640]{0:T(1024)S(1)}, f32[640]{0:T(1024)}, u32[]{:S(2)}) copy-start(f32[640]{0:T(1024)} %param.24) | copy-start | bytes 7684
  82.9 35.8 %copy-start.2 = (bf16[256,640]{1,0:T(8,128)(2,1)S(1)}, bf16[256,640]{1,0:T(8,128)(2,1)}, u32[]{:S(2)}) copy-start(bf16[256,640]{1,0:T(8,128)(2,1)} %cot_ref.3) | copy-start | bytes 983044
  103.7 15.0 %copy-start.3 = (bf16[4,272,640]{2,1,0:T(8,128)(2,1)}, bf16[4,272,640]{2,1,0:T(8,128)(2,1)S(1)}, u32[]{:S(2)}) copy-start(bf16[4,272,640]{2,1,0:T(8,128)(2,1)S(1)} %all_to_all.51.own_ref) | copy-start | bytes 4177924
  103.7 6.2 %collective-permute-start = (bf16[4,272,640]{2,1,0:T(8,128)(2,1)S(1)}, bf16[4,272,640]{2,1,0:T(8,128)(2,1)S(1)}, u32[]{:S(2)}, u32[]{:S(2)}) collective-permute-start(bf16[4,272,640]{2,1,0:T(8,128)(2,1)S(1)} %all_to_all.51.own_ref), channel_id=1, source_target_pairs={{0,1},{1,0},{2,3},{3,2},{4,5},{5,4},{6,7},{7,6},{8,9},{9,8},{10,11... | collective-permute-start | bytes 4177928 | tf_op jit(solution)/shard_map/ppermute | solution.py:187
  109.9 1.2 copy-start.6
  118.7 17.2 %copy-start.1 = (bf16[5120,640]{1,0:T(8,128)(2,1)S(1)}, bf16[5120,640]{1,0:T(8,128)(2,1)}, u32[]{:S(2)}) copy-start(bf16[5120,640]{1,0:T(8,128)(2,1)} %all-gather.2.cloned.1.call-done) | copy-start | bytes 19660804
  138.7 6.0 %collective-permute-start.1 = (bf16[4,256,640]{2,1,0:T(8,128)(2,1)S(1)}, bf16[4,256,640]{2,1,0:T(8,128)(2,1)S(1)}, u32[]{:S(2)}, u32[]{:S(2)}) collective-permute-start(bf16[4,256,640]{2,1,0:T(8,128)(2,1)S(1)} %get-tuple-element.28), channel_id=1, source_target_pairs={{0,1},{1,0},{2,3},{3,2},{4,5},{5,4},{6,7},{7,6},{8,9},{9,8},{10,11... | collective-permute-start | bytes 3932168 | tf_op jit(solution)/shard_map/ppermute | solution.py:187
  146.1 21.6 %all-to-all-start.5 = ((bf16[4,256,640]{2,1,0:T(8,128)(2,1)}), bf16[4,256,640]{2,1,0:T(8,128)(2,1)S(1)}, u32[]{:S(2)}, u32[]{:S(2)}) async-start(bf16[4,256,640]{2,1,0:T(8,128)(2,1)} %add_convert_fusion), calls=%async_computation.5 | async-start | bytes 2621440 | tf_op jit(solution)/shard_map/all_to_all | solution.py:28
  168.4 1.2 copy-start.7
  169.7 1.5 copy-start.5
  169.7 1.5 copy-start.8
  177.6 9.1 %all-to-all-start.6 = ((f32[8,20,128]{2,1,0:T(8,128)}), f32[8,20,128]{2,1,0:T(8,128)S(1)}, u32[]{:S(2)}, u32[]{:S(2)}) async-start(f32[8,20,128]{2,1,0:T(8,128)} %select_maximum_fusion), calls=%async_computation.6 | async-start | bytes 196608 | tf_op jit(solution)/shard_map/all_to_all | solution.py:28
  223.8 16.6 %all-to-all-start.9 = ((f32[8,20,128]{2,1,0:T(8,128)}), f32[8,20,128]{2,1,0:T(8,128)S(1)}, u32[]{:S(2)}, u32[]{:S(2)}) async-start(f32[8,20,128]{2,1,0:T(8,128)} %broadcast_in_dim.49), calls=%async_computation.9 | async-start | bytes 196608 | tf_op jit(solution)/shard_map/all_to_all | solution.py:28
Sparse Core Ops, SparseCore 0:
  19.5 99.1 all-gather.1

commit v5 on v4

--- a/solution.py
+++ b/solution.py
@@ -178,6 +178,89 @@
     )(sums, query, gain[None], last, weights)
 
 
+def split(x):
+    high = x.astype(bf16)
+    return high, (x - high.astype(f32)).astype(bf16)
+
+
+def back_kernel(
+    sums_ref,
+    inverse_ref,
+    scale_ref,
+    normed_ref,
+    select_ref,
+    w_three_ref,
+    slope_two_ref,
+    one_t_ref,
+    w_two_t_ref,
+    slope_one_ref,
+    pose_t_ref,
+    pair_ref,
+    slot_ref,
+    small_ref,
+):
+    width = normed_ref.shape[1]
+    full = N_TP * width
+    sums = jnp.sum(sums_ref[...], axis=0)
+    sums = [sums[k : k + 1] for k in range(6)]
+    rinv = lax.rsqrt(sums[0] / full + epsilon)
+    pull = sums[1] / full * rinv * rinv * rinv
+    grad_mean = (sums[3] * rinv - sums[2] * pull) / full
+    grad_cross = ((sums[1] - sums[5]) * rinv - (sums[0] - sums[4]) * pull) / full
+    total = sum(pair_ref[k].astype(f32) for k in range(pair_ref.shape[0]))
+    normed_grad = total * (1.0 + scale_ref[...])
+    latent_grad = across(inverse_ref[...], width) * (
+        normed_grad - across(grad_mean, width) - normed_ref[...] * across(grad_cross, width)
+    )
+    slot_grad = dot(select_ref[...], latent_grad.astype(bf16), ((1,), (0,))).astype(bf16)
+    slot_ref[...] = slot_grad
+    two_grad = dot(slot_grad, w_three_ref[...], ((1,), (1,))) * slope_two_ref[...]
+    part = w_two_t_ref.shape[0]
+    grad_two = jnp.zeros((part, part), f32)
+    one_grad = []
+    for k in range(two_grad.shape[1] // part):
+        here = slice(k * part, (k + 1) * part)
+        back_one = 0.0
+        for piece in split(two_grad[:, here]):
+            grad_two += jnp.dot(one_t_ref[here, :], piece, preferred_element_type=f32)
+            back_one += jnp.dot(piece, w_two_t_ref[...], preferred_element_type=f32)
+        one_grad.append(back_one * slope_one_ref[:, here])
+    one_grad = jnp.concatenate(one_grad, axis=1)
+    cross = sum(
+        jnp.dot(pose_t_ref[...], piece, preferred_element_type=f32) for piece in split(one_grad)
+    )
+    cell = lax.broadcasted_iota(jnp.int32, cross.shape, 0) >> 4
+    block = lax.broadcasted_iota(jnp.int32, cross.shape, 1) >> 5
+    holds = (block & 8) + ((block & 2) << 1) + ((block & 4) >> 1) + (block & 1)
+    cross = jnp.where(cell == holds, cross, 0.0)
+    cross = sum(cross[16 * k : 16 * (k + 1)] for k in range(16))
+    cross = sum(cross[:, 128 * k : 128 * (k + 1)] for k in range(4))
+    cross = cross + pltpu.roll(cross, 64, 1)
+    grad_one = cross + pltpu.roll(cross, 32, 1)
+    rows_two, rows_one = part // N_TP, 16 // N_TP
+    for k in range(N_TP):
+        small_ref[k, :rows_two] = grad_two[k * rows_two : (k + 1) * rows_two]
+        small_ref[k, rows_two:] = jnp.concatenate(
+            [grad_one[k * rows_one : (k + 1) * rows_one], jnp.zeros((4 - rows_one, part), f32)]
+        )
+
+
+def back(*operands):
+    normed, select, w_two_t = operands[3], operands[4], operands[8]
+    part = w_two_t.shape[0]
+    return pl.pallas_call(
+        back_kernel,
+        name="back",
+        out_shape=(
+            jax.ShapeDtypeStruct((select.shape[0], normed.shape[1]), bf16),
+            jax.ShapeDtypeStruct((N_TP, part // N_TP + 4, part), f32),
+        ),
+        in_specs=in_vmem(len(operands)),
+        out_specs=tuple(in_vmem(2)),
+        compiler_params=pltpu.CompilerParams(vmem_limit_bytes=VMEM_LIMIT),
+    )(*operands)
+
+
 def halves(x):
     high = lax.reduce_precision(x, 8, 7)
     return jnp.stack([high, x - high]).astype(bf16)
@@ -208,7 +291,6 @@
     full_width = width * N_TP
     query_width = cols * N_TP
     slots = N_SEQ * CAP
-    c = lax.axis_index("c")
 
     w_rows = copies(w_query, "x", N_X).reshape(N_X * w_query.shape[0], cols)
     w_rows, pose_rows, dest_device, dest_slot = lax.optimization_barrier(
@@ -221,19 +303,34 @@
     earlier = jnp.arange(rows)[:, None] > jnp.arange(rows)[None, :]
     before = dot(earlier.astype(bf16), marks.astype(bf16), ((1,), (0,)))
     rank = jnp.sum(jnp.where(marks, before, 0.0), axis=1).astype(jnp.int32)
-    position = owner * CAP + rank
-    place = (jnp.arange(slots, dtype=jnp.int32)[:, None] == position[None, :]).astype(bf16)
-    half = pose_rows.shape[1] // 2
-    pose_half = lax.dynamic_slice_in_dim(pose_rows, c * half, half, axis=1)
-    label = jnp.broadcast_to((dest_slot + 1).astype(bf16)[:, None], (rows, half))
-    packed = dot(place, jnp.concatenate([pose_half, label], axis=1), ((1,), (0,))).astype(bf16)
-    outgoing = jnp.concatenate(
-        [packed[:, :half].reshape(N_SEQ, CAP, half), packed[:, half:].reshape(N_SEQ, CAP, half)],
-        axis=1,
-    )
-    incoming = exchange(outgoing, SEQ)
-    pose = lax.all_gather(incoming[:, :CAP].reshape(slots, half), "c", axis=1, tiled=True)
-    slot = incoming[:, CAP:, :1].reshape(slots, 1).astype(jnp.int32) - 1
+    share = pose_rows.shape[1] // N_TP
+    lane = jnp.arange(4 * share, dtype=jnp.int32)
+    side, column = lane // (2 * share), lane % (2 * share)
+    mine = lax.axis_index("y") * N_C + lax.axis_index("c")
+    pick = (jnp.arange(pose_rows.shape[1])[:, None] == mine * share + column) & (column < share)
+    line_data = dot(pose_rows, pick.astype(bf16), ((1,), (0,)))
+    line_data = jnp.where(column == share, (dest_slot + 1).astype(f32)[:, None], line_data)
+    line_data = jnp.where(side == rank[:, None] // (CAP // 2), line_data, 0.0).astype(bf16)
+    line = owner * (CAP // 2) + rank % (CAP // 2)
+    lines = slots // 2
+    place = (jnp.arange(lines, dtype=jnp.int32)[:, None] == line[None, :]).astype(bf16)
+    outgoing = dot(place, line_data, ((1,), (0,))).astype(bf16)
+    incoming = exchange(outgoing.reshape(N_SEQ, CAP // 2, 4 * share), SEQ)
+    incoming = incoming.reshape(lines, 4 * share)
+    pieces = copies(incoming, TP, N_TP).transpose(1, 0, 2).reshape(lines, N_TP * 4 * share)
+    source = jnp.arange(N_TP * 4 * share, dtype=jnp.int32)
+    origin, source = source // (4 * share), source % (4 * share)
+    to = jnp.where(
+        source % (2 * share) < share,
+        source // (2 * share) * N_TP * share + origin * share + source % (2 * share),
+        -1,
+    )
+    order = (to[:, None] == jnp.arange(2 * N_TP * share, dtype=jnp.int32)[None, :]).astype(bf16)
+    pose = dot(pieces, order, ((1,), (0,))).astype(bf16)
+    pose = jnp.concatenate([pose[:, : N_TP * share], pose[:, N_TP * share :]])
+    slot = jnp.concatenate(
+        [incoming[:, share : share + 1], incoming[:, 3 * share : 3 * share + 1]]
+    ).astype(jnp.int32) - 1
     select = (slot == jnp.arange(tokens, dtype=jnp.int32)[None, :]).astype(bf16)
 
     cell_in, c_one = w_section1.shape
@@ -270,9 +367,23 @@
     extra = jnp.pad(extra, ((0, 12), (0, 0)))
     own = copies(jnp.concatenate([modulated, extra]), "y", N_Y)
     other = swap_cores(own)
-    normed, slope_one, slope_two, other = lax.optimization_barrier(
-        (normed, silu_slope(z_one), silu_slope(z_two), other)
-    )
+    per = stacked_two.shape[1] // N_SEQ
+    row = jnp.arange(stacked_two.shape[1], dtype=jnp.int32)
+    leaves = row // per % N_X * (N_Z * per) + row // (per * N_X) * per + row % per
+    order = (leaves[:, None] == row[None, :]).astype(bf16)
+    ready = (
+        normed,
+        inverse.reshape(1, tokens),
+        select,
+        dot(stacked_two, order, ((1,), (0,))).astype(bf16),
+        silu_slope(z_two),
+        stacked_one.T,
+        silu_slope(z_one),
+        pose.T,
+        w_section2.T,
+    )
+    ready, other = lax.optimization_barrier((ready, other))
+    normed, inverse, select, leaving_two, slope_two, one_t, slope_one, pose_t, w_two_t = ready
 
     query, sums = query_matmul(own, other, bias_query, gain_query, cotangent, weights)
     sums = exchange(sums, TP)
@@ -283,47 +394,26 @@
     mine, normed_query = partial_matmul(
         mine_kernel, "mine", sums, query, gain_query, query_grad, weights
     )
-    sums = jnp.sum(sums, axis=0)
-    rinv = lax.rsqrt(sums[0] / query_width + epsilon)
-    pull = sums[1] / query_width * rinv**3
-    grad_mean = ((sums[3] * rinv - sums[2] * pull) / full_width)[:, None]
-    grad_cross = (((sums[1] - sums[5]) * rinv - (sums[0] - sums[4]) * pull) / full_width)[:, None]
     pair = (mine.astype(f32) + theirs.astype(f32)).astype(bf16)
-    modulated_grad = jnp.sum(exchange(pair, "y").astype(f32), axis=0)
-    normed_grad = modulated_grad * (1.0 + scale_mod)
-    latent_grad = (inverse * (normed_grad - grad_mean - normed * grad_cross)).astype(bf16)
-
-    slot_grad = dot(select, latent_grad, ((1,), (0,))).astype(bf16)
-    grad_three = dot(stacked_two, slot_grad, ((0,), (0,))).astype(bf16)
-    per = grad_three.shape[0] // N_SEQ
-    grad_three = grad_three.reshape(N_Z, N_X, per, width).transpose(1, 0, 2, 3)
-
-    two_grad = dot(slot_grad, w_section3, ((1,), (1,))) * slope_two
-    grad_two = sum(
-        dot(
-            stacked_one[:, k * c_two : (k + 1) * c_two].astype(f32),
-            two_grad[:, k * c_two : (k + 1) * c_two],
-            ((0,), (0,)),
-            lax.Precision.HIGHEST,
-        )
-        for k in range(4)
-    )
-    one_grad = dot(two_grad, w_two.astype(f32), ((1,), (1,)), lax.Precision.HIGHEST) * slope_one
-    cross = dot(pose.astype(f32), one_grad, ((0,), (0,)), lax.Precision.HIGHEST)
-    cross = jnp.where(cell_mask, cross, 0.0)
-    cross = jnp.sum(cross.reshape(16, cell_in, 16 * c_one), axis=0)
-    grad_one = sum(cross[:, k * c_one : (k + 1) * c_one] for k in range(16))
+    pair = exchange(pair, "y")
+    slot_grad, small = back(
+        sums,
+        inverse,
+        scale_mod[None],
+        normed,
+        select,
+        w_section3,
+        slope_two,
+        one_t,
+        w_two_t,
+        slope_one,
+        pose_t,
+        pair,
+    )
+    grad_three = dot(leaving_two, slot_grad, ((0,), (0,))).astype(bf16)
 
     rows_two = c_two // N_TP
-    left = grad_one.size // N_TP
     lines = 4
-    small = jnp.concatenate(
-        [
-            grad_two.reshape(N_TP, rows_two, c_two),
-            jnp.pad(grad_one.reshape(N_TP, 1, left), ((0, 0), (0, 3), (0, c_two - left))),
-        ],
-        axis=1,
-    )
     small = jnp.sum(exchange(small, TP), axis=0).astype(bf16).reshape(1, lines, width)
     shares = jnp.concatenate(
         [
@@ -343,8 +433,9 @@
     total = jnp.sum(exchange(shares, "z").astype(f32), axis=0)
     section_three_grad = total[:per]
     small = copies(total[per:].reshape(lines * width // c_two, c_two), TP, N_TP)
-    section_two_grad = small[:, :rows_two].reshape(grad_two.shape)
-    section_one_grad = small[:, rows_two, :left].reshape(grad_one.shape)
+    section_two_grad = small[:, :rows_two].reshape(c_two, c_two)
+    section_one_grad = small[:, rows_two : rows_two + cell_in // N_TP, :c_one]
+    section_one_grad = section_one_grad.reshape(cell_in, c_one)
     return (normed_query, section_three_grad, section_two_grad, section_one_grad)
 
 

time: 249 us -> 240 us (0.964)
  blocking collectives: 87.8 us -> 75.2 us
  starting transfers between devices: 47.7 us -> 55.1 us
  local copies, waits for them, and re-layouts: 7.99 us -> 13.8 us
  waiting for transfers between devices: 58.1 us -> 52.4 us
  matrix products: 14.8 us -> 9.77 us
  Pallas kernels: 12.1 us -> 15.1 us
  other arithmetic: 5.43 us -> 2.84 us
    all_gather x1 -> x0, blocking collectives: 8.86 us -> none  [body(): lax.all_gather(incoming[:, :CAP].reshape(slots, half), 'c', axis=1, tiled...]
    all_gather x1, waiting for transfers between devices: 7.65 us -> 0.01 us  [body(): lax.all_gather(w_rows, 'z', axis=0, tiled=True).reshape(N_TP, width, cols)]
    all_to_all x5 -> x6, starting transfers between devices: 41.6 us -> 48.9 us  [exchange(): return lax.all_to_all(x, axis, split_axis=0, concat_axis=0, tiled=True)]
    dot_general x14 -> x8, matrix products: 14.8 us -> 9.77 us  [dot(): lax.dot_general(a, b, (dims, ((), ())), precision=precision, preferred_el...]
    all_to_all x5 -> x6, waiting for transfers between devices: 47.7 us -> 52.3 us  [exchange(): return lax.all_to_all(x, axis, split_axis=0, concat_axis=0, tiled=True)]
    all_to_all x5, blocking collectives: 78.9 us -> 75.2 us  [exchange(): return lax.all_to_all(x, axis, split_axis=0, concat_axis=0, tiled=True)]
    unnamed x42 -> x41, local copies, waits for them, and re-layouts: 1.87 us -> 5.47 us
    pallas_call x0 -> x1, Pallas kernels: none -> 2.89 us  [back(): pl.pallas_call(back_kernel, name='back', out_shape=(jax.ShapeDtypeStruct(...]
  transfers between devices with their start and end apart: 8 -> 9, of which waited for: 7 -> 6; matrix products, arithmetic and copies ran while one was open for 5% -> 7% of each run, Pallas kernels for 1% -> 1%
where the time goes in v5:
time: 240 us; the launch traced here: 239 us
  blocking collectives  75.2 us (31%)
  starting transfers between devices  55.1 us (23%)
  waiting for transfers between devices  52.4 us (22%)
  Pallas kernels  15.1 us (6%)
  between operations  14.6 us (6%)
  local copies, waits for them, and re-layouts  13.8 us (6%)
  matrix products  9.77 us (4%)
  other arithmetic  2.84 us (1%)
    all_to_all x5, blocking collectives, exchange(): return lax.all_to_all(x, axis, split_axis=0, concat_axis=0, tiled=True)  75.2 us
    all_to_all x6, waiting for transfers between devices, exchange(): return lax.all_to_all(x, axis, split_axis=0, concat_axis=0, tiled=True)  52.3 us
    all_to_all x6, starting transfers between devices, exchange(): return lax.all_to_all(x, axis, split_axis=0, concat_axis=0, tiled=True)  48.9 us
    dot_general x8, matrix products, dot(): lax.dot_general(a, b, (dims, ((), ())), precision=precision, preferred_el...  9.77 us
    ppermute x2, starting transfers between devices, swap_cores(): return lax.ppermute(x, 'c', [(0, 1), (1, 0)])  6.16 us
    pallas_call x1, Pallas kernels, query_matmul(): pl.pallas_call(query_kernel, name='query', out_shape=(jax.ShapeDtypeStruc...  6.16 us
    pallas_call x2, Pallas kernels, partial_matmul(): pl.pallas_call(kernel, name=name, out_shape=(jax.ShapeDtypeStruct((groups...  6.08 us
    unnamed x41, local copies, waits for them, and re-layouts  5.47 us
  transfers between devices with their start and end apart: 9, of which 6 were waited for; matrix products, arithmetic and copies ran while one was open for 7% of the time, Pallas kernels for 1%

profile of v5, /device:TPU:1, one launch (start us, length us, event | category | flops | bytes accessed | tf_op | source)
XLA Modules:
  0.0 238.8 jit_solution(3868724321351531325)
XLA Ops:
  8.2 11.1 %all_to_all.55 = bf16[4,80,640]{2,1,0:T(8,128)(2,1)} all-to-all(bf16[4,80,640]{2,1,0:T(8,128)(2,1)S(1)} %broadcast_in_dim.54), channel_id=1, replica_groups=mesh['z'=16,'x'=4,'y'=4,'c'=2] {'x'}, dimensions={0} | all-to-all | bytes 819200 | tf_op jit(solution)/shard_map/all_to_all | solution.py:28
  20.7 17.4 %all-to-all-start.1 = ((bf16[64,4,128]{2,1,0:T(4,128)(2,1)}), bf16[64,4,128]{2,1,0:T(4,128)(2,1)S(1)}, u32[]{:S(2)}, u32[]{:S(2)}) async-start(bf16[64,4,128]{2,1,0:T(4,128)(2,1)} %bitcast.2), calls=%async_computation.1 | async-start | bytes 131072 | tf_op jit(solution)/shard_map/all_to_all | solution.py:28
  38.1 14.1 %all-to-all-done.1 = bf16[64,4,128]{2,1,0:T(4,128)(2,1)S(1)} async-done(((bf16[64,4,128]{2,1,0:T(4,128)(2,1)}), bf16[64,4,128]{2,1,0:T(4,128)(2,1)S(1)}, u32[]{:S(2)}, u32[]{:S(2)}) %all-to-all-start.1) | async-done | bytes 65568 | tf_op jit(solution)/shard_map/all_to_all | solution.py:28
  53.2 8.2 %all-to-all-start.2 = ((bf16[8,256,128]{1,2,0:T(8,128)(2,1)}), bf16[8,256,128]{1,2,0:T(8,128)(2,1)S(1)}, u32[]{:S(2)}, u32[]{:S(2)}) async-start(bf16[8,256,128]{1,2,0:T(8,128)(2,1)} %broadcast_in_dim.59), calls=%async_computation.2 | async-start | bytes 1048576 | tf_op jit(solution)/shard_map/all_to_all | solution.py:28
  62.9 8.0 %all-to-all-done.2 = bf16[8,256,128]{1,2,0:T(8,128)(2,1)S(1)} async-done(((bf16[8,256,128]{1,2,0:T(8,128)(2,1)}), bf16[8,256,128]{1,2,0:T(8,128)(2,1)S(1)}, u32[]{:S(2)}, u32[]{:S(2)}) %all-to-all-start.2) | async-done | bytes 524320 | tf_op jit(solution)/shard_map/all_to_all | solution.py:28
  71.8 1.6 add_multiply_fusion
  73.6 1.8 add_multiply_fusion.1
  77.2 4.1 %all-to-all-start.3 = ((f32[8,2,256]{2,1,0:T(2,128)}), f32[8,2,256]{2,1,0:T(2,128)S(1)}, u32[]{:S(2)}, u32[]{:S(2)}) async-start(f32[8,2,256]{2,1,0:T(2,128)} %broadcast_in_dim.62), calls=%async_computation.3 | async-start | bytes 32768 | tf_op jit(solution)/shard_map/all_to_all | solution.py:28
  81.4 4.7 %all-to-all-done.3 = f32[8,2,256]{2,1,0:T(2,128)S(1)} async-done(((f32[8,2,256]{2,1,0:T(2,128)}), f32[8,2,256]{2,1,0:T(2,128)S(1)}, u32[]{:S(2)}, u32[]{:S(2)}) %all-to-all-start.3) | async-done | bytes 16416 | tf_op jit(solution)/shard_map/all_to_all | solution.py:28
  86.6 21.3 %all_to_all.56.own_ref = bf16[4,272,640]{2,1,0:T(8,128)(2,1)} all-to-all(bf16[4,272,640]{2,1,0:T(8,128)(2,1)S(1)} %broadcast_in_dim.63), channel_id=1, replica_groups=mesh['z'=16,'x'=4,'y'=4,'c'=2] {'y'}, dimensions={0} | all-to-all | bytes 2785280 | tf_op jit(solution)/shard_map/all_to_all | solution.py:28
  107.9 3.5 %collective-permute-start = (bf16[4,272,640]{2,1,0:T(8,128)(2,1)}, bf16[4,272,640]{2,1,0:T(8,128)(2,1)}, u32[]{:S(2)}, u32[]{:S(2)}) collective-permute-start(bf16[4,272,640]{2,1,0:T(8,128)(2,1)} %all_to_all.56.own_ref), channel_id=1, source_target_pairs={{0,1},{1,0},{2,3},{3,2},{4,5},{5,4},{6,7},{7,6},{8,9},{9,8},{10,11... | collective-permute-start | bytes 4177928 | tf_op jit(solution)/shard_map/ppermute | solution.py:270
  111.7 1.6 copy.55
  114.5 1.4 convolution_convert_fusion.2
  115.9 6.2 %query.1 = (f32[256,640]{1,0:T(8,128)S(1)}, f32[8,8,256]{2,1,0:T(8,128)S(1)}) custom-call(f32[1,640]{1,0:T(1,128)S(1)} %broadcast_in_dim.52.bias_ref, f32[1,640]{1,0:T(1,128)S(1)} %broadcast_in_dim.53.gain_ref, bf16[256,640]{1,0:T(8,128)(2,1)S(1)} %copy-done.2, bf16[4,272,640]{2,1,0:T(8,128)(2,1)} %all_to_all.56.own_ref, ...), custom_call_target="tpu_custom_call" | custom-call | tf_op jit(solution)/shard_map/query/pallas_call | solution.py:100
  122.1 7.4 %all_to_all.57.sums_ref = f32[8,8,256]{2,1,0:T(8,128)S(1)} all-to-all(f32[8,8,256]{2,1,0:T(8,128)S(1)} %get-tuple-element.31), channel_id=1, replica_groups=mesh['z'=16,'x'=4,'y'=4,'c'=2] {'y','c'}, dimensions={0} | all-to-all | bytes 131072 | tf_op jit(solution)/shard_map/all_to_all | solution.py:28
  129.5 2.8 %theirs.1 = (bf16[4,256,640]{2,1,0:T(8,128)(2,1)S(1)}, bf16[256,640]{1,0:T(8,128)(2,1)S(1)}) custom-call(f32[8,8,256]{2,1,0:T(8,128)S(1)} %all_to_all.57.sums_ref, f32[256,640]{1,0:T(8,128)S(1)} %get-tuple-element.32.query_ref, f32[1,640]{1,0:T(1,128)S(1)} %broadcast_in_dim.53.gain_ref, bf16[256,640]{1,0:T(8,128)(2,1)S(1)} %copy-done.2, ...), custom_call_target="tpu_custom_call" | custom-call | flops 838860800 | bytes 3276800 | tf_op jit(solution)/shard_map/theirs/pallas_call | solution.py:159
  132.3 2.7 %collective-permute-start.1 = (bf16[4,256,640]{2,1,0:T(8,128)(2,1)S(1)}, bf16[4,256,640]{2,1,0:T(8,128)(2,1)S(1)}, u32[]{:S(2)}, u32[]{:S(2)}) collective-permute-start(bf16[4,256,640]{2,1,0:T(8,128)(2,1)S(1)} %get-tuple-element.45), channel_id=1, source_target_pairs={{0,1},{1,0},{2,3},{3,2},{4,5},{5,4},{6,7},{7,6},{8,9},{9,8},{10,11... | collective-permute-start | bytes 3932168 | tf_op jit(solution)/shard_map/ppermute | solution.py:270
  135.0 3.3 %mine.1 = (bf16[4,256,640]{2,1,0:T(8,128)(2,1)S(1)}, bf16[256,640]{1,0:T(8,128)(2,1)}) custom-call(f32[8,8,256]{2,1,0:T(8,128)S(1)} %all_to_all.57.sums_ref, f32[256,640]{1,0:T(8,128)S(1)} %get-tuple-element.32.query_ref, f32[1,640]{1,0:T(1,128)S(1)} %broadcast_in_dim.53.gain_ref, bf16[256,640]{1,0:T(8,128)(2,1)S(1)} %get-tuple-element.33.grad_ref, ...), custom_call_target="tpu_custom_call" | custom-call | flops 838860800 | bytes 3276800 | tf_op jit(solution)/shard_map/mine/pallas_call | solution.py:159
  138.3 1.4 add_convert_fusion
  139.7 3.5 %all-to-all-start.6 = ((bf16[4,256,640]{2,1,0:T(8,128)(2,1)}), bf16[4,256,640]{2,1,0:T(8,128)(2,1)S(1)}, u32[]{:S(2)}, u32[]{:S(2)}) async-start(bf16[4,256,640]{2,1,0:T(8,128)(2,1)} %add_convert_fusion), calls=%async_computation.6 | async-start | bytes 2621440 | tf_op jit(solution)/shard_map/all_to_all | solution.py:28
  143.3 18.0 %all-to-all-done.6.pair_ref = bf16[4,256,640]{2,1,0:T(8,128)(2,1)S(1)} async-done(((bf16[4,256,640]{2,1,0:T(8,128)(2,1)}), bf16[4,256,640]{2,1,0:T(8,128)(2,1)S(1)}, u32[]{:S(2)}, u32[]{:S(2)}) %all-to-all-start.6) | async-done | bytes 1310752 | tf_op jit(solution)/shard_map/all_to_all | solution.py:28
  161.3 1.2 copy-done.3
  162.5 1.2 copy-done.4
  163.7 1.1 copy-done.6
  164.8 2.9 %back.1 = (bf16[512,640]{1,0:T(8,128)(2,1)S(1)}, f32[8,20,128]{2,1,0:T(8,128)}) custom-call(f32[8,8,256]{2,1,0:T(8,128)S(1)} %all_to_all.57.sums_ref, f32[1,256]{1,0:T(1,128)S(1)} %bitcast.58, f32[1,640]{1,0:T(1,128)S(1)} %broadcast_in_dim.64.scale_ref, f32[256,640]{1,0:T(8,128)S(1)} %get-tuple-element.37.normed_ref, ...), custom_call_target="tpu_custom_call" | custom-call | tf_op jit(solution)/shard_map/back/pallas_call | solution.py:251
  168.6 4.1 %all-to-all-start.7 = ((f32[8,20,128]{2,1,0:T(8,128)}), f32[8,20,128]{2,1,0:T(8,128)S(1)}, u32[]{:S(2)}, u32[]{:S(2)}) async-start(f32[8,20,128]{2,1,0:T(8,128)} %get-tuple-element.47), calls=%async_computation.7 | async-start | bytes 196608 | tf_op jit(solution)/shard_map/all_to_all | solution.py:28
  172.6 1.8 convolution_convert_fusion
  174.5 3.1 %all-to-all-done.7 = f32[8,20,128]{2,1,0:T(8,128)S(1)} async-done(((f32[8,20,128]{2,1,0:T(8,128)}), f32[8,20,128]{2,1,0:T(8,128)S(1)}, u32[]{:S(2)}, u32[]{:S(2)}) %all-to-all-start.7) | async-done | bytes 81952 | tf_op jit(solution)/shard_map/all_to_all | solution.py:28
  177.7 14.0 %all_to_all.58 = bf16[4,132,640]{2,1,0:T(8,128)(2,1)S(1)} all-to-all(bf16[4,132,640]{2,1,0:T(8,128)(2,1)S(1)} %pad_maximum_fusion), channel_id=1, replica_groups=mesh['z'=16,'x'=4,'y'=4,'c'=2] {'x'}, dimensions={0} | all-to-all | bytes 1351680 | tf_op jit(solution)/shard_map/all_to_all | solution.py:28
  192.0 21.4 %all_to_all.59 = bf16[16,12,640]{2,1,0:T(8,128)(2,1)S(1)} all-to-all(bf16[16,12,640]{2,1,0:T(8,128)(2,1)S(1)} %pad_maximum_fusion.2), channel_id=1, replica_groups=mesh['z'=16,'x'=4,'y'=4,'c'=2] {'z'}, dimensions={0} | all-to-all | bytes 491520 | tf_op jit(solution)/shard_map/all_to_all | solution.py:28
  214.2 11.6 %all-to-all-start.10 = ((f32[8,20,128]{2,1,0:T(8,128)}), f32[8,20,128]{2,1,0:T(8,128)S(1)}, u32[]{:S(2)}, u32[]{:S(2)}) async-start(f32[8,20,128]{2,1,0:T(8,128)} %broadcast_in_dim.68), calls=%async_computation.10 | async-start | bytes 196608 | tf_op jit(solution)/shard_map/all_to_all | solution.py:28
  226.3 4.4 %all-to-all-done.10 = f32[8,20,128]{2,1,0:T(8,128)S(1)} async-done(((f32[8,20,128]{2,1,0:T(8,128)}), f32[8,20,128]{2,1,0:T(8,128)S(1)}, u32[]{:S(2)}, u32[]{:S(2)}) %all-to-all-start.10) | async-done | bytes 81952 | tf_op jit(solution)/shard_map/all_to_all | solution.py:28
  (105 shorter events, 13.4 us)
Async XLA Ops:
  7.2 12.5 %copy-start = (bf16[256,256]{1,0:T(8,128)(2,1)S(1)}, bf16[256,256]{1,0:T(8,128)(2,1)}, u32[]{:S(2)}) copy-start(bf16[256,256]{1,0:T(8,128)(2,1)} %param.14) | copy-start | bytes 393220
  7.2 12.2 %copy-start.15 = (s32[256,1]{0,1:T(1,128)S(1)}, s32[256,1]{0,1:T(1,128)}, u32[]{:S(2)}) copy-start(s32[256,1]{0,1:T(1,128)} %param.15) | copy-start | bytes 3076
  7.2 12.4 %copy-start.17 = (s32[256]{0:T(256)S(1)}, s32[256]{0:T(256)}, u32[]{:S(2)}) copy-start(s32[256]{0:T(256)} %param.16) | copy-start | bytes 3076
  7.2 12.2 %copy-start.10 = (f32[640]{0:T(1024)S(1)}, f32[640]{0:T(1024)}, u32[]{:S(2)}) copy-start(f32[640]{0:T(1024)} %param.20) | copy-start | bytes 7684
  7.2 30.9 %copy-start.11 = (f32[640]{0:T(1024)S(1)}, f32[640]{0:T(1024)}, u32[]{:S(2)}) copy-start(f32[640]{0:T(1024)} %param.21) | copy-start | bytes 7684
  7.2 108.7 %all-gather.2.cloned.1.call-start = ((), (), s32[]{:S(2)}) async-start(), calls=%async_computation.11 | async-start | bytes 6963200 | tf_op jit(solution)/shard_map/all_gather | solution.py:299
  19.3 42.1 %copy-start.12 = (bf16[16,32]{1,0:T(8,128)(2,1)S(1)}, bf16[16,32]{1,0:T(8,128)(2,1)}, u32[]{:S(2)}) copy-start(bf16[16,32]{1,0:T(8,128)(2,1)} %param.17) | copy-start | bytes 3076
  20.7 31.5 %all-to-all-start.1 = ((bf16[64,4,128]{2,1,0:T(4,128)(2,1)}), bf16[64,4,128]{2,1,0:T(4,128)(2,1)S(1)}, u32[]{:S(2)}, u32[]{:S(2)}) async-start(bf16[64,4,128]{2,1,0:T(4,128)(2,1)} %bitcast.2), calls=%async_computation.1 | async-start | bytes 131072 | tf_op jit(solution)/shard_map/all_to_all | solution.py:28
  53.2 17.7 %all-to-all-start.2 = ((bf16[8,256,128]{1,2,0:T(8,128)(2,1)}), bf16[8,256,128]{1,2,0:T(8,128)(2,1)S(1)}, u32[]{:S(2)}, u32[]{:S(2)}) async-start(bf16[8,256,128]{1,2,0:T(8,128)(2,1)} %broadcast_in_dim.59), calls=%async_computation.2 | async-start | bytes 1048576 | tf_op jit(solution)/shard_map/all_to_all | solution.py:28
  71.8 1.6 copy-start.9
  73.4 1.9 copy-start.8
  73.6 1.8 copy-start.5
  73.6 1.8 copy-start.16
  75.3 1.1 copy-start.18
  77.2 8.9 %all-to-all-start.3 = ((f32[8,2,256]{2,1,0:T(2,128)}), f32[8,2,256]{2,1,0:T(2,128)S(1)}, u32[]{:S(2)}, u32[]{:S(2)}) async-start(f32[8,2,256]{2,1,0:T(2,128)} %broadcast_in_dim.62), calls=%async_computation.3 | async-start | bytes 32768 | tf_op jit(solution)/shard_map/all_to_all | solution.py:28
  86.5 25.0 %copy-start.13 = (f32[640]{0:T(1024)S(1)}, f32[640]{0:T(1024)}, u32[]{:S(2)}) copy-start(f32[640]{0:T(1024)} %param.24) | copy-start | bytes 7684
  86.5 25.0 %copy-start.14 = (f32[640]{0:T(1024)S(1)}, f32[640]{0:T(1024)}, u32[]{:S(2)}) copy-start(f32[640]{0:T(1024)} %param.23) | copy-start | bytes 7684
  107.9 8.0 %collective-permute-start = (bf16[4,272,640]{2,1,0:T(8,128)(2,1)}, bf16[4,272,640]{2,1,0:T(8,128)(2,1)}, u32[]{:S(2)}, u32[]{:S(2)}) collective-permute-start(bf16[4,272,640]{2,1,0:T(8,128)(2,1)} %all_to_all.56.own_ref), channel_id=1, source_target_pairs={{0,1},{1,0},{2,3},{3,2},{4,5},{5,4},{6,7},{7,6},{8,9},{9,8},{10,11... | collective-permute-start | bytes 4177928 | tf_op jit(solution)/shard_map/ppermute | solution.py:270
  113.2 1.2 copy-start.19
  114.5 1.4 copy-start.2
  115.9 13.6 %copy-start.1 = (bf16[5120,640]{1,0:T(8,128)(2,1)S(1)}, bf16[5120,640]{1,0:T(8,128)(2,1)}, u32[]{:S(2)}) copy-start(bf16[5120,640]{1,0:T(8,128)(2,1)} %all-gather.2.cloned.1.call-done) | copy-start | bytes 19660804
  132.3 6.0 %collective-permute-start.1 = (bf16[4,256,640]{2,1,0:T(8,128)(2,1)S(1)}, bf16[4,256,640]{2,1,0:T(8,128)(2,1)S(1)}, u32[]{:S(2)}, u32[]{:S(2)}) collective-permute-start(bf16[4,256,640]{2,1,0:T(8,128)(2,1)S(1)} %get-tuple-element.45), channel_id=1, source_target_pairs={{0,1},{1,0},{2,3},{3,2},{4,5},{5,4},{6,7},{7,6},{8,9},{9,8},{10,11... | collective-permute-start | bytes 3932168 | tf_op jit(solution)/shard_map/ppermute | solution.py:270
  139.7 21.6 %all-to-all-start.6 = ((bf16[4,256,640]{2,1,0:T(8,128)(2,1)}), bf16[4,256,640]{2,1,0:T(8,128)(2,1)S(1)}, u32[]{:S(2)}, u32[]{:S(2)}) async-start(bf16[4,256,640]{2,1,0:T(8,128)(2,1)} %add_convert_fusion), calls=%async_computation.6 | async-start | bytes 2621440 | tf_op jit(solution)/shard_map/all_to_all | solution.py:28
  161.3 1.2 copy-start.3
  162.5 1.2 copy-start.4
  163.7 1.1 copy-start.6
  167.7 0.8 copy-start.7
  168.6 9.1 %all-to-all-start.7 = ((f32[8,20,128]{2,1,0:T(8,128)}), f32[8,20,128]{2,1,0:T(8,128)S(1)}, u32[]{:S(2)}, u32[]{:S(2)}) async-start(f32[8,20,128]{2,1,0:T(8,128)} %get-tuple-element.47), calls=%async_computation.7 | async-start | bytes 196608 | tf_op jit(solution)/shard_map/all_to_all | solution.py:28
  214.2 16.6 %all-to-all-start.10 = ((f32[8,20,128]{2,1,0:T(8,128)}), f32[8,20,128]{2,1,0:T(8,128)S(1)}, u32[]{:S(2)}, u32[]{:S(2)}) async-start(f32[8,20,128]{2,1,0:T(8,128)} %broadcast_in_dim.68), calls=%async_computation.10 | async-start | bytes 196608 | tf_op jit(solution)/shard_map/all_to_all | solution.py:28
Sparse Core Ops, SparseCore 0:
  19.4 93.2 all-gather.1

commit v6 on v5

--- a/solution.py
+++ b/solution.py
@@ -33,6 +33,7 @@
 
 
 VMEM_LIMIT = 32 * 1024 * 1024
+BACK_VMEM_LIMIT = 56 * 1024 * 1024
 QUERY_VMEM_LIMIT = 52 * 1024 * 1024
 
 
@@ -187,18 +188,53 @@
     sums_ref,
     inverse_ref,
     scale_ref,
+    w_two_t_ref,
+    pair_hbm,
+    normed_hbm,
+    select_hbm,
+    w_three_hbm,
+    slope_two_hbm,
+    one_t_hbm,
+    slope_one_hbm,
+    pose_t_hbm,
+    slot_ref,
+    small_ref,
+    pair_ref,
     normed_ref,
     select_ref,
     w_three_ref,
     slope_two_ref,
     one_t_ref,
-    w_two_t_ref,
     slope_one_ref,
     pose_t_ref,
-    pair_ref,
-    slot_ref,
-    small_ref,
+    sems,
 ):
+    far = (
+        pair_hbm,
+        normed_hbm,
+        select_hbm,
+        w_three_hbm,
+        slope_two_hbm,
+        one_t_hbm,
+        slope_one_hbm,
+        pose_t_hbm,
+    )
+    near = (
+        pair_ref,
+        normed_ref,
+        select_ref,
+        w_three_ref,
+        slope_two_ref,
+        one_t_ref,
+        slope_one_ref,
+        pose_t_ref,
+    )
+    fetches = [
+        pltpu.make_async_copy(source, target, sems.at[k])
+        for k, (source, target) in enumerate(zip(far, near, strict=True))
+    ]
+    for fetch in fetches:
+        fetch.start()
     width = normed_ref.shape[1]
     full = N_TP * width
     sums = jnp.sum(sums_ref[...], axis=0)
@@ -207,6 +243,8 @@
     pull = sums[1] / full * rinv * rinv * rinv
     grad_mean = (sums[3] * rinv - sums[2] * pull) / full
     grad_cross = ((sums[1] - sums[5]) * rinv - (sums[0] - sums[4]) * pull) / full
+    for fetch in fetches[:3]:
+        fetch.wait()
     total = sum(pair_ref[k].astype(f32) for k in range(pair_ref.shape[0]))
     normed_grad = total * (1.0 + scale_ref[...])
     latent_grad = across(inverse_ref[...], width) * (
@@ -214,6 +252,8 @@
     )
     slot_grad = dot(select_ref[...], latent_grad.astype(bf16), ((1,), (0,))).astype(bf16)
     slot_ref[...] = slot_grad
+    for fetch in fetches[3:]:
+        fetch.wait()
     two_grad = dot(slot_grad, w_three_ref[...], ((1,), (1,))) * slope_two_ref[...]
     part = w_two_t_ref.shape[0]
     grad_two = jnp.zeros((part, part), f32)
@@ -241,24 +281,52 @@
     for k in range(N_TP):
         small_ref[k, :rows_two] = grad_two[k * rows_two : (k + 1) * rows_two]
         small_ref[k, rows_two:] = jnp.concatenate(
-            [grad_one[k * rows_one : (k + 1) * rows_one], jnp.zeros((4 - rows_one, part), f32)]
+            [grad_one[k * rows_one : (k + 1) * rows_one], jnp.zeros((8 - rows_one, part), f32)]
         )
 
 
-def back(*operands):
-    normed, select, w_two_t = operands[3], operands[4], operands[8]
-    part = w_two_t.shape[0]
+def back(near, far):
+    normed, select = far[1:3]
+    part = near[3].shape[0]
     return pl.pallas_call(
         back_kernel,
         name="back",
         out_shape=(
             jax.ShapeDtypeStruct((select.shape[0], normed.shape[1]), bf16),
-            jax.ShapeDtypeStruct((N_TP, part // N_TP + 4, part), f32),
+            jax.ShapeDtypeStruct((N_TP, part // N_TP + 8, part), f32),
         ),
-        in_specs=in_vmem(len(operands)),
+        in_specs=in_vmem(len(near)) + [pl.BlockSpec(memory_space=pl.ANY)] * len(far),
         out_specs=tuple(in_vmem(2)),
-        compiler_params=pltpu.CompilerParams(vmem_limit_bytes=VMEM_LIMIT),
-    )(*operands)
+        scratch_shapes=[pltpu.VMEM(x.shape, x.dtype) for x in far]
+        + [pltpu.SemaphoreType.DMA((len(far),))],
+        compiler_params=pltpu.CompilerParams(vmem_limit_bytes=BACK_VMEM_LIMIT),
+    )(*near, *far)
+
+
+def three_kernel(slot_ref, two_t_hbm, out_ref, two_t_ref, sem):
+    fetch = pltpu.make_async_copy(two_t_hbm, two_t_ref, sem)
+    fetch.start()
+    fetch.wait()
+    out_ref[...] = jnp.dot(
+        two_t_ref[...], slot_ref[...], preferred_element_type=f32
+    ).astype(out_ref.dtype)
+
+
+def three(slot_grad, two_t):
+    rows, slots = two_t.shape
+    width = slot_grad.shape[1]
+    return pl.pallas_call(
+        three_kernel,
+        name="three",
+        out_shape=jax.ShapeDtypeStruct((rows, width), bf16),
+        in_specs=in_vmem(1) + [pl.BlockSpec(memory_space=pl.ANY)],
+        out_specs=pl.BlockSpec(memory_space=pltpu.VMEM),
+        scratch_shapes=[pltpu.VMEM(two_t.shape, bf16), pltpu.SemaphoreType.DMA],
+        compiler_params=pltpu.CompilerParams(vmem_limit_bytes=BACK_VMEM_LIMIT),
+        cost_estimate=pl.CostEstimate(
+            flops=2 * rows * slots * width, bytes_accessed=2 * rows * slots, transcendentals=0
+        ),
+    )(slot_grad, two_t)
 
 
 def halves(x):
@@ -366,7 +434,6 @@
     extra = jnp.concatenate([halves(1.0 + scale_mod), halves(shift_mod)])
     extra = jnp.pad(extra, ((0, 12), (0, 0)))
     own = copies(jnp.concatenate([modulated, extra]), "y", N_Y)
-    other = swap_cores(own)
     per = stacked_two.shape[1] // N_SEQ
     row = jnp.arange(stacked_two.shape[1], dtype=jnp.int32)
     leaves = row // per % N_X * (N_Z * per) + row // (per * N_X) * per + row % per
@@ -375,15 +442,16 @@
         normed,
         inverse.reshape(1, tokens),
         select,
-        dot(stacked_two, order, ((1,), (0,))).astype(bf16),
+        dot(order, stacked_two, ((0,), (1,))).astype(bf16),
         silu_slope(z_two),
         stacked_one.T,
         silu_slope(z_one),
         pose.T,
         w_section2.T,
     )
-    ready, other = lax.optimization_barrier((ready, other))
+    ready, own = lax.optimization_barrier((ready, own))
     normed, inverse, select, leaving_two, slope_two, one_t, slope_one, pose_t, w_two_t = ready
+    other = swap_cores(own)
 
     query, sums = query_matmul(own, other, bias_query, gain_query, cotangent, weights)
     sums = exchange(sums, TP)
@@ -397,28 +465,20 @@
     pair = (mine.astype(f32) + theirs.astype(f32)).astype(bf16)
     pair = exchange(pair, "y")
     slot_grad, small = back(
-        sums,
-        inverse,
-        scale_mod[None],
-        normed,
-        select,
-        w_section3,
-        slope_two,
-        one_t,
-        w_two_t,
-        slope_one,
-        pose_t,
-        pair,
-    )
-    grad_three = dot(leaving_two, slot_grad, ((0,), (0,))).astype(bf16)
+        (sums, inverse, scale_mod[None], w_two_t),
+        (pair, normed, select, w_section3, slope_two, one_t, slope_one, pose_t),
+    )
+    grad_three = three(slot_grad, leaving_two)
 
     rows_two = c_two // N_TP
-    lines = 4
-    small = jnp.sum(exchange(small, TP), axis=0).astype(bf16).reshape(1, lines, width)
+    small = jnp.sum(exchange(small, TP), axis=0).astype(bf16)
+    wide = small.shape[0] // per * c_two
+    small = jnp.concatenate([small[k : k + per] for k in range(0, small.shape[0], per)], axis=1)
+    small = jnp.pad(small, ((0, 0), (0, width - wide)))
     shares = jnp.concatenate(
         [
             grad_three.reshape(N_X, N_Z * per, width),
-            jnp.broadcast_to(small, (N_X, lines, width)),
+            jnp.broadcast_to(small[None], (N_X, per, width)),
         ],
         axis=1,
     )
@@ -426,13 +486,14 @@
     shares = jnp.concatenate(
         [
             shares[: N_Z * per].reshape(N_Z, per, width),
-            jnp.broadcast_to(shares[None, N_Z * per :], (N_Z, lines, width)),
+            jnp.broadcast_to(shares[None, N_Z * per :, :wide], (N_Z, per, wide)),
         ],
-        axis=1,
+        axis=2,
     )
     total = jnp.sum(exchange(shares, "z").astype(f32), axis=0)
-    section_three_grad = total[:per]
-    small = copies(total[per:].reshape(lines * width // c_two, c_two), TP, N_TP)
+    section_three_grad = total[:, :width]
+    small = [total[:, k : k + c_two] for k in range(width, width + wide, c_two)]
+    small = copies(jnp.concatenate(small), TP, N_TP)
     section_two_grad = small[:, :rows_two].reshape(c_two, c_two)
     section_one_grad = small[:, rows_two : rows_two + cell_in // N_TP, :c_one]
     section_one_grad = section_one_grad.reshape(cell_in, c_one)

time: 240 us -> 238 us (level)
  blocking collectives: 75.2 us -> 51.1 us
  waiting for transfers between devices: 52.4 us -> 64.3 us
  Pallas kernels: 15.1 us -> 21.6 us
  other arithmetic: 2.84 us -> 6.88 us
    all_to_all x5 -> x4, blocking collectives: 75.2 us -> 51.1 us  [exchange(): return lax.all_to_all(x, axis, split_axis=0, concat_axis=0, tiled=True)]
    all_to_all x6 -> x7, waiting for transfers between devices: 52.3 us -> 61.8 us  [exchange(): return lax.all_to_all(x, axis, split_axis=0, concat_axis=0, tiled=True)]
    pallas_call x0 -> x1, Pallas kernels: none -> 3.57 us  [three(): pl.pallas_call(three_kernel, name='three', out_shape=jax.ShapeDtypeStruct...]
    pallas_call x1, Pallas kernels: 2.89 us -> 5.89 us  [back(): pl.pallas_call(back_kernel, name='back', out_shape=(jax.ShapeDtypeStruct(...]
    ppermute x2, waiting for transfers between devices: 0.01 us -> 2.54 us  [swap_cores(): return lax.ppermute(x, 'c', [(0, 1), (1, 0)])]
    unnamed x41 -> x43, local copies, waits for them, and re-layouts: 5.47 us -> 2.99 us
    all_to_all x6 -> x7, starting transfers between devices: 48.9 us -> 51.2 us  [exchange(): return lax.all_to_all(x, axis, split_axis=0, concat_axis=0, tiled=True)]
    dot_general x8 -> x7, matrix products: 9.77 us -> 7.99 us  [dot(): lax.dot_general(a, b, (dims, ((), ())), precision=precision, preferred_el...]
  transfers between devices with their start and end apart: 9 -> 10, of which waited for: 6 -> 8; matrix products, arithmetic and copies ran while one was open for 7% -> 8% of each run, Pallas kernels for 1% -> 3%
where the time goes in v6:
time: 238 us; the launch traced here: 237 us
  waiting for transfers between devices  64.3 us (27%)
  starting transfers between devices  57.5 us (24%)
  blocking collectives  51.1 us (21%)
  Pallas kernels  21.6 us (9%)
  between operations  14.6 us (6%)
  local copies, waits for them, and re-layouts  13 us (5%)
  matrix products  7.99 us (3%)
  other arithmetic  6.88 us (3%)
    all_to_all x7, waiting for transfers between devices, exchange(): return lax.all_to_all(x, axis, split_axis=0, concat_axis=0, tiled=True)  61.8 us
    all_to_all x7, starting transfers between devices, exchange(): return lax.all_to_all(x, axis, split_axis=0, concat_axis=0, tiled=True)  51.2 us
    all_to_all x4, blocking collectives, exchange(): return lax.all_to_all(x, axis, split_axis=0, concat_axis=0, tiled=True)  51.1 us
    dot_general x7, matrix products, dot(): lax.dot_general(a, b, (dims, ((), ())), precision=precision, preferred_el...  7.99 us
    ppermute x2, starting transfers between devices, swap_cores(): return lax.ppermute(x, 'c', [(0, 1), (1, 0)])  6.27 us
    pallas_call x1, Pallas kernels, query_matmul(): pl.pallas_call(query_kernel, name='query', out_shape=(jax.ShapeDtypeStruc...  6.09 us
    pallas_call x2, Pallas kernels, partial_matmul(): pl.pallas_call(kernel, name=name, out_shape=(jax.ShapeDtypeStruct((groups...  6.03 us
    pallas_call x1, Pallas kernels, back(): pl.pallas_call(back_kernel, name='back', out_shape=(jax.ShapeDtypeStruct(...  5.89 us
  transfers between devices with their start and end apart: 10, of which 8 were waited for; matrix products, arithmetic and copies ran while one was open for 8% of the time, Pallas kernels for 3%

profile of v6, /device:TPU:1, one launch (start us, length us, event | category | flops | bytes accessed | tf_op | source)
XLA Modules:
  0.0 237.1 jit_solution(16199215659032990768)
XLA Ops:
  8.2 11.1 %all_to_all.55 = bf16[4,80,640]{2,1,0:T(8,128)(2,1)} all-to-all(bf16[4,80,640]{2,1,0:T(8,128)(2,1)S(1)} %broadcast_in_dim.52), channel_id=1, replica_groups=mesh['z'=16,'x'=4,'y'=4,'c'=2] {'x'}, dimensions={0} | all-to-all | bytes 819200 | tf_op jit(solution)/shard_map/all_to_all | solution.py:28
  20.7 17.4 %all-to-all-start.1 = ((bf16[64,4,128]{2,1,0:T(4,128)(2,1)}), bf16[64,4,128]{2,1,0:T(4,128)(2,1)S(1)}, u32[]{:S(2)}, u32[]{:S(2)}) async-start(bf16[64,4,128]{2,1,0:T(4,128)(2,1)} %bitcast.2), calls=%async_computation.1 | async-start | bytes 131072 | tf_op jit(solution)/shard_map/all_to_all | solution.py:28
  38.1 14.1 %all-to-all-done.1 = bf16[64,4,128]{2,1,0:T(4,128)(2,1)S(1)} async-done(((bf16[64,4,128]{2,1,0:T(4,128)(2,1)}), bf16[64,4,128]{2,1,0:T(4,128)(2,1)S(1)}, u32[]{:S(2)}, u32[]{:S(2)}) %all-to-all-start.1) | async-done | bytes 65568 | tf_op jit(solution)/shard_map/all_to_all | solution.py:28
  53.2 8.2 %all-to-all-start.2 = ((bf16[8,256,128]{1,2,0:T(8,128)(2,1)}), bf16[8,256,128]{1,2,0:T(8,128)(2,1)S(1)}, u32[]{:S(2)}, u32[]{:S(2)}) async-start(bf16[8,256,128]{1,2,0:T(8,128)(2,1)} %broadcast_in_dim.57), calls=%async_computation.2 | async-start | bytes 1048576 | tf_op jit(solution)/shard_map/all_to_all | solution.py:28
  62.9 8.0 %all-to-all-done.2 = bf16[8,256,128]{1,2,0:T(8,128)(2,1)S(1)} async-done(((bf16[8,256,128]{1,2,0:T(8,128)(2,1)}), bf16[8,256,128]{1,2,0:T(8,128)(2,1)S(1)}, u32[]{:S(2)}, u32[]{:S(2)}) %all-to-all-start.2) | async-done | bytes 524320 | tf_op jit(solution)/shard_map/all_to_all | solution.py:28
  71.8 1.6 add_multiply_fusion
  73.6 1.7 add_multiply_fusion.1
  77.3 4.1 %all-to-all-start.3 = ((f32[8,2,256]{2,1,0:T(2,128)}), f32[8,2,256]{2,1,0:T(2,128)S(1)}, u32[]{:S(2)}, u32[]{:S(2)}) async-start(f32[8,2,256]{2,1,0:T(2,128)} %broadcast_in_dim.60), calls=%async_computation.3 | async-start | bytes 32768 | tf_op jit(solution)/shard_map/all_to_all | solution.py:28
  81.4 4.7 %all-to-all-done.3 = f32[8,2,256]{2,1,0:T(2,128)S(1)} async-done(((f32[8,2,256]{2,1,0:T(2,128)}), f32[8,2,256]{2,1,0:T(2,128)S(1)}, u32[]{:S(2)}, u32[]{:S(2)}) %all-to-all-start.3) | async-done | bytes 16416 | tf_op jit(solution)/shard_map/all_to_all | solution.py:28
  87.3 1.2 broadcast_in_dim.61
  88.5 3.6 %all-to-all-start.4 = ((bf16[4,272,640]{2,1,0:T(8,128)(2,1)}), bf16[4,272,640]{2,1,0:T(8,128)(2,1)S(1)}, u32[]{:S(2)}, u32[]{:S(2)}) async-start(bf16[4,272,640]{2,1,0:T(8,128)(2,1)} %broadcast_in_dim.61), calls=%async_computation.4 | async-start | bytes 2785280 | tf_op jit(solution)/shard_map/all_to_all | solution.py:28
  93.6 1.6 copy.36
  97.1 1.5 convolution_convert_fusion.1.two_t_hbm
  98.5 11.8 %all-to-all-done.4.own_ref = bf16[4,272,640]{2,1,0:T(8,128)(2,1)S(1)} async-done(((bf16[4,272,640]{2,1,0:T(8,128)(2,1)}), bf16[4,272,640]{2,1,0:T(8,128)(2,1)S(1)}, u32[]{:S(2)}, u32[]{:S(2)}) %all-to-all-start.4) | async-done | bytes 1392672 | tf_op jit(solution)/shard_map/all_to_all | solution.py:28
  110.3 3.6 %collective-permute-start = (bf16[4,272,640]{2,1,0:T(8,128)(2,1)S(1)}, bf16[4,272,640]{2,1,0:T(8,128)(2,1)S(1)}, u32[]{:S(2)}, u32[]{:S(2)}) collective-permute-start(bf16[4,272,640]{2,1,0:T(8,128)(2,1)S(1)} %all-to-all-done.4.own_ref), channel_id=1, source_target_pairs={{0,1},{1,0},{2,3},{3,2},{4,5},{5,4},{6,7},{7,6},{8,9},{9,8},{10,11... | collective-permute-start | bytes 4177928 | tf_op jit(solution)/shard_map/ppermute | solution.py:338
  113.9 2.5 %collective-permute-done.other_ref = bf16[4,272,640]{2,1,0:T(8,128)(2,1)S(1)} collective-permute-done((bf16[4,272,640]{2,1,0:T(8,128)(2,1)S(1)}, bf16[4,272,640]{2,1,0:T(8,128)(2,1)S(1)}, u32[]{:S(2)}, u32[]{:S(2)}) %collective-permute-start) | collective-permute-done | bytes 1392672 | tf_op jit(solution)/shard_map/ppermute | solution.py:338
  117.6 6.1 %query.1 = (f32[256,640]{1,0:T(8,128)S(1)}, f32[8,8,256]{2,1,0:T(8,128)S(1)}) custom-call(f32[1,640]{1,0:T(1,128)S(1)} %broadcast_in_dim.50.bias_ref, f32[1,640]{1,0:T(1,128)S(1)} %broadcast_in_dim.51.gain_ref, bf16[256,640]{1,0:T(8,128)(2,1)S(1)} %copy-done.2, bf16[4,272,640]{2,1,0:T(8,128)(2,1)} %copy-done.4, bf16[4,272,640]{2,1,0:T(8,128)(2,1)} %copy-done.6, ...), custom_call_target="tpu_custom_call" | custom-call | tf_op jit(solution)/shard_map/query/pallas_call | solution.py:101
  123.7 7.6 %all_to_all.56.sums_ref = f32[8,8,256]{2,1,0:T(8,128)S(1)} all-to-all(f32[8,8,256]{2,1,0:T(8,128)S(1)} %get-tuple-element.31), channel_id=1, replica_groups=mesh['z'=16,'x'=4,'y'=4,'c'=2] {'y','c'}, dimensions={0} | all-to-all | bytes 131072 | tf_op jit(solution)/shard_map/all_to_all | solution.py:28
  131.3 2.8 %theirs.1 = (bf16[4,256,640]{2,1,0:T(8,128)(2,1)S(1)}, bf16[256,640]{1,0:T(8,128)(2,1)S(1)}) custom-call(f32[8,8,256]{2,1,0:T(8,128)S(1)} %all_to_all.56.sums_ref, f32[256,640]{1,0:T(8,128)S(1)} %get-tuple-element.32.query_ref, f32[1,640]{1,0:T(1,128)S(1)} %broadcast_in_dim.51.gain_ref, bf16[256,640]{1,0:T(8,128)(2,1)S(1)} %copy-done.2, ...), custom_call_target="tpu_custom_call" | custom-call | flops 838860800 | bytes 3276800 | tf_op jit(solution)/shard_map/theirs/pallas_call | solution.py:160
  134.0 2.7 %collective-permute-start.1 = (bf16[4,256,640]{2,1,0:T(8,128)(2,1)S(1)}, bf16[4,256,640]{2,1,0:T(8,128)(2,1)S(1)}, u32[]{:S(2)}, u32[]{:S(2)}) collective-permute-start(bf16[4,256,640]{2,1,0:T(8,128)(2,1)S(1)} %get-tuple-element.38), channel_id=1, source_target_pairs={{0,1},{1,0},{2,3},{3,2},{4,5},{5,4},{6,7},{7,6},{8,9},{9,8},{10,11... | collective-permute-start | bytes 3932168 | tf_op jit(solution)/shard_map/ppermute | solution.py:338
  136.7 3.3 %mine.1 = (bf16[4,256,640]{2,1,0:T(8,128)(2,1)S(1)}, bf16[256,640]{1,0:T(8,128)(2,1)}) custom-call(f32[8,8,256]{2,1,0:T(8,128)S(1)} %all_to_all.56.sums_ref, f32[256,640]{1,0:T(8,128)S(1)} %get-tuple-element.32.query_ref, f32[1,640]{1,0:T(1,128)S(1)} %broadcast_in_dim.51.gain_ref, bf16[256,640]{1,0:T(8,128)(2,1)S(1)} %get-tuple-element.33.grad_ref, ...), custom_call_target="tpu_custom_call" | custom-call | flops 838860800 | bytes 3276800 | tf_op jit(solution)/shard_map/mine/pallas_call | solution.py:160
  140.0 1.4 add_convert_fusion
  141.4 3.5 %all-to-all-start.6 = ((bf16[4,256,640]{2,1,0:T(8,128)(2,1)}), bf16[4,256,640]{2,1,0:T(8,128)(2,1)S(1)}, u32[]{:S(2)}, u32[]{:S(2)}) async-start(bf16[4,256,640]{2,1,0:T(8,128)(2,1)} %add_convert_fusion), calls=%async_computation.6 | async-start | bytes 2621440 | tf_op jit(solution)/shard_map/all_to_all | solution.py:28
  145.6 17.5 %all-to-all-done.6.pair_hbm = bf16[4,256,640]{2,1,0:T(8,128)(2,1)S(1)} async-done(((bf16[4,256,640]{2,1,0:T(8,128)(2,1)}), bf16[4,256,640]{2,1,0:T(8,128)(2,1)S(1)}, u32[]{:S(2)}, u32[]{:S(2)}) %all-to-all-start.6) | async-done | bytes 1310752 | tf_op jit(solution)/shard_map/all_to_all | solution.py:28
  164.1 5.9 %back.1 = (bf16[512,640]{1,0:T(8,128)(2,1)}, f32[8,24,128]{2,1,0:T(8,128)}) custom-call(f32[8,8,256]{2,1,0:T(8,128)} %copy-done.3, f32[1,256]{1,0:T(1,128)} %bitcast.63, f32[1,640]{1,0:T(1,128)} %broadcast_in_dim.62.scale_ref, bf16[128,128]{1,0:T(8,128)(2,1)} %bitcast.61, bf16[4,256,640]{2,1,0:T(8,128)(2,1)} %copy-done.5, ...), custom_call_target="tpu_custom_call" | custom-call | tf_op jit(solution)/shard_map/back/pallas_call | solution.py:291
  170.0 4.1 %all-to-all-start.7 = ((f32[8,24,128]{2,1,0:T(8,128)}), f32[8,24,128]{2,1,0:T(8,128)S(1)}, u32[]{:S(2)}, u32[]{:S(2)}) async-start(f32[8,24,128]{2,1,0:T(8,128)} %get-tuple-element.47), calls=%async_computation.7 | async-start | bytes 196608 | tf_op jit(solution)/shard_map/all_to_all | solution.py:28
  174.1 3.6 %three.1 = bf16[512,640]{1,0:T(8,128)(2,1)} custom-call(bf16[512,640]{1,0:T(8,128)(2,1)} %get-tuple-element.45.slot_ref, bf16[512,512]{1,0:T(8,128)(2,1)} %convolution_convert_fusion.1.two_t_hbm), custom_call_target="tpu_custom_call" | custom-call | flops 335544320 | bytes 524288 | tf_op jit(solution)/shard_map/three/pallas_call | solution.py:318
  177.6 1.4 all-to-all-done.7
  180.3 12.6 %all_to_all.57 = bf16[4,136,640]{2,1,0:T(8,128)(2,1)S(1)} all-to-all(bf16[4,136,640]{2,1,0:T(8,128)(2,1)S(1)} %pad_maximum_fusion), channel_id=1, replica_groups=mesh['z'=16,'x'=4,'y'=4,'c'=2] {'x'}, dimensions={0} | all-to-all | bytes 1392640 | tf_op jit(solution)/shard_map/all_to_all | solution.py:28
  193.1 19.8 %all_to_all.58 = bf16[16,8,1024]{2,1,0:T(8,128)(2,1)S(1)} all-to-all(bf16[16,8,1024]{2,1,0:T(8,128)(2,1)S(1)} %pad_maximum_fusion.3), channel_id=1, replica_groups=mesh['z'=16,'x'=4,'y'=4,'c'=2] {'z'}, dimensions={0} | all-to-all | bytes 524288 | tf_op jit(solution)/shard_map/all_to_all | solution.py:28
  213.6 10.4 %all-to-all-start.10 = ((f32[8,24,128]{2,1,0:T(8,128)}), f32[8,24,128]{2,1,0:T(8,128)S(1)}, u32[]{:S(2)}, u32[]{:S(2)}) async-start(f32[8,24,128]{2,1,0:T(8,128)} %broadcast_in_dim.65), calls=%async_computation.10 | async-start | bytes 196608 | tf_op jit(solution)/shard_map/all_to_all | solution.py:28
  224.6 4.4 %all-to-all-done.10 = f32[8,24,128]{2,1,0:T(8,128)S(1)} async-done(((f32[8,24,128]{2,1,0:T(8,128)}), f32[8,24,128]{2,1,0:T(8,128)S(1)}, u32[]{:S(2)}, u32[]{:S(2)}) %all-to-all-start.10) | async-done | bytes 98336 | tf_op jit(solution)/shard_map/all_to_all | solution.py:28
  (109 shorter events, 18.9 us)
Async XLA Ops:
  7.2 12.5 %copy-start = (bf16[256,256]{1,0:T(8,128)(2,1)S(1)}, bf16[256,256]{1,0:T(8,128)(2,1)}, u32[]{:S(2)}) copy-start(bf16[256,256]{1,0:T(8,128)(2,1)} %param.14) | copy-start | bytes 393220
  7.2 12.2 %copy-start.16 = (s32[256,1]{0,1:T(1,128)S(1)}, s32[256,1]{0,1:T(1,128)}, u32[]{:S(2)}) copy-start(s32[256,1]{0,1:T(1,128)} %param.15) | copy-start | bytes 3076
  7.2 12.4 %copy-start.18 = (s32[256]{0:T(256)S(1)}, s32[256]{0:T(256)}, u32[]{:S(2)}) copy-start(s32[256]{0:T(256)} %param.16) | copy-start | bytes 3076
  7.2 12.2 %copy-start.10 = (f32[640]{0:T(1024)S(1)}, f32[640]{0:T(1024)}, u32[]{:S(2)}) copy-start(f32[640]{0:T(1024)} %param.20) | copy-start | bytes 7684
  7.2 30.9 %copy-start.11 = (f32[640]{0:T(1024)S(1)}, f32[640]{0:T(1024)}, u32[]{:S(2)}) copy-start(f32[640]{0:T(1024)} %param.21) | copy-start | bytes 7684
  7.2 109.2 %all-gather.2.cloned.1.call-start = ((), (), s32[]{:S(2)}) async-start(), calls=%async_computation.11 | async-start | bytes 6963200 | tf_op jit(solution)/shard_map/all_gather | solution.py:367
  19.3 42.1 %copy-start.13 = (bf16[16,32]{1,0:T(8,128)(2,1)S(1)}, bf16[16,32]{1,0:T(8,128)(2,1)}, u32[]{:S(2)}) copy-start(bf16[16,32]{1,0:T(8,128)(2,1)} %param.17) | copy-start | bytes 3076
  20.7 31.5 %all-to-all-start.1 = ((bf16[64,4,128]{2,1,0:T(4,128)(2,1)}), bf16[64,4,128]{2,1,0:T(4,128)(2,1)S(1)}, u32[]{:S(2)}, u32[]{:S(2)}) async-start(bf16[64,4,128]{2,1,0:T(4,128)(2,1)} %bitcast.2), calls=%async_computation.1 | async-start | bytes 131072 | tf_op jit(solution)/shard_map/all_to_all | solution.py:28
  53.2 17.7 %all-to-all-start.2 = ((bf16[8,256,128]{1,2,0:T(8,128)(2,1)}), bf16[8,256,128]{1,2,0:T(8,128)(2,1)S(1)}, u32[]{:S(2)}, u32[]{:S(2)}) async-start(bf16[8,256,128]{1,2,0:T(8,128)(2,1)} %broadcast_in_dim.57), calls=%async_computation.2 | async-start | bytes 1048576 | tf_op jit(solution)/shard_map/all_to_all | solution.py:28
  71.8 1.7 copy-start.9
  73.4 1.9 copy-start.7
  73.6 1.8 copy-start.8
  73.6 1.8 copy-start.17
  75.4 1.1 copy-start.19
  77.3 8.9 %all-to-all-start.3 = ((f32[8,2,256]{2,1,0:T(2,128)}), f32[8,2,256]{2,1,0:T(2,128)S(1)}, u32[]{:S(2)}, u32[]{:S(2)}) async-start(f32[8,2,256]{2,1,0:T(2,128)} %broadcast_in_dim.60), calls=%async_computation.3 | async-start | bytes 32768 | tf_op jit(solution)/shard_map/all_to_all | solution.py:28
  86.2 2.3 copy-start.12
  88.5 21.8 %all-to-all-start.4 = ((bf16[4,272,640]{2,1,0:T(8,128)(2,1)}), bf16[4,272,640]{2,1,0:T(8,128)(2,1)S(1)}, u32[]{:S(2)}, u32[]{:S(2)}) async-start(bf16[4,272,640]{2,1,0:T(8,128)(2,1)} %broadcast_in_dim.61), calls=%async_computation.4 | async-start | bytes 2785280 | tf_op jit(solution)/shard_map/all_to_all | solution.py:28
  95.2 1.8 copy-start.20
  97.1 16.8 %copy-start.14 = (f32[640]{0:T(1024)S(1)}, f32[640]{0:T(1024)}, u32[]{:S(2)}) copy-start(f32[640]{0:T(1024)} %param.24) | copy-start | bytes 7684
  97.1 16.8 %copy-start.15 = (f32[640]{0:T(1024)S(1)}, f32[640]{0:T(1024)}, u32[]{:S(2)}) copy-start(f32[640]{0:T(1024)} %param.23) | copy-start | bytes 7684
  97.1 20.5 %copy-start.2 = (bf16[256,640]{1,0:T(8,128)(2,1)S(1)}, bf16[256,640]{1,0:T(8,128)(2,1)}, u32[]{:S(2)}) copy-start(bf16[256,640]{1,0:T(8,128)(2,1)} %cot_ref.3) | copy-start | bytes 983044
  110.3 6.2 %copy-start.4 = (bf16[4,272,640]{2,1,0:T(8,128)(2,1)}, bf16[4,272,640]{2,1,0:T(8,128)(2,1)S(1)}, u32[]{:S(2)}) copy-start(bf16[4,272,640]{2,1,0:T(8,128)(2,1)S(1)} %all-to-all-done.4.own_ref) | copy-start | bytes 4177924
  110.3 6.2 %collective-permute-start = (bf16[4,272,640]{2,1,0:T(8,128)(2,1)S(1)}, bf16[4,272,640]{2,1,0:T(8,128)(2,1)S(1)}, u32[]{:S(2)}, u32[]{:S(2)}) collective-permute-start(bf16[4,272,640]{2,1,0:T(8,128)(2,1)S(1)} %all-to-all-done.4.own_ref), channel_id=1, source_target_pairs={{0,1},{1,0},{2,3},{3,2},{4,5},{5,4},{6,7},{7,6},{8,9},{9,8},{10,11... | collective-permute-start | bytes 4177928 | tf_op jit(solution)/shard_map/ppermute | solution.py:338
  116.5 1.1 copy-start.6
  117.6 13.7 %copy-start.1 = (bf16[5120,640]{1,0:T(8,128)(2,1)S(1)}, bf16[5120,640]{1,0:T(8,128)(2,1)}, u32[]{:S(2)}) copy-start(bf16[5120,640]{1,0:T(8,128)(2,1)} %all-gather.2.cloned.1.call-done) | copy-start | bytes 19660804
  131.3 5.5 %copy-start.3 = (f32[8,8,256]{2,1,0:T(8,128)}, f32[8,8,256]{2,1,0:T(8,128)S(1)}, u32[]{:S(2)}) copy-start(f32[8,8,256]{2,1,0:T(8,128)S(1)} %all_to_all.56.sums_ref) | copy-start | bytes 196612
  134.0 6.0 %collective-permute-start.1 = (bf16[4,256,640]{2,1,0:T(8,128)(2,1)S(1)}, bf16[4,256,640]{2,1,0:T(8,128)(2,1)S(1)}, u32[]{:S(2)}, u32[]{:S(2)}) collective-permute-start(bf16[4,256,640]{2,1,0:T(8,128)(2,1)S(1)} %get-tuple-element.38), channel_id=1, source_target_pairs={{0,1},{1,0},{2,3},{3,2},{4,5},{5,4},{6,7},{7,6},{8,9},{9,8},{10,11... | collective-permute-start | bytes 3932168 | tf_op jit(solution)/shard_map/ppermute | solution.py:338
  141.4 21.6 %all-to-all-start.6 = ((bf16[4,256,640]{2,1,0:T(8,128)(2,1)}), bf16[4,256,640]{2,1,0:T(8,128)(2,1)S(1)}, u32[]{:S(2)}, u32[]{:S(2)}) async-start(bf16[4,256,640]{2,1,0:T(8,128)(2,1)} %add_convert_fusion), calls=%async_computation.6 | async-start | bytes 2621440 | tf_op jit(solution)/shard_map/all_to_all | solution.py:28
  163.0 1.1 copy-start.5
  170.0 9.1 %all-to-all-start.7 = ((f32[8,24,128]{2,1,0:T(8,128)}), f32[8,24,128]{2,1,0:T(8,128)S(1)}, u32[]{:S(2)}, u32[]{:S(2)}) async-start(f32[8,24,128]{2,1,0:T(8,128)} %get-tuple-element.47), calls=%async_computation.7 | async-start | bytes 196608 | tf_op jit(solution)/shard_map/all_to_all | solution.py:28
  213.6 15.3 %all-to-all-start.10 = ((f32[8,24,128]{2,1,0:T(8,128)}), f32[8,24,128]{2,1,0:T(8,128)S(1)}, u32[]{:S(2)}, u32[]{:S(2)}) async-start(f32[8,24,128]{2,1,0:T(8,128)} %broadcast_in_dim.65), calls=%async_computation.10 | async-start | bytes 196608 | tf_op jit(solution)/shard_map/all_to_all | solution.py:28
Sparse Core Ops, SparseCore 0:
  19.4 93.2 all-gather.1

commit v7 on v6

--- a/solution.py
+++ b/solution.py
@@ -32,13 +32,15 @@
     return exchange(jnp.broadcast_to(x[None], (count,) + x.shape), axis)
 
 
-VMEM_LIMIT = 32 * 1024 * 1024
-BACK_VMEM_LIMIT = 56 * 1024 * 1024
-QUERY_VMEM_LIMIT = 52 * 1024 * 1024
+VMEM_LIMIT = 24 * 1024 * 1024
 
 
 def in_vmem(count):
     return [pl.BlockSpec(memory_space=pltpu.VMEM)] * count
+
+
+def in_hbm(*arrays):
+    return tuple(pltpu.with_memory_space_constraint(x, pltpu.HBM) for x in arrays)
 
 
 def across(column, width):
@@ -47,9 +49,26 @@
 
 
 def query_kernel(
-    bias_ref, gain_ref, cot_ref, own_ref, other_ref, w_ref, out_ref, sums_ref, left, held, sems
+    cot_ref,
+    bias_hbm,
+    gain_hbm,
+    own_ref,
+    other_ref,
+    w_ref,
+    out_ref,
+    sums_ref,
+    bias_ref,
+    gain_ref,
+    left,
+    held,
+    row_sems,
+    sems,
 ):
     core = lax.axis_index("c")
+    row_fetches = (
+        pltpu.make_async_copy(bias_hbm, bias_ref, row_sems.at[0]),
+        pltpu.make_async_copy(gain_hbm, gain_ref, row_sems.at[1]),
+    )
     groups, _, width = own_ref.shape
     tokens, cols = out_ref.shape
     fetches = []
@@ -64,7 +83,7 @@
                     w_ref.at[which], held.at[pl.ds(place * width, width)], sems.at[1, place]
                 )
             )
-    for fetch in fetches:
+    for fetch in (*fetches, *row_fetches):
         fetch.start()
     total = None
     for i in range(groups):
@@ -75,6 +94,8 @@
             both, held[2 * i * width : 2 * (i + 1) * width], preferred_element_type=f32
         )
         total = term if total is None else total + term
+    for fetch in row_fetches:
+        fetch.wait()
     query = total[:tokens] + bias_ref[...]
     out_ref[...] = query
     scale_w = total[tokens : tokens + 1] + total[tokens + 1 : tokens + 2]
@@ -105,15 +126,18 @@
             jax.ShapeDtypeStruct((tokens, cols), f32),
             jax.ShapeDtypeStruct((N_TP, 8, tokens), f32),
         ),
-        in_specs=in_vmem(3) + [pl.BlockSpec(memory_space=pl.ANY)] * 3,
+        in_specs=in_vmem(1) + [pl.BlockSpec(memory_space=pl.ANY)] * 5,
         out_specs=tuple(in_vmem(2)),
         scratch_shapes=[
+            pltpu.VMEM((1, cols), f32),
+            pltpu.VMEM((1, cols), f32),
             pltpu.VMEM((2 * own.shape[0],) + own.shape[1:], bf16),
             pltpu.VMEM((weights.shape[0] * weights.shape[1], cols), bf16),
+            pltpu.SemaphoreType.DMA((2,)),
             pltpu.SemaphoreType.DMA((2, weights.shape[0])),
         ],
-        compiler_params=pltpu.CompilerParams(vmem_limit_bytes=QUERY_VMEM_LIMIT),
-    )(bias[None], gain[None], cotangent, own, other, weights)
+        compiler_params=pltpu.CompilerParams(vmem_limit_bytes=VMEM_LIMIT),
+    )(cotangent, *in_hbm(bias[None], gain[None], own, other, weights))
 
 
 def fetch_blocks(w_ref, held, sems, core):
@@ -189,46 +213,24 @@
     inverse_ref,
     scale_ref,
     w_two_t_ref,
-    pair_hbm,
-    normed_hbm,
-    select_hbm,
-    w_three_hbm,
-    slope_two_hbm,
-    one_t_hbm,
-    slope_one_hbm,
-    pose_t_hbm,
-    slot_ref,
-    small_ref,
     pair_ref,
     normed_ref,
     select_ref,
+    one_t_ref,
+    pose_t_ref,
+    w_three_hbm,
+    slope_two_hbm,
+    slope_one_hbm,
+    slot_hbm,
+    small_ref,
     w_three_ref,
     slope_two_ref,
-    one_t_ref,
     slope_one_ref,
-    pose_t_ref,
+    slot_ref,
     sems,
 ):
-    far = (
-        pair_hbm,
-        normed_hbm,
-        select_hbm,
-        w_three_hbm,
-        slope_two_hbm,
-        one_t_hbm,
-        slope_one_hbm,
-        pose_t_hbm,
-    )
-    near = (
-        pair_ref,
-        normed_ref,
-        select_ref,
-        w_three_ref,
-        slope_two_ref,
-        one_t_ref,
-        slope_one_ref,
-        pose_t_ref,
-    )
+    far = (w_three_hbm, slope_two_hbm, slope_one_hbm)
+    near = (w_three_ref, slope_two_ref, slope_one_ref)
     fetches = [
         pltpu.make_async_copy(source, target, sems.at[k])
         for k, (source, target) in enumerate(zip(far, near, strict=True))
@@ -243,8 +245,6 @@
     pull = sums[1] / full * rinv * rinv * rinv
     grad_mean = (sums[3] * rinv - sums[2] * pull) / full
     grad_cross = ((sums[1] - sums[5]) * rinv - (sums[0] - sums[4]) * pull) / full
-    for fetch in fetches[:3]:
-        fetch.wait()
     total = sum(pair_ref[k].astype(f32) for k in range(pair_ref.shape[0]))
     normed_grad = total * (1.0 + scale_ref[...])
     latent_grad = across(inverse_ref[...], width) * (
@@ -252,7 +252,9 @@
     )
     slot_grad = dot(select_ref[...], latent_grad.astype(bf16), ((1,), (0,))).astype(bf16)
     slot_ref[...] = slot_grad
-    for fetch in fetches[3:]:
+    store = pltpu.make_async_copy(slot_ref, slot_hbm, sems.at[len(fetches)])
+    store.start()
+    for fetch in fetches:
         fetch.wait()
     two_grad = dot(slot_grad, w_three_ref[...], ((1,), (1,))) * slope_two_ref[...]
     part = w_two_t_ref.shape[0]
@@ -283,30 +285,39 @@
         small_ref[k, rows_two:] = jnp.concatenate(
             [grad_one[k * rows_one : (k + 1) * rows_one], jnp.zeros((8 - rows_one, part), f32)]
         )
+    store.wait()
 
 
 def back(near, far):
-    normed, select = far[1:3]
+    normed, select = near[5:7]
     part = near[3].shape[0]
     return pl.pallas_call(
         back_kernel,
         name="back",
         out_shape=(
-            jax.ShapeDtypeStruct((select.shape[0], normed.shape[1]), bf16),
+            pltpu.HBM((select.shape[0], normed.shape[1]), bf16),
             jax.ShapeDtypeStruct((N_TP, part // N_TP + 8, part), f32),
         ),
         in_specs=in_vmem(len(near)) + [pl.BlockSpec(memory_space=pl.ANY)] * len(far),
-        out_specs=tuple(in_vmem(2)),
+        out_specs=(pl.BlockSpec(memory_space=pltpu.HBM), *in_vmem(1)),
         scratch_shapes=[pltpu.VMEM(x.shape, x.dtype) for x in far]
-        + [pltpu.SemaphoreType.DMA((len(far),))],
-        compiler_params=pltpu.CompilerParams(vmem_limit_bytes=BACK_VMEM_LIMIT),
-    )(*near, *far)
-
-
-def three_kernel(slot_ref, two_t_hbm, out_ref, two_t_ref, sem):
-    fetch = pltpu.make_async_copy(two_t_hbm, two_t_ref, sem)
-    fetch.start()
-    fetch.wait()
+        + [
+            pltpu.VMEM((select.shape[0], normed.shape[1]), bf16),
+            pltpu.SemaphoreType.DMA((len(far) + 1,)),
+        ],
+        compiler_params=pltpu.CompilerParams(vmem_limit_bytes=VMEM_LIMIT),
+    )(*near, *in_hbm(*far))
+
+
+def three_kernel(slot_hbm, two_t_hbm, out_ref, slot_ref, two_t_ref, sems):
+    fetches = (
+        pltpu.make_async_copy(slot_hbm, slot_ref, sems.at[0]),
+        pltpu.make_async_copy(two_t_hbm, two_t_ref, sems.at[1]),
+    )
+    for fetch in fetches:
+        fetch.start()
+    for fetch in fetches:
+        fetch.wait()
     out_ref[...] = jnp.dot(
         two_t_ref[...], slot_ref[...], preferred_element_type=f32
     ).astype(out_ref.dtype)
@@ -319,14 +330,18 @@
         three_kernel,
         name="three",
         out_shape=jax.ShapeDtypeStruct((rows, width), bf16),
-        in_specs=in_vmem(1) + [pl.BlockSpec(memory_space=pl.ANY)],
+        in_specs=[pl.BlockSpec(memory_space=pl.ANY)] * 2,
         out_specs=pl.BlockSpec(memory_space=pltpu.VMEM),
-        scratch_shapes=[pltpu.VMEM(two_t.shape, bf16), pltpu.SemaphoreType.DMA],
-        compiler_params=pltpu.CompilerParams(vmem_limit_bytes=BACK_VMEM_LIMIT),
+        scratch_shapes=[
+            pltpu.VMEM(slot_grad.shape, bf16),
+            pltpu.VMEM(two_t.shape, bf16),
+            pltpu.SemaphoreType.DMA((2,)),
+        ],
+        compiler_params=pltpu.CompilerParams(vmem_limit_bytes=VMEM_LIMIT),
         cost_estimate=pl.CostEstimate(
             flops=2 * rows * slots * width, bytes_accessed=2 * rows * slots, transcendentals=0
         ),
-    )(slot_grad, two_t)
+    )(*in_hbm(slot_grad, two_t))
 
 
 def halves(x):
@@ -465,8 +480,8 @@
     pair = (mine.astype(f32) + theirs.astype(f32)).astype(bf16)
     pair = exchange(pair, "y")
     slot_grad, small = back(
-        (sums, inverse, scale_mod[None], w_two_t),
-        (pair, normed, select, w_section3, slope_two, one_t, slope_one, pose_t),
+        (sums, inverse, scale_mod[None], w_two_t, pair, normed, select, one_t, pose_t),
+        (w_section3, slope_two, slope_one),
     )
     grad_three = three(slot_grad, leaving_two)
 

time: 238 us -> 235 us (0.987)
  other arithmetic: 6.88 us -> 2.78 us
  waiting for transfers between devices: 64.3 us -> 67.9 us
  Pallas kernels: 21.6 us -> 19.1 us
    all_to_all x7, waiting for transfers between devices: 61.8 us -> 66.1 us  [exchange(): return lax.all_to_all(x, axis, split_axis=0, concat_axis=0, tiled=True)]
  transfers between devices with their start and end apart: 10 -> 10, of which waited for: 8 -> 8; matrix products, arithmetic and copies ran while one was open for 8% -> 8% of each run, Pallas kernels for 3% -> 2%
where the time goes in v7:
time: 235 us; the launch traced here: 234 us
  waiting for transfers between devices  67.9 us (29%)
  starting transfers between devices  58.2 us (25%)
  blocking collectives  50.4 us (21%)
  Pallas kernels  19.1 us (8%)
  between operations  14.6 us (6%)
  local copies, waits for them, and re-layouts  11.7 us (5%)
  matrix products  9.46 us (4%)
  other arithmetic  2.78 us (1%)
    all_to_all x7, waiting for transfers between devices, exchange(): return lax.all_to_all(x, axis, split_axis=0, concat_axis=0, tiled=True)  66.1 us
    all_to_all x7, starting transfers between devices, exchange(): return lax.all_to_all(x, axis, split_axis=0, concat_axis=0, tiled=True)  51.8 us
    all_to_all x4, blocking collectives, exchange(): return lax.all_to_all(x, axis, split_axis=0, concat_axis=0, tiled=True)  50.4 us
    dot_general x7, matrix products, dot(): lax.dot_general(a, b, (dims, ((), ())), precision=precision, preferred_el...  9.46 us
    pallas_call x1, Pallas kernels, query_matmul(): pl.pallas_call(query_kernel, name='query', out_shape=(jax.ShapeDtypeStruc...  6.28 us
    ppermute x2, starting transfers between devices, swap_cores(): return lax.ppermute(x, 'c', [(0, 1), (1, 0)])  6.27 us
    pallas_call x2, Pallas kernels, partial_matmul(): pl.pallas_call(kernel, name=name, out_shape=(jax.ShapeDtypeStruct((groups...  6.06 us
    pallas_call x1, Pallas kernels, back(): pl.pallas_call(back_kernel, name='back', out_shape=(pltpu.HBM((select.sha...  4.96 us
  transfers between devices with their start and end apart: 10, of which 8 were waited for; matrix products, arithmetic and copies ran while one was open for 8% of the time, Pallas kernels for 2%

profile of v7, /device:TPU:1, one launch (start us, length us, event | category | flops | bytes accessed | tf_op | source)
XLA Modules:
  0.0 234.1 jit_solution(13087636012168064139)
XLA Ops:
  8.2 11.1 %all_to_all.55 = bf16[4,80,640]{2,1,0:T(8,128)(2,1)} all-to-all(bf16[4,80,640]{2,1,0:T(8,128)(2,1)S(1)} %broadcast_in_dim.52), channel_id=1, replica_groups=mesh['z'=16,'x'=4,'y'=4,'c'=2] {'x'}, dimensions={0} | all-to-all | bytes 819200 | tf_op jit(solution)/shard_map/all_to_all | solution.py:28
  20.7 17.4 %all-to-all-start.1 = ((bf16[64,4,128]{2,1,0:T(4,128)(2,1)}), bf16[64,4,128]{2,1,0:T(4,128)(2,1)S(1)}, u32[]{:S(2)}, u32[]{:S(2)}) async-start(bf16[64,4,128]{2,1,0:T(4,128)(2,1)} %bitcast.2), calls=%async_computation.1 | async-start | bytes 131072 | tf_op jit(solution)/shard_map/all_to_all | solution.py:28
  38.1 14.1 %all-to-all-done.1 = bf16[64,4,128]{2,1,0:T(4,128)(2,1)S(1)} async-done(((bf16[64,4,128]{2,1,0:T(4,128)(2,1)}), bf16[64,4,128]{2,1,0:T(4,128)(2,1)S(1)}, u32[]{:S(2)}, u32[]{:S(2)}) %all-to-all-start.1) | async-done | bytes 65568 | tf_op jit(solution)/shard_map/all_to_all | solution.py:28
  53.2 8.2 %all-to-all-start.2 = ((bf16[8,256,128]{1,2,0:T(8,128)(2,1)}), bf16[8,256,128]{1,2,0:T(8,128)(2,1)S(1)}, u32[]{:S(2)}, u32[]{:S(2)}) async-start(bf16[8,256,128]{1,2,0:T(8,128)(2,1)} %broadcast_in_dim.57), calls=%async_computation.2 | async-start | bytes 1048576 | tf_op jit(solution)/shard_map/all_to_all | solution.py:28
  62.9 8.0 %all-to-all-done.2 = bf16[8,256,128]{1,2,0:T(8,128)(2,1)S(1)} async-done(((bf16[8,256,128]{1,2,0:T(8,128)(2,1)}), bf16[8,256,128]{1,2,0:T(8,128)(2,1)S(1)}, u32[]{:S(2)}, u32[]{:S(2)}) %all-to-all-start.2) | async-done | bytes 524320 | tf_op jit(solution)/shard_map/all_to_all | solution.py:28
  71.8 1.6 add_multiply_fusion
  73.6 2.0 add_multiply_fusion.1
  75.6 2.3 fusion.112
  78.7 4.1 %all-to-all-start.3 = ((f32[8,2,256]{2,1,0:T(2,128)}), f32[8,2,256]{2,1,0:T(2,128)S(1)}, u32[]{:S(2)}, u32[]{:S(2)}) async-start(f32[8,2,256]{2,1,0:T(2,128)} %broadcast_in_dim.60), calls=%async_computation.3 | async-start | bytes 32768 | tf_op jit(solution)/shard_map/all_to_all | solution.py:28
  82.9 4.7 %all-to-all-done.3 = f32[8,2,256]{2,1,0:T(2,128)S(1)} async-done(((f32[8,2,256]{2,1,0:T(2,128)}), f32[8,2,256]{2,1,0:T(2,128)S(1)}, u32[]{:S(2)}, u32[]{:S(2)}) %all-to-all-start.3) | async-done | bytes 16416 | tf_op jit(solution)/shard_map/all_to_all | solution.py:28
  89.2 4.3 %all-to-all-start.4 = ((bf16[4,272,640]{2,1,0:T(8,128)(2,1)}), bf16[4,272,640]{2,1,0:T(8,128)(2,1)}, u32[]{:S(2)}, u32[]{:S(2)}) async-start(bf16[4,272,640]{2,1,0:T(8,128)(2,1)} %broadcast_in_dim.61), calls=%async_computation.4 | async-start | bytes 2785280 | tf_op jit(solution)/shard_map/all_to_all | solution.py:28
  93.8 1.6 copy.36
  96.6 1.5 convolution_convert_fusion.1.two_t_hbm
  98.1 13.7 %all-to-all-done.4.own_ref = bf16[4,272,640]{2,1,0:T(8,128)(2,1)} async-done(((bf16[4,272,640]{2,1,0:T(8,128)(2,1)}), bf16[4,272,640]{2,1,0:T(8,128)(2,1)}, u32[]{:S(2)}, u32[]{:S(2)}) %all-to-all-start.4) | async-done | bytes 1392672 | tf_op jit(solution)/shard_map/all_to_all | solution.py:28
  111.8 3.6 %collective-permute-start = (bf16[4,272,640]{2,1,0:T(8,128)(2,1)}, bf16[4,272,640]{2,1,0:T(8,128)(2,1)}, u32[]{:S(2)}, u32[]{:S(2)}) collective-permute-start(bf16[4,272,640]{2,1,0:T(8,128)(2,1)} %all-to-all-done.4.own_ref), channel_id=1, source_target_pairs={{0,1},{1,0},{2,3},{3,2},{4,5},{5,4},{6,7},{7,6},{8,9},{9,8},{10,11... | collective-permute-start | bytes 4177928 | tf_op jit(solution)/shard_map/ppermute | solution.py:353
  116.6 1.7 collective-permute-done.other_ref
  118.3 6.3 %query.1 = (f32[256,640]{1,0:T(8,128)S(1)}, f32[8,8,256]{2,1,0:T(8,128)S(1)}) custom-call(bf16[256,640]{1,0:T(8,128)(2,1)S(1)} %copy-done.2, f32[1,640]{1,0:T(1,128)} %broadcast_in_dim.50.bias_hbm, f32[1,640]{1,0:T(1,128)} %broadcast_in_dim.51.gain_hbm.gain_ref, bf16[4,272,640]{2,1,0:T(8,128)(2,1)} %all-to-all-done.4.own_ref, ...), custom_call_target="tpu_custom_call" | custom-call | tf_op jit(solution)/shard_map/query/pallas_call | solution.py:122
  124.6 7.6 %all_to_all.56.sums_ref = f32[8,8,256]{2,1,0:T(8,128)S(1)} all-to-all(f32[8,8,256]{2,1,0:T(8,128)S(1)} %get-tuple-element.31), channel_id=1, replica_groups=mesh['z'=16,'x'=4,'y'=4,'c'=2] {'y','c'}, dimensions={0} | all-to-all | bytes 131072 | tf_op jit(solution)/shard_map/all_to_all | solution.py:28
  132.2 2.8 %theirs.1 = (bf16[4,256,640]{2,1,0:T(8,128)(2,1)S(1)}, bf16[256,640]{1,0:T(8,128)(2,1)S(1)}) custom-call(f32[8,8,256]{2,1,0:T(8,128)S(1)} %all_to_all.56.sums_ref, f32[256,640]{1,0:T(8,128)S(1)} %get-tuple-element.32.query_ref, f32[1,640]{1,0:T(1,128)S(1)} %copy-done.3, bf16[256,640]{1,0:T(8,128)(2,1)S(1)} %copy-done.2, bf16[8,640,640]{2,1,0:T(8,128)(2,1)S(1)} %bitcast.53), custom_call_target="tpu_custom_call" | custom-call | flops 838860800 | bytes 3276800 | tf_op jit(solution)/shard_map/theirs/pallas_call | solution.py:184
  135.0 2.7 %collective-permute-start.1 = (bf16[4,256,640]{2,1,0:T(8,128)(2,1)S(1)}, bf16[4,256,640]{2,1,0:T(8,128)(2,1)S(1)}, u32[]{:S(2)}, u32[]{:S(2)}) collective-permute-start(bf16[4,256,640]{2,1,0:T(8,128)(2,1)S(1)} %get-tuple-element.38), channel_id=1, source_target_pairs={{0,1},{1,0},{2,3},{3,2},{4,5},{5,4},{6,7},{7,6},{8,9},{9,8},{10,11... | collective-permute-start | bytes 3932168 | tf_op jit(solution)/shard_map/ppermute | solution.py:353
  137.7 3.3 %mine.1 = (bf16[4,256,640]{2,1,0:T(8,128)(2,1)S(1)}, bf16[256,640]{1,0:T(8,128)(2,1)}) custom-call(f32[8,8,256]{2,1,0:T(8,128)S(1)} %all_to_all.56.sums_ref, f32[256,640]{1,0:T(8,128)S(1)} %get-tuple-element.32.query_ref, f32[1,640]{1,0:T(1,128)S(1)} %copy-done.3, bf16[256,640]{1,0:T(8,128)(2,1)S(1)} %get-tuple-element.33.grad_ref, ...), custom_call_target="tpu_custom_call" | custom-call | flops 838860800 | bytes 3276800 | tf_op jit(solution)/shard_map/mine/pallas_call | solution.py:184
  141.0 1.4 add_convert_fusion
  142.4 3.5 %all-to-all-start.6 = ((bf16[4,256,640]{2,1,0:T(8,128)(2,1)}), bf16[4,256,640]{2,1,0:T(8,128)(2,1)S(1)}, u32[]{:S(2)}, u32[]{:S(2)}) async-start(bf16[4,256,640]{2,1,0:T(8,128)(2,1)} %add_convert_fusion), calls=%async_computation.6 | async-start | bytes 2621440 | tf_op jit(solution)/shard_map/all_to_all | solution.py:28
  146.0 18.0 %all-to-all-done.6.pair_ref = bf16[4,256,640]{2,1,0:T(8,128)(2,1)S(1)} async-done(((bf16[4,256,640]{2,1,0:T(8,128)(2,1)}), bf16[4,256,640]{2,1,0:T(8,128)(2,1)S(1)}, u32[]{:S(2)}, u32[]{:S(2)}) %all-to-all-start.6) | async-done | bytes 1310752 | tf_op jit(solution)/shard_map/all_to_all | solution.py:28
  164.0 5.0 %back.1 = (bf16[512,640]{1,0:T(8,128)(2,1)}, f32[8,24,128]{2,1,0:T(8,128)}) custom-call(f32[8,8,256]{2,1,0:T(8,128)S(1)} %all_to_all.56.sums_ref, f32[1,256]{1,0:T(1,128)S(1)} %bitcast.57, f32[1,640]{1,0:T(1,128)S(1)} %broadcast_in_dim.62.scale_ref, bf16[128,128]{1,0:T(8,128)(2,1)S(1)} %bitcast.56, bf16[4,256,640]{2,1,0:T(8,128)(2,1)S(1)} %all-to-all-done.6.pair_ref, ...), custom_call_target="tpu_custom_call" | custom-call | tf_op jit(solution)/shard_map/back/pallas_call | solution.py:294
  169.0 4.1 %all-to-all-start.7 = ((f32[8,24,128]{2,1,0:T(8,128)}), f32[8,24,128]{2,1,0:T(8,128)S(1)}, u32[]{:S(2)}, u32[]{:S(2)}) async-start(f32[8,24,128]{2,1,0:T(8,128)} %get-tuple-element.47), calls=%async_computation.7 | async-start | bytes 196608 | tf_op jit(solution)/shard_map/all_to_all | solution.py:28
  173.1 1.8 three.1
  174.9 3.2 %all-to-all-done.7 = f32[8,24,128]{2,1,0:T(8,128)S(1)} async-done(((f32[8,24,128]{2,1,0:T(8,128)}), f32[8,24,128]{2,1,0:T(8,128)S(1)}, u32[]{:S(2)}, u32[]{:S(2)}) %all-to-all-start.7) | async-done | bytes 98336 | tf_op jit(solution)/shard_map/all_to_all | solution.py:28
  178.2 12.6 %all_to_all.57 = bf16[4,136,640]{2,1,0:T(8,128)(2,1)S(1)} all-to-all(bf16[4,136,640]{2,1,0:T(8,128)(2,1)S(1)} %pad_maximum_fusion), channel_id=1, replica_groups=mesh['z'=16,'x'=4,'y'=4,'c'=2] {'x'}, dimensions={0} | all-to-all | bytes 1392640 | tf_op jit(solution)/shard_map/all_to_all | solution.py:28
  191.0 19.0 %all_to_all.58 = bf16[16,8,1024]{2,1,0:T(8,128)(2,1)S(1)} all-to-all(bf16[16,8,1024]{2,1,0:T(8,128)(2,1)S(1)} %pad_maximum_fusion.3), channel_id=1, replica_groups=mesh['z'=16,'x'=4,'y'=4,'c'=2] {'z'}, dimensions={0} | all-to-all | bytes 524288 | tf_op jit(solution)/shard_map/all_to_all | solution.py:28
  210.8 10.2 %all-to-all-start.10 = ((f32[8,24,128]{2,1,0:T(8,128)}), f32[8,24,128]{2,1,0:T(8,128)S(1)}, u32[]{:S(2)}, u32[]{:S(2)}) async-start(f32[8,24,128]{2,1,0:T(8,128)} %broadcast_in_dim.65), calls=%async_computation.10 | async-start | bytes 196608 | tf_op jit(solution)/shard_map/all_to_all | solution.py:28
  221.6 4.4 %all-to-all-done.10 = f32[8,24,128]{2,1,0:T(8,128)S(1)} async-done(((f32[8,24,128]{2,1,0:T(8,128)}), f32[8,24,128]{2,1,0:T(8,128)S(1)}, u32[]{:S(2)}, u32[]{:S(2)}) %all-to-all-start.10) | async-done | bytes 98336 | tf_op jit(solution)/shard_map/all_to_all | solution.py:28
  (99 shorter events, 13.7 us)
Async XLA Ops:
  7.2 12.5 %copy-start = (bf16[256,256]{1,0:T(8,128)(2,1)S(1)}, bf16[256,256]{1,0:T(8,128)(2,1)}, u32[]{:S(2)}) copy-start(bf16[256,256]{1,0:T(8,128)(2,1)} %param.14) | copy-start | bytes 393220
  7.2 12.2 %copy-start.12 = (s32[256,1]{0,1:T(1,128)S(1)}, s32[256,1]{0,1:T(1,128)}, u32[]{:S(2)}) copy-start(s32[256,1]{0,1:T(1,128)} %param.15) | copy-start | bytes 3076
  7.2 12.4 %copy-start.14 = (s32[256]{0:T(256)S(1)}, s32[256]{0:T(256)}, u32[]{:S(2)}) copy-start(s32[256]{0:T(256)} %param.16) | copy-start | bytes 3076
  7.2 12.2 %copy-start.7 = (f32[640]{0:T(1024)S(1)}, f32[640]{0:T(1024)}, u32[]{:S(2)}) copy-start(f32[640]{0:T(1024)} %param.20) | copy-start | bytes 7684
  7.2 30.9 %copy-start.8 = (f32[640]{0:T(1024)S(1)}, f32[640]{0:T(1024)}, u32[]{:S(2)}) copy-start(f32[640]{0:T(1024)} %param.21) | copy-start | bytes 7684
  7.2 111.1 %all-gather.2.cloned.1.call-start = ((), (), s32[]{:S(2)}) async-start(), calls=%async_computation.11 | async-start | bytes 6963200 | tf_op jit(solution)/shard_map/all_gather | solution.py:382
  19.3 42.1 %copy-start.9 = (bf16[16,32]{1,0:T(8,128)(2,1)S(1)}, bf16[16,32]{1,0:T(8,128)(2,1)}, u32[]{:S(2)}) copy-start(bf16[16,32]{1,0:T(8,128)(2,1)} %param.17) | copy-start | bytes 3076
  20.7 31.5 %all-to-all-start.1 = ((bf16[64,4,128]{2,1,0:T(4,128)(2,1)}), bf16[64,4,128]{2,1,0:T(4,128)(2,1)S(1)}, u32[]{:S(2)}, u32[]{:S(2)}) async-start(bf16[64,4,128]{2,1,0:T(4,128)(2,1)} %bitcast.2), calls=%async_computation.1 | async-start | bytes 131072 | tf_op jit(solution)/shard_map/all_to_all | solution.py:28
  53.2 17.7 %all-to-all-start.2 = ((bf16[8,256,128]{1,2,0:T(8,128)(2,1)}), bf16[8,256,128]{1,2,0:T(8,128)(2,1)S(1)}, u32[]{:S(2)}, u32[]{:S(2)}) async-start(bf16[8,256,128]{1,2,0:T(8,128)(2,1)} %broadcast_in_dim.57), calls=%async_computation.2 | async-start | bytes 1048576 | tf_op jit(solution)/shard_map/all_to_all | solution.py:28
  71.8 1.6 copy-start.6
  73.4 2.2 copy-start.4
  73.5 2.0 copy-start.5
  73.6 2.0 copy-start.13
  78.7 8.9 %all-to-all-start.3 = ((f32[8,2,256]{2,1,0:T(2,128)}), f32[8,2,256]{2,1,0:T(2,128)S(1)}, u32[]{:S(2)}, u32[]{:S(2)}) async-start(f32[8,2,256]{2,1,0:T(2,128)} %broadcast_in_dim.60), calls=%async_computation.3 | async-start | bytes 32768 | tf_op jit(solution)/shard_map/all_to_all | solution.py:28
  89.2 22.6 %all-to-all-start.4 = ((bf16[4,272,640]{2,1,0:T(8,128)(2,1)}), bf16[4,272,640]{2,1,0:T(8,128)(2,1)}, u32[]{:S(2)}, u32[]{:S(2)}) async-start(bf16[4,272,640]{2,1,0:T(8,128)(2,1)} %broadcast_in_dim.61), calls=%async_computation.4 | async-start | bytes 2785280 | tf_op jit(solution)/shard_map/all_to_all | solution.py:28
  95.4 1.2 copy-start.15
  96.6 18.8 %copy-start.10 = (f32[640]{0:T(1024)S(1)}, f32[640]{0:T(1024)}, u32[]{:S(2)}) copy-start(f32[640]{0:T(1024)} %param.24) | copy-start | bytes 7684
  96.6 19.4 %copy-start.11 = (f32[640]{0:T(1024)S(1)}, f32[640]{0:T(1024)}, u32[]{:S(2)}) copy-start(f32[640]{0:T(1024)} %param.23) | copy-start | bytes 7684
  96.6 21.7 %copy-start.2 = (bf16[256,640]{1,0:T(8,128)(2,1)S(1)}, bf16[256,640]{1,0:T(8,128)(2,1)}, u32[]{:S(2)}) copy-start(bf16[256,640]{1,0:T(8,128)(2,1)} %cot_ref.3) | copy-start | bytes 983044
  111.8 6.5 %collective-permute-start = (bf16[4,272,640]{2,1,0:T(8,128)(2,1)}, bf16[4,272,640]{2,1,0:T(8,128)(2,1)}, u32[]{:S(2)}, u32[]{:S(2)}) collective-permute-start(bf16[4,272,640]{2,1,0:T(8,128)(2,1)} %all-to-all-done.4.own_ref), channel_id=1, source_target_pairs={{0,1},{1,0},{2,3},{3,2},{4,5},{5,4},{6,7},{7,6},{8,9},{9,8},{10,11... | collective-permute-start | bytes 4177928 | tf_op jit(solution)/shard_map/ppermute | solution.py:353
  118.3 13.9 %copy-start.1 = (bf16[5120,640]{1,0:T(8,128)(2,1)S(1)}, bf16[5120,640]{1,0:T(8,128)(2,1)}, u32[]{:S(2)}) copy-start(bf16[5120,640]{1,0:T(8,128)(2,1)} %all-gather.2.cloned.1.call-done) | copy-start | bytes 19660804
  118.3 13.9 %copy-start.3 = (f32[1,640]{1,0:T(1,128)S(1)}, f32[1,640]{1,0:T(1,128)}, u32[]{:S(2)}) copy-start(f32[1,640]{1,0:T(1,128)} %broadcast_in_dim.51.gain_hbm.gain_ref) | copy-start | bytes 7684
  135.0 6.0 %collective-permute-start.1 = (bf16[4,256,640]{2,1,0:T(8,128)(2,1)S(1)}, bf16[4,256,640]{2,1,0:T(8,128)(2,1)S(1)}, u32[]{:S(2)}, u32[]{:S(2)}) collective-permute-start(bf16[4,256,640]{2,1,0:T(8,128)(2,1)S(1)} %get-tuple-element.38), channel_id=1, source_target_pairs={{0,1},{1,0},{2,3},{3,2},{4,5},{5,4},{6,7},{7,6},{8,9},{9,8},{10,11... | collective-permute-start | bytes 3932168 | tf_op jit(solution)/shard_map/ppermute | solution.py:353
  142.4 21.6 %all-to-all-start.6 = ((bf16[4,256,640]{2,1,0:T(8,128)(2,1)}), bf16[4,256,640]{2,1,0:T(8,128)(2,1)S(1)}, u32[]{:S(2)}, u32[]{:S(2)}) async-start(bf16[4,256,640]{2,1,0:T(8,128)(2,1)} %add_convert_fusion), calls=%async_computation.6 | async-start | bytes 2621440 | tf_op jit(solution)/shard_map/all_to_all | solution.py:28
  169.0 9.1 %all-to-all-start.7 = ((f32[8,24,128]{2,1,0:T(8,128)}), f32[8,24,128]{2,1,0:T(8,128)S(1)}, u32[]{:S(2)}, u32[]{:S(2)}) async-start(f32[8,24,128]{2,1,0:T(8,128)} %get-tuple-element.47), calls=%async_computation.7 | async-start | bytes 196608 | tf_op jit(solution)/shard_map/all_to_all | solution.py:28
  210.8 15.2 %all-to-all-start.10 = ((f32[8,24,128]{2,1,0:T(8,128)}), f32[8,24,128]{2,1,0:T(8,128)S(1)}, u32[]{:S(2)}, u32[]{:S(2)}) async-start(f32[8,24,128]{2,1,0:T(8,128)} %broadcast_in_dim.65), calls=%async_computation.10 | async-start | bytes 196608 | tf_op jit(solution)/shard_map/all_to_all | solution.py:28
Sparse Core Ops, SparseCore 0:
  19.4 93.2 all-gather.1

commit v8 on v7

--- a/solution.py
+++ b/solution.py
@@ -140,16 +140,6 @@
     )(cotangent, *in_hbm(bias[None], gain[None], own, other, weights))
 
 
-def fetch_blocks(w_ref, held, sems, core):
-    fetches = [
-        pltpu.make_async_copy(w_ref.at[2 * i + core], held.at[i], sems.at[i])
-        for i in range(held.shape[0])
-    ]
-    for fetch in fetches:
-        fetch.start()
-    return fetches
-
-
 def token_scales(sums_ref, query_width, width):
     sums = jnp.sum(sums_ref[...], axis=0)
     rinv = lax.rsqrt(sums[0:1] / query_width + epsilon)
@@ -157,23 +147,21 @@
     return across(rinv, width), across(pull, width)
 
 
-def theirs_kernel(sums_ref, query_ref, gain_ref, cot_ref, w_ref, out_ref, grad_ref, held, sems):
-    fetches = fetch_blocks(w_ref, held, sems, 1 - lax.axis_index("c"))
+def theirs_kernel(sums_ref, query_ref, gain_ref, cot_ref, w_ref, out_ref, grad_ref):
+    core = 1 - lax.axis_index("c")
     cols = query_ref.shape[1]
     rinv, pull = token_scales(sums_ref, N_TP * cols, cols)
     upstream = cot_ref[...].astype(f32) * gain_ref[...]
     grad_ref[...] = (upstream * rinv - query_ref[...] * pull).astype(bf16)
-    for i, fetch in enumerate(fetches):
-        fetch.wait()
-        out_ref[i] = dot(grad_ref[...], held[i], ((1,), (1,))).astype(bf16)
-
-
-def mine_kernel(sums_ref, query_ref, gain_ref, grad_ref, w_ref, out_ref, normed_ref, held, sems):
-    fetches = fetch_blocks(w_ref, held, sems, lax.axis_index("c"))
+    for i in range(out_ref.shape[0]):
+        out_ref[i] = dot(grad_ref[...], w_ref[2 * i + core], ((1,), (1,))).astype(bf16)
+
+
+def mine_kernel(sums_ref, query_ref, gain_ref, grad_ref, w_ref, out_ref, normed_ref):
+    core = lax.axis_index("c")
     cols = query_ref.shape[1]
-    for i, fetch in enumerate(fetches):
-        fetch.wait()
-        out_ref[i] = dot(grad_ref[...], held[i], ((1,), (1,))).astype(bf16)
+    for i in range(out_ref.shape[0]):
+        out_ref[i] = dot(grad_ref[...], w_ref[2 * i + core], ((1,), (1,))).astype(bf16)
     rinv, _ = token_scales(sums_ref, N_TP * cols, cols)
     normed_ref[...] = (query_ref[...] * rinv * gain_ref[...]).astype(bf16)
 
@@ -188,12 +176,8 @@
             jax.ShapeDtypeStruct((groups, tokens, width), bf16),
             jax.ShapeDtypeStruct((tokens, cols), bf16),
         ),
-        in_specs=in_vmem(4) + [pl.BlockSpec(memory_space=pl.ANY)],
+        in_specs=in_vmem(5),
         out_specs=tuple(in_vmem(2)),
-        scratch_shapes=[
-            pltpu.VMEM((groups, width, cols), bf16),
-            pltpu.SemaphoreType.DMA((groups,)),
-        ],
         compiler_params=pltpu.CompilerParams(vmem_limit_bytes=VMEM_LIMIT),
         cost_estimate=pl.CostEstimate(
             flops=2 * groups * tokens * cols * width,
@@ -254,9 +238,11 @@
     slot_ref[...] = slot_grad
     store = pltpu.make_async_copy(slot_ref, slot_hbm, sems.at[len(fetches)])
     store.start()
-    for fetch in fetches:
-        fetch.wait()
-    two_grad = dot(slot_grad, w_three_ref[...], ((1,), (1,))) * slope_two_ref[...]
+    fetches[0].wait()
+    two_grad = dot(slot_grad, w_three_ref[...], ((1,), (1,)))
+    fetches[1].wait()
+    two_grad = two_grad * slope_two_ref[...]
+    fetches[2].wait()
     part = w_two_t_ref.shape[0]
     grad_two = jnp.zeros((part, part), f32)
     one_grad = []
@@ -342,6 +328,29 @@
             flops=2 * rows * slots * width, bytes_accessed=2 * rows * slots, transcendentals=0
         ),
     )(*in_hbm(slot_grad, two_t))
+
+
+def unpack_kernel(small_ref, two_ref, one_ref):
+    rows_two, rows_one = two_ref.shape[0] // N_TP, one_ref.shape[0] // N_TP
+    for k in range(N_TP):
+        two_ref[k * rows_two : (k + 1) * rows_two] = small_ref[k, :rows_two]
+        one_ref[k * rows_one : (k + 1) * rows_one] = small_ref[
+            k, rows_two : rows_two + rows_one, : one_ref.shape[1]
+        ]
+
+
+def unpack(small, cell_in, c_one, c_two):
+    return pl.pallas_call(
+        unpack_kernel,
+        name="unpack",
+        out_shape=(
+            jax.ShapeDtypeStruct((c_two, c_two), f32),
+            jax.ShapeDtypeStruct((cell_in, c_one), f32),
+        ),
+        in_specs=in_vmem(1),
+        out_specs=tuple(in_vmem(2)),
+        compiler_params=pltpu.CompilerParams(vmem_limit_bytes=VMEM_LIMIT),
+    )(small)
 
 
 def halves(x):
@@ -485,7 +494,6 @@
     )
     grad_three = three(slot_grad, leaving_two)
 
-    rows_two = c_two // N_TP
     small = jnp.sum(exchange(small, TP), axis=0).astype(bf16)
     wide = small.shape[0] // per * c_two
     small = jnp.concatenate([small[k : k + per] for k in range(0, small.shape[0], per)], axis=1)
@@ -509,9 +517,7 @@
     section_three_grad = total[:, :width]
     small = [total[:, k : k + c_two] for k in range(width, width + wide, c_two)]
     small = copies(jnp.concatenate(small), TP, N_TP)
-    section_two_grad = small[:, :rows_two].reshape(c_two, c_two)
-    section_one_grad = small[:, rows_two : rows_two + cell_in // N_TP, :c_one]
-    section_one_grad = section_one_grad.reshape(cell_in, c_one)
+    section_two_grad, section_one_grad = unpack(small, cell_in, c_one, c_two)
     return (normed_query, section_three_grad, section_two_grad, section_one_grad)
 
 

time: 235 us -> 232 us (0.987)
    pallas_call x2, Pallas kernels: 6.06 us -> 3.64 us  [partial_matmul(): pl.pallas_call(kernel, name=name, out_shape=(jax.ShapeDtypeStruct((groups...]
  transfers between devices with their start and end apart: 10 -> 10, of which waited for: 8 -> 9; matrix products, arithmetic and copies ran while one was open for 8% -> 8% of each run, Pallas kernels for 2% -> 2%
where the time goes in v8:
time: 232 us; the launch traced here: 231 us
  waiting for transfers between devices  68 us (29%)
  starting transfers between devices  58.5 us (25%)
  blocking collectives  50.4 us (22%)
  Pallas kernels  16.8 us (7%)
  between operations  14.6 us (6%)
  local copies, waits for them, and re-layouts  10.5 us (5%)
  matrix products  9.46 us (4%)
  other arithmetic  2.78 us (1%)
    all_to_all x7, waiting for transfers between devices, exchange(): return lax.all_to_all(x, axis, split_axis=0, concat_axis=0, tiled=True)  65.7 us
    all_to_all x7, starting transfers between devices, exchange(): return lax.all_to_all(x, axis, split_axis=0, concat_axis=0, tiled=True)  52.2 us
    all_to_all x4, blocking collectives, exchange(): return lax.all_to_all(x, axis, split_axis=0, concat_axis=0, tiled=True)  50.4 us
    dot_general x7, matrix products, dot(): lax.dot_general(a, b, (dims, ((), ())), precision=precision, preferred_el...  9.46 us
    pallas_call x1, Pallas kernels, query_matmul(): pl.pallas_call(query_kernel, name='query', out_shape=(jax.ShapeDtypeStruc...  6.28 us
    ppermute x2, starting transfers between devices, swap_cores(): return lax.ppermute(x, 'c', [(0, 1), (1, 0)])  6.27 us
  transfers between devices with their start and end apart: 10, of which 9 were waited for; matrix products, arithmetic and copies ran while one was open for 8% of the time, Pallas kernels for 2%

profile of v8, /device:TPU:1, one launch (start us, length us, event | category | flops | bytes accessed | tf_op | source)
XLA Modules:
  0.0 231.0 jit_solution(6058400814339057200)
XLA Ops:
  8.2 11.1 %all_to_all.55 = bf16[4,80,640]{2,1,0:T(8,128)(2,1)} all-to-all(bf16[4,80,640]{2,1,0:T(8,128)(2,1)S(1)} %broadcast_in_dim.52), channel_id=1, replica_groups=mesh['z'=16,'x'=4,'y'=4,'c'=2] {'x'}, dimensions={0} | all-to-all | bytes 819200 | tf_op jit(solution)/shard_map/all_to_all | solution.py:28
  20.7 17.4 %all-to-all-start.1 = ((bf16[64,4,128]{2,1,0:T(4,128)(2,1)}), bf16[64,4,128]{2,1,0:T(4,128)(2,1)S(1)}, u32[]{:S(2)}, u32[]{:S(2)}) async-start(bf16[64,4,128]{2,1,0:T(4,128)(2,1)} %bitcast.2), calls=%async_computation.1 | async-start | bytes 131072 | tf_op jit(solution)/shard_map/all_to_all | solution.py:28
  38.1 14.1 %all-to-all-done.1 = bf16[64,4,128]{2,1,0:T(4,128)(2,1)S(1)} async-done(((bf16[64,4,128]{2,1,0:T(4,128)(2,1)}), bf16[64,4,128]{2,1,0:T(4,128)(2,1)S(1)}, u32[]{:S(2)}, u32[]{:S(2)}) %all-to-all-start.1) | async-done | bytes 65568 | tf_op jit(solution)/shard_map/all_to_all | solution.py:28
  53.2 8.2 %all-to-all-start.2 = ((bf16[8,256,128]{1,2,0:T(8,128)(2,1)}), bf16[8,256,128]{1,2,0:T(8,128)(2,1)S(1)}, u32[]{:S(2)}, u32[]{:S(2)}) async-start(bf16[8,256,128]{1,2,0:T(8,128)(2,1)} %broadcast_in_dim.57), calls=%async_computation.2 | async-start | bytes 1048576 | tf_op jit(solution)/shard_map/all_to_all | solution.py:28
  62.9 8.0 %all-to-all-done.2 = bf16[8,256,128]{1,2,0:T(8,128)(2,1)S(1)} async-done(((bf16[8,256,128]{1,2,0:T(8,128)(2,1)}), bf16[8,256,128]{1,2,0:T(8,128)(2,1)S(1)}, u32[]{:S(2)}, u32[]{:S(2)}) %all-to-all-start.2) | async-done | bytes 524320 | tf_op jit(solution)/shard_map/all_to_all | solution.py:28
  71.8 1.6 add_multiply_fusion
  73.6 2.0 add_multiply_fusion.1
  75.6 2.3 fusion.112
  78.7 4.1 %all-to-all-start.3 = ((f32[8,2,256]{2,1,0:T(2,128)}), f32[8,2,256]{2,1,0:T(2,128)S(1)}, u32[]{:S(2)}, u32[]{:S(2)}) async-start(f32[8,2,256]{2,1,0:T(2,128)} %broadcast_in_dim.60), calls=%async_computation.3 | async-start | bytes 32768 | tf_op jit(solution)/shard_map/all_to_all | solution.py:28
  82.9 4.7 %all-to-all-done.3 = f32[8,2,256]{2,1,0:T(2,128)S(1)} async-done(((f32[8,2,256]{2,1,0:T(2,128)}), f32[8,2,256]{2,1,0:T(2,128)S(1)}, u32[]{:S(2)}, u32[]{:S(2)}) %all-to-all-start.3) | async-done | bytes 16416 | tf_op jit(solution)/shard_map/all_to_all | solution.py:28
  89.2 4.3 %all-to-all-start.4 = ((bf16[4,272,640]{2,1,0:T(8,128)(2,1)}), bf16[4,272,640]{2,1,0:T(8,128)(2,1)}, u32[]{:S(2)}, u32[]{:S(2)}) async-start(bf16[4,272,640]{2,1,0:T(8,128)(2,1)} %broadcast_in_dim.61), calls=%async_computation.4 | async-start | bytes 2785280 | tf_op jit(solution)/shard_map/all_to_all | solution.py:28
  93.8 1.6 copy.36
  96.6 1.5 convolution_convert_fusion.1.two_t_hbm
  98.1 13.7 %all-to-all-done.4.own_ref = bf16[4,272,640]{2,1,0:T(8,128)(2,1)} async-done(((bf16[4,272,640]{2,1,0:T(8,128)(2,1)}), bf16[4,272,640]{2,1,0:T(8,128)(2,1)}, u32[]{:S(2)}, u32[]{:S(2)}) %all-to-all-start.4) | async-done | bytes 1392672 | tf_op jit(solution)/shard_map/all_to_all | solution.py:28
  111.8 3.6 %collective-permute-start = (bf16[4,272,640]{2,1,0:T(8,128)(2,1)}, bf16[4,272,640]{2,1,0:T(8,128)(2,1)}, u32[]{:S(2)}, u32[]{:S(2)}) collective-permute-start(bf16[4,272,640]{2,1,0:T(8,128)(2,1)} %all-to-all-done.4.own_ref), channel_id=1, source_target_pairs={{0,1},{1,0},{2,3},{3,2},{4,5},{5,4},{6,7},{7,6},{8,9},{9,8},{10,11... | collective-permute-start | bytes 4177928 | tf_op jit(solution)/shard_map/ppermute | solution.py:362
  116.6 1.7 collective-permute-done.other_ref
  118.3 6.3 %query.1 = (f32[256,640]{1,0:T(8,128)S(1)}, f32[8,8,256]{2,1,0:T(8,128)S(1)}) custom-call(bf16[256,640]{1,0:T(8,128)(2,1)S(1)} %copy-done.2, f32[1,640]{1,0:T(1,128)} %broadcast_in_dim.50.bias_hbm, f32[1,640]{1,0:T(1,128)} %broadcast_in_dim.51.gain_hbm.gain_ref, bf16[4,272,640]{2,1,0:T(8,128)(2,1)} %all-to-all-done.4.own_ref, ...), custom_call_target="tpu_custom_call" | custom-call | tf_op jit(solution)/shard_map/query/pallas_call | solution.py:122
  124.6 7.6 %all_to_all.56.sums_ref = f32[8,8,256]{2,1,0:T(8,128)S(1)} all-to-all(f32[8,8,256]{2,1,0:T(8,128)S(1)} %get-tuple-element.33), channel_id=1, replica_groups=mesh['z'=16,'x'=4,'y'=4,'c'=2] {'y','c'}, dimensions={0} | all-to-all | bytes 131072 | tf_op jit(solution)/shard_map/all_to_all | solution.py:28
  132.2 1.5 theirs.1
  133.7 2.7 %collective-permute-start.1 = (bf16[4,256,640]{2,1,0:T(8,128)(2,1)S(1)}, bf16[4,256,640]{2,1,0:T(8,128)(2,1)S(1)}, u32[]{:S(2)}, u32[]{:S(2)}) collective-permute-start(bf16[4,256,640]{2,1,0:T(8,128)(2,1)S(1)} %get-tuple-element.40), channel_id=1, source_target_pairs={{0,1},{1,0},{2,3},{3,2},{4,5},{5,4},{6,7},{7,6},{8,9},{9,8},{10,11... | collective-permute-start | bytes 3932168 | tf_op jit(solution)/shard_map/ppermute | solution.py:362
  136.4 2.1 mine.1
  139.1 1.4 add_convert_fusion
  140.5 3.5 %all-to-all-start.6 = ((bf16[4,256,640]{2,1,0:T(8,128)(2,1)}), bf16[4,256,640]{2,1,0:T(8,128)(2,1)S(1)}, u32[]{:S(2)}, u32[]{:S(2)}) async-start(bf16[4,256,640]{2,1,0:T(8,128)(2,1)} %add_convert_fusion), calls=%async_computation.6 | async-start | bytes 2621440 | tf_op jit(solution)/shard_map/all_to_all | solution.py:28
  144.0 17.6 %all-to-all-done.6.pair_ref = bf16[4,256,640]{2,1,0:T(8,128)(2,1)S(1)} async-done(((bf16[4,256,640]{2,1,0:T(8,128)(2,1)}), bf16[4,256,640]{2,1,0:T(8,128)(2,1)S(1)}, u32[]{:S(2)}, u32[]{:S(2)}) %all-to-all-start.6) | async-done | bytes 1310752 | tf_op jit(solution)/shard_map/all_to_all | solution.py:28
  161.7 4.4 %back.1 = (bf16[512,640]{1,0:T(8,128)(2,1)}, f32[8,24,128]{2,1,0:T(8,128)}) custom-call(f32[8,8,256]{2,1,0:T(8,128)S(1)} %all_to_all.56.sums_ref, f32[1,256]{1,0:T(1,128)S(1)} %bitcast.55, f32[1,640]{1,0:T(1,128)S(1)} %broadcast_in_dim.62.scale_ref, bf16[128,128]{1,0:T(8,128)(2,1)S(1)} %bitcast.54, bf16[4,256,640]{2,1,0:T(8,128)(2,1)S(1)} %all-to-all-done.6.pair_ref, ...), custom_call_target="tpu_custom_call" | custom-call | tf_op jit(solution)/shard_map/back/pallas_call | solution.py:280
  166.1 4.5 %all-to-all-start.7 = ((f32[8,24,128]{2,1,0:T(8,128)}), f32[8,24,128]{2,1,0:T(8,128)S(1)}, u32[]{:S(2)}, u32[]{:S(2)}) async-start(f32[8,24,128]{2,1,0:T(8,128)} %get-tuple-element.49), calls=%async_computation.7 | async-start | bytes 196608 | tf_op jit(solution)/shard_map/all_to_all | solution.py:28
  170.6 1.8 three.1
  172.4 3.2 %all-to-all-done.7 = f32[8,24,128]{2,1,0:T(8,128)S(1)} async-done(((f32[8,24,128]{2,1,0:T(8,128)}), f32[8,24,128]{2,1,0:T(8,128)S(1)}, u32[]{:S(2)}, u32[]{:S(2)}) %all-to-all-start.7) | async-done | bytes 98336 | tf_op jit(solution)/shard_map/all_to_all | solution.py:28
  175.7 12.6 %all_to_all.57 = bf16[4,136,640]{2,1,0:T(8,128)(2,1)S(1)} all-to-all(bf16[4,136,640]{2,1,0:T(8,128)(2,1)S(1)} %pad_maximum_fusion), channel_id=1, replica_groups=mesh['z'=16,'x'=4,'y'=4,'c'=2] {'x'}, dimensions={0} | all-to-all | bytes 1392640 | tf_op jit(solution)/shard_map/all_to_all | solution.py:28
  188.6 19.1 %all_to_all.58 = bf16[16,8,1024]{2,1,0:T(8,128)(2,1)S(1)} all-to-all(bf16[16,8,1024]{2,1,0:T(8,128)(2,1)S(1)} %pad_maximum_fusion.3), channel_id=1, replica_groups=mesh['z'=16,'x'=4,'y'=4,'c'=2] {'z'}, dimensions={0} | all-to-all | bytes 524288 | tf_op jit(solution)/shard_map/all_to_all | solution.py:28
  208.3 10.2 %all-to-all-start.10 = ((f32[8,24,128]{2,1,0:T(8,128)}), f32[8,24,128]{2,1,0:T(8,128)S(1)}, u32[]{:S(2)}, u32[]{:S(2)}) async-start(f32[8,24,128]{2,1,0:T(8,128)} %broadcast_in_dim.65), calls=%async_computation.10 | async-start | bytes 196608 | tf_op jit(solution)/shard_map/all_to_all | solution.py:28
  219.1 4.4 %all-to-all-done.10.small_ref = f32[8,24,128]{2,1,0:T(8,128)S(1)} async-done(((f32[8,24,128]{2,1,0:T(8,128)}), f32[8,24,128]{2,1,0:T(8,128)S(1)}, u32[]{:S(2)}, u32[]{:S(2)}) %all-to-all-start.10) | async-done | bytes 98336 | tf_op jit(solution)/shard_map/all_to_all | solution.py:28
  (98 shorter events, 13.6 us)
Async XLA Ops:
  7.2 12.5 %copy-start = (bf16[256,256]{1,0:T(8,128)(2,1)S(1)}, bf16[256,256]{1,0:T(8,128)(2,1)}, u32[]{:S(2)}) copy-start(bf16[256,256]{1,0:T(8,128)(2,1)} %param.14) | copy-start | bytes 393220
  7.2 12.2 %copy-start.12 = (s32[256,1]{0,1:T(1,128)S(1)}, s32[256,1]{0,1:T(1,128)}, u32[]{:S(2)}) copy-start(s32[256,1]{0,1:T(1,128)} %param.15) | copy-start | bytes 3076
  7.2 12.4 %copy-start.14 = (s32[256]{0:T(256)S(1)}, s32[256]{0:T(256)}, u32[]{:S(2)}) copy-start(s32[256]{0:T(256)} %param.16) | copy-start | bytes 3076
  7.2 12.2 %copy-start.7 = (f32[640]{0:T(1024)S(1)}, f32[640]{0:T(1024)}, u32[]{:S(2)}) copy-start(f32[640]{0:T(1024)} %param.20) | copy-start | bytes 7684
  7.2 30.9 %copy-start.8 = (f32[640]{0:T(1024)S(1)}, f32[640]{0:T(1024)}, u32[]{:S(2)}) copy-start(f32[640]{0:T(1024)} %param.21) | copy-start | bytes 7684
  7.2 111.1 %all-gather.2.cloned.1.call-start = ((), (), s32[]{:S(2)}) async-start(), calls=%async_computation.11 | async-start | bytes 6963200 | tf_op jit(solution)/shard_map/all_gather | solution.py:391
  19.3 42.1 %copy-start.9 = (bf16[16,32]{1,0:T(8,128)(2,1)S(1)}, bf16[16,32]{1,0:T(8,128)(2,1)}, u32[]{:S(2)}) copy-start(bf16[16,32]{1,0:T(8,128)(2,1)} %param.17) | copy-start | bytes 3076
  20.7 31.5 %all-to-all-start.1 = ((bf16[64,4,128]{2,1,0:T(4,128)(2,1)}), bf16[64,4,128]{2,1,0:T(4,128)(2,1)S(1)}, u32[]{:S(2)}, u32[]{:S(2)}) async-start(bf16[64,4,128]{2,1,0:T(4,128)(2,1)} %bitcast.2), calls=%async_computation.1 | async-start | bytes 131072 | tf_op jit(solution)/shard_map/all_to_all | solution.py:28
  53.2 17.7 %all-to-all-start.2 = ((bf16[8,256,128]{1,2,0:T(8,128)(2,1)}), bf16[8,256,128]{1,2,0:T(8,128)(2,1)S(1)}, u32[]{:S(2)}, u32[]{:S(2)}) async-start(bf16[8,256,128]{1,2,0:T(8,128)(2,1)} %broadcast_in_dim.57), calls=%async_computation.2 | async-start | bytes 1048576 | tf_op jit(solution)/shard_map/all_to_all | solution.py:28
  71.8 1.6 copy-start.6
  73.4 2.2 copy-start.4
  73.5 2.0 copy-start.5
  73.6 2.0 copy-start.13
  78.7 8.9 %all-to-all-start.3 = ((f32[8,2,256]{2,1,0:T(2,128)}), f32[8,2,256]{2,1,0:T(2,128)S(1)}, u32[]{:S(2)}, u32[]{:S(2)}) async-start(f32[8,2,256]{2,1,0:T(2,128)} %broadcast_in_dim.60), calls=%async_computation.3 | async-start | bytes 32768 | tf_op jit(solution)/shard_map/all_to_all | solution.py:28
  89.2 22.6 %all-to-all-start.4 = ((bf16[4,272,640]{2,1,0:T(8,128)(2,1)}), bf16[4,272,640]{2,1,0:T(8,128)(2,1)}, u32[]{:S(2)}, u32[]{:S(2)}) async-start(bf16[4,272,640]{2,1,0:T(8,128)(2,1)} %broadcast_in_dim.61), calls=%async_computation.4 | async-start | bytes 2785280 | tf_op jit(solution)/shard_map/all_to_all | solution.py:28
  95.4 1.2 copy-start.15
  96.6 18.8 %copy-start.10 = (f32[640]{0:T(1024)S(1)}, f32[640]{0:T(1024)}, u32[]{:S(2)}) copy-start(f32[640]{0:T(1024)} %param.24) | copy-start | bytes 7684
  96.6 19.4 %copy-start.11 = (f32[640]{0:T(1024)S(1)}, f32[640]{0:T(1024)}, u32[]{:S(2)}) copy-start(f32[640]{0:T(1024)} %param.23) | copy-start | bytes 7684
  96.6 21.7 %copy-start.2 = (bf16[256,640]{1,0:T(8,128)(2,1)S(1)}, bf16[256,640]{1,0:T(8,128)(2,1)}, u32[]{:S(2)}) copy-start(bf16[256,640]{1,0:T(8,128)(2,1)} %cot_ref.3) | copy-start | bytes 983044
  111.8 6.5 %collective-permute-start = (bf16[4,272,640]{2,1,0:T(8,128)(2,1)}, bf16[4,272,640]{2,1,0:T(8,128)(2,1)}, u32[]{:S(2)}, u32[]{:S(2)}) collective-permute-start(bf16[4,272,640]{2,1,0:T(8,128)(2,1)} %all-to-all-done.4.own_ref), channel_id=1, source_target_pairs={{0,1},{1,0},{2,3},{3,2},{4,5},{5,4},{6,7},{7,6},{8,9},{9,8},{10,11... | collective-permute-start | bytes 4177928 | tf_op jit(solution)/shard_map/ppermute | solution.py:362
  118.3 13.9 %copy-start.1 = (bf16[5120,640]{1,0:T(8,128)(2,1)S(1)}, bf16[5120,640]{1,0:T(8,128)(2,1)}, u32[]{:S(2)}) copy-start(bf16[5120,640]{1,0:T(8,128)(2,1)} %all-gather.2.cloned.1.call-done) | copy-start | bytes 19660804
  118.3 13.9 %copy-start.3 = (f32[1,640]{1,0:T(1,128)S(1)}, f32[1,640]{1,0:T(1,128)}, u32[]{:S(2)}) copy-start(f32[1,640]{1,0:T(1,128)} %broadcast_in_dim.51.gain_hbm.gain_ref) | copy-start | bytes 7684
  133.7 5.3 %collective-permute-start.1 = (bf16[4,256,640]{2,1,0:T(8,128)(2,1)S(1)}, bf16[4,256,640]{2,1,0:T(8,128)(2,1)S(1)}, u32[]{:S(2)}, u32[]{:S(2)}) collective-permute-start(bf16[4,256,640]{2,1,0:T(8,128)(2,1)S(1)} %get-tuple-element.40), channel_id=1, source_target_pairs={{0,1},{1,0},{2,3},{3,2},{4,5},{5,4},{6,7},{7,6},{8,9},{9,8},{10,11... | collective-permute-start | bytes 3932168 | tf_op jit(solution)/shard_map/ppermute | solution.py:362
  140.5 21.2 %all-to-all-start.6 = ((bf16[4,256,640]{2,1,0:T(8,128)(2,1)}), bf16[4,256,640]{2,1,0:T(8,128)(2,1)S(1)}, u32[]{:S(2)}, u32[]{:S(2)}) async-start(bf16[4,256,640]{2,1,0:T(8,128)(2,1)} %add_convert_fusion), calls=%async_computation.6 | async-start | bytes 2621440 | tf_op jit(solution)/shard_map/all_to_all | solution.py:28
  166.1 9.5 %all-to-all-start.7 = ((f32[8,24,128]{2,1,0:T(8,128)}), f32[8,24,128]{2,1,0:T(8,128)S(1)}, u32[]{:S(2)}, u32[]{:S(2)}) async-start(f32[8,24,128]{2,1,0:T(8,128)} %get-tuple-element.49), calls=%async_computation.7 | async-start | bytes 196608 | tf_op jit(solution)/shard_map/all_to_all | solution.py:28
  208.3 15.2 %all-to-all-start.10 = ((f32[8,24,128]{2,1,0:T(8,128)}), f32[8,24,128]{2,1,0:T(8,128)S(1)}, u32[]{:S(2)}, u32[]{:S(2)}) async-start(f32[8,24,128]{2,1,0:T(8,128)} %broadcast_in_dim.65), calls=%async_computation.10 | async-start | bytes 196608 | tf_op jit(solution)/shard_map/all_to_all | solution.py:28
Sparse Core Ops, SparseCore 0:
  19.4 93.2 all-gather.1

commit v9 on v8

--- a/solution.py
+++ b/solution.py
@@ -57,10 +57,10 @@
     w_ref,
     out_ref,
     sums_ref,
+    held,
     bias_ref,
     gain_ref,
     left,
-    held,
     row_sems,
     sems,
 ):
@@ -125,14 +125,14 @@
         out_shape=(
             jax.ShapeDtypeStruct((tokens, cols), f32),
             jax.ShapeDtypeStruct((N_TP, 8, tokens), f32),
+            pltpu.VMEM((weights.shape[0] * weights.shape[1], cols), bf16),
         ),
         in_specs=in_vmem(1) + [pl.BlockSpec(memory_space=pl.ANY)] * 5,
-        out_specs=tuple(in_vmem(2)),
+        out_specs=tuple(in_vmem(3)),
         scratch_shapes=[
             pltpu.VMEM((1, cols), f32),
             pltpu.VMEM((1, cols), f32),
             pltpu.VMEM((2 * own.shape[0],) + own.shape[1:], bf16),
-            pltpu.VMEM((weights.shape[0] * weights.shape[1], cols), bf16),
             pltpu.SemaphoreType.DMA((2,)),
             pltpu.SemaphoreType.DMA((2, weights.shape[0])),
         ],
@@ -148,20 +148,18 @@
 
 
 def theirs_kernel(sums_ref, query_ref, gain_ref, cot_ref, w_ref, out_ref, grad_ref):
-    core = 1 - lax.axis_index("c")
     cols = query_ref.shape[1]
     rinv, pull = token_scales(sums_ref, N_TP * cols, cols)
     upstream = cot_ref[...].astype(f32) * gain_ref[...]
     grad_ref[...] = (upstream * rinv - query_ref[...] * pull).astype(bf16)
     for i in range(out_ref.shape[0]):
-        out_ref[i] = dot(grad_ref[...], w_ref[2 * i + core], ((1,), (1,))).astype(bf16)
+        out_ref[i] = dot(grad_ref[...], w_ref[2 * i + 1], ((1,), (1,))).astype(bf16)
 
 
 def mine_kernel(sums_ref, query_ref, gain_ref, grad_ref, w_ref, out_ref, normed_ref):
-    core = lax.axis_index("c")
     cols = query_ref.shape[1]
     for i in range(out_ref.shape[0]):
-        out_ref[i] = dot(grad_ref[...], w_ref[2 * i + core], ((1,), (1,))).astype(bf16)
+        out_ref[i] = dot(grad_ref[...], w_ref[2 * i], ((1,), (1,))).astype(bf16)
     rinv, _ = token_scales(sums_ref, N_TP * cols, cols)
     normed_ref[...] = (query_ref[...] * rinv * gain_ref[...]).astype(bf16)
 
@@ -477,7 +475,8 @@
     normed, inverse, select, leaving_two, slope_two, one_t, slope_one, pose_t, w_two_t = ready
     other = swap_cores(own)
 
-    query, sums = query_matmul(own, other, bias_query, gain_query, cotangent, weights)
+    query, sums, held = query_matmul(own, other, bias_query, gain_query, cotangent, weights)
+    weights = held.reshape(weights.shape)
     sums = exchange(sums, TP)
     theirs, query_grad = partial_matmul(
         theirs_kernel, "theirs", sums, query, gain_query, cotangent, weights

time: 232 us -> 232 us (level)
  no operation moved by 1% of the time
where the time goes in v9:
time: 232 us; the launch traced here: 231 us
  waiting for transfers between devices  67.9 us (29%)
  starting transfers between devices  58.6 us (25%)
  blocking collectives  50.3 us (22%)
  Pallas kernels  16.7 us (7%)
  between operations  14.6 us (6%)
  local copies, waits for them, and re-layouts  10.6 us (5%)
  matrix products  9.45 us (4%)
  other arithmetic  2.75 us (1%)
    all_to_all x7, waiting for transfers between devices, exchange(): return lax.all_to_all(x, axis, split_axis=0, concat_axis=0, tiled=True)  65.6 us
    all_to_all x7, starting transfers between devices, exchange(): return lax.all_to_all(x, axis, split_axis=0, concat_axis=0, tiled=True)  52.2 us
    all_to_all x4, blocking collectives, exchange(): return lax.all_to_all(x, axis, split_axis=0, concat_axis=0, tiled=True)  50.3 us
    dot_general x7, matrix products, dot(): lax.dot_general(a, b, (dims, ((), ())), precision=precision, preferred_el...  9.45 us
    ppermute x2, starting transfers between devices, swap_cores(): return lax.ppermute(x, 'c', [(0, 1), (1, 0)])  6.27 us
    pallas_call x1, Pallas kernels, query_matmul(): pl.pallas_call(query_kernel, name='query', out_shape=(jax.ShapeDtypeStruc...  6.14 us
  transfers between devices with their start and end apart: 10, of which 9 were waited for; matrix products, arithmetic and copies ran while one was open for 8% of the time, Pallas kernels for 2%

profile of v9, /device:TPU:1, one launch (start us, length us, event | category | flops | bytes accessed | tf_op | source)
XLA Modules:
  0.0 230.8 jit_solution(5281857224442564930)
XLA Ops:
  8.2 11.1 %all_to_all.55 = bf16[4,80,640]{2,1,0:T(8,128)(2,1)} all-to-all(bf16[4,80,640]{2,1,0:T(8,128)(2,1)S(1)} %broadcast_in_dim.52), channel_id=1, replica_groups=mesh['z'=16,'x'=4,'y'=4,'c'=2] {'x'}, dimensions={0} | all-to-all | bytes 819200 | tf_op jit(solution)/shard_map/all_to_all | solution.py:28
  20.7 17.4 %all-to-all-start.1 = ((bf16[64,4,128]{2,1,0:T(4,128)(2,1)}), bf16[64,4,128]{2,1,0:T(4,128)(2,1)S(1)}, u32[]{:S(2)}, u32[]{:S(2)}) async-start(bf16[64,4,128]{2,1,0:T(4,128)(2,1)} %bitcast.2), calls=%async_computation.1 | async-start | bytes 131072 | tf_op jit(solution)/shard_map/all_to_all | solution.py:28
  38.1 14.1 %all-to-all-done.1 = bf16[64,4,128]{2,1,0:T(4,128)(2,1)S(1)} async-done(((bf16[64,4,128]{2,1,0:T(4,128)(2,1)}), bf16[64,4,128]{2,1,0:T(4,128)(2,1)S(1)}, u32[]{:S(2)}, u32[]{:S(2)}) %all-to-all-start.1) | async-done | bytes 65568 | tf_op jit(solution)/shard_map/all_to_all | solution.py:28
  53.2 8.2 %all-to-all-start.2 = ((bf16[8,256,128]{1,2,0:T(8,128)(2,1)}), bf16[8,256,128]{1,2,0:T(8,128)(2,1)S(1)}, u32[]{:S(2)}, u32[]{:S(2)}) async-start(bf16[8,256,128]{1,2,0:T(8,128)(2,1)} %broadcast_in_dim.57), calls=%async_computation.2 | async-start | bytes 1048576 | tf_op jit(solution)/shard_map/all_to_all | solution.py:28
  63.0 7.9 %all-to-all-done.2 = bf16[8,256,128]{1,2,0:T(8,128)(2,1)S(1)} async-done(((bf16[8,256,128]{1,2,0:T(8,128)(2,1)}), bf16[8,256,128]{1,2,0:T(8,128)(2,1)S(1)}, u32[]{:S(2)}, u32[]{:S(2)}) %all-to-all-start.2) | async-done | bytes 524320 | tf_op jit(solution)/shard_map/all_to_all | solution.py:28
  71.8 1.6 add_multiply_fusion
  73.6 2.0 add_multiply_fusion.1
  75.6 2.3 fusion.112
  78.7 4.1 %all-to-all-start.3 = ((f32[8,2,256]{2,1,0:T(2,128)}), f32[8,2,256]{2,1,0:T(2,128)S(1)}, u32[]{:S(2)}, u32[]{:S(2)}) async-start(f32[8,2,256]{2,1,0:T(2,128)} %broadcast_in_dim.60), calls=%async_computation.3 | async-start | bytes 32768 | tf_op jit(solution)/shard_map/all_to_all | solution.py:28
  82.9 4.7 %all-to-all-done.3 = f32[8,2,256]{2,1,0:T(2,128)S(1)} async-done(((f32[8,2,256]{2,1,0:T(2,128)}), f32[8,2,256]{2,1,0:T(2,128)S(1)}, u32[]{:S(2)}, u32[]{:S(2)}) %all-to-all-start.3) | async-done | bytes 16416 | tf_op jit(solution)/shard_map/all_to_all | solution.py:28
  89.2 4.3 %all-to-all-start.4 = ((bf16[4,272,640]{2,1,0:T(8,128)(2,1)}), bf16[4,272,640]{2,1,0:T(8,128)(2,1)}, u32[]{:S(2)}, u32[]{:S(2)}) async-start(bf16[4,272,640]{2,1,0:T(8,128)(2,1)} %broadcast_in_dim.61), calls=%async_computation.4 | async-start | bytes 2785280 | tf_op jit(solution)/shard_map/all_to_all | solution.py:28
  93.8 1.6 copy.36
  96.6 1.4 convolution_convert_fusion.1.two_t_hbm
  98.1 13.8 %all-to-all-done.4.own_ref = bf16[4,272,640]{2,1,0:T(8,128)(2,1)} async-done(((bf16[4,272,640]{2,1,0:T(8,128)(2,1)}), bf16[4,272,640]{2,1,0:T(8,128)(2,1)}, u32[]{:S(2)}, u32[]{:S(2)}) %all-to-all-start.4) | async-done | bytes 1392672 | tf_op jit(solution)/shard_map/all_to_all | solution.py:28
  111.8 3.6 %collective-permute-start = (bf16[4,272,640]{2,1,0:T(8,128)(2,1)}, bf16[4,272,640]{2,1,0:T(8,128)(2,1)}, u32[]{:S(2)}, u32[]{:S(2)}) collective-permute-start(bf16[4,272,640]{2,1,0:T(8,128)(2,1)} %all-to-all-done.4.own_ref), channel_id=1, source_target_pairs={{0,1},{1,0},{2,3},{3,2},{4,5},{5,4},{6,7},{7,6},{8,9},{9,8},{10,11... | collective-permute-start | bytes 4177928 | tf_op jit(solution)/shard_map/ppermute | solution.py:360
  116.6 1.7 collective-permute-done.other_ref
  118.3 6.1 %query.1 = (f32[256,640]{1,0:T(8,128)S(1)}, f32[8,8,256]{2,1,0:T(8,128)S(1)}, bf16[5120,640]{1,0:T(8,128)(2,1)S(1)}) custom-call(bf16[256,640]{1,0:T(8,128)(2,1)S(1)} %copy-done.1, f32[1,640]{1,0:T(1,128)} %broadcast_in_dim.50.bias_hbm, f32[1,640]{1,0:T(1,128)} %broadcast_in_dim.51.gain_hbm.gain_ref, bf16[4,272,640]{2,1,0:T(8,128)(2,1)} %all-to-all-done.4.own_ref, ...), custom_call_target="tpu_custom_call" | custom-call | tf_op jit(solution)/shard_map/query/pallas_call | solution.py:122
  124.5 7.6 %all_to_all.56.sums_ref = f32[8,8,256]{2,1,0:T(8,128)S(1)} all-to-all(f32[8,8,256]{2,1,0:T(8,128)S(1)} %get-tuple-element.34), channel_id=1, replica_groups=mesh['z'=16,'x'=4,'y'=4,'c'=2] {'y','c'}, dimensions={0} | all-to-all | bytes 131072 | tf_op jit(solution)/shard_map/all_to_all | solution.py:28
  132.1 1.5 theirs.1
  133.6 2.7 %collective-permute-start.1 = (bf16[4,256,640]{2,1,0:T(8,128)(2,1)S(1)}, bf16[4,256,640]{2,1,0:T(8,128)(2,1)S(1)}, u32[]{:S(2)}, u32[]{:S(2)}) collective-permute-start(bf16[4,256,640]{2,1,0:T(8,128)(2,1)S(1)} %get-tuple-element.42), channel_id=1, source_target_pairs={{0,1},{1,0},{2,3},{3,2},{4,5},{5,4},{6,7},{7,6},{8,9},{9,8},{10,11... | collective-permute-start | bytes 3932168 | tf_op jit(solution)/shard_map/ppermute | solution.py:360
  136.3 2.1 mine.1
  138.9 1.4 add_convert_fusion
  140.3 3.5 %all-to-all-start.6 = ((bf16[4,256,640]{2,1,0:T(8,128)(2,1)}), bf16[4,256,640]{2,1,0:T(8,128)(2,1)S(1)}, u32[]{:S(2)}, u32[]{:S(2)}) async-start(bf16[4,256,640]{2,1,0:T(8,128)(2,1)} %add_convert_fusion), calls=%async_computation.6 | async-start | bytes 2621440 | tf_op jit(solution)/shard_map/all_to_all | solution.py:28
  143.9 17.6 %all-to-all-done.6.pair_ref = bf16[4,256,640]{2,1,0:T(8,128)(2,1)S(1)} async-done(((bf16[4,256,640]{2,1,0:T(8,128)(2,1)}), bf16[4,256,640]{2,1,0:T(8,128)(2,1)S(1)}, u32[]{:S(2)}, u32[]{:S(2)}) %all-to-all-start.6) | async-done | bytes 1310752 | tf_op jit(solution)/shard_map/all_to_all | solution.py:28
  161.5 4.4 %back.1 = (bf16[512,640]{1,0:T(8,128)(2,1)}, f32[8,24,128]{2,1,0:T(8,128)}) custom-call(f32[8,8,256]{2,1,0:T(8,128)S(1)} %all_to_all.56.sums_ref, f32[1,256]{1,0:T(1,128)S(1)} %bitcast.55, f32[1,640]{1,0:T(1,128)S(1)} %broadcast_in_dim.62.scale_ref, bf16[128,128]{1,0:T(8,128)(2,1)S(1)} %bitcast.54, bf16[4,256,640]{2,1,0:T(8,128)(2,1)S(1)} %all-to-all-done.6.pair_ref, ...), custom_call_target="tpu_custom_call" | custom-call | tf_op jit(solution)/shard_map/back/pallas_call | solution.py:278
  165.9 4.5 %all-to-all-start.7 = ((f32[8,24,128]{2,1,0:T(8,128)}), f32[8,24,128]{2,1,0:T(8,128)S(1)}, u32[]{:S(2)}, u32[]{:S(2)}) async-start(f32[8,24,128]{2,1,0:T(8,128)} %get-tuple-element.51), calls=%async_computation.7 | async-start | bytes 196608 | tf_op jit(solution)/shard_map/all_to_all | solution.py:28
  170.4 1.8 three.1
  172.3 3.2 %all-to-all-done.7 = f32[8,24,128]{2,1,0:T(8,128)S(1)} async-done(((f32[8,24,128]{2,1,0:T(8,128)}), f32[8,24,128]{2,1,0:T(8,128)S(1)}, u32[]{:S(2)}, u32[]{:S(2)}) %all-to-all-start.7) | async-done | bytes 98336 | tf_op jit(solution)/shard_map/all_to_all | solution.py:28
  175.6 12.6 %all_to_all.57 = bf16[4,136,640]{2,1,0:T(8,128)(2,1)S(1)} all-to-all(bf16[4,136,640]{2,1,0:T(8,128)(2,1)S(1)} %pad_maximum_fusion), channel_id=1, replica_groups=mesh['z'=16,'x'=4,'y'=4,'c'=2] {'x'}, dimensions={0} | all-to-all | bytes 1392640 | tf_op jit(solution)/shard_map/all_to_all | solution.py:28
  188.4 19.0 %all_to_all.58 = bf16[16,8,1024]{2,1,0:T(8,128)(2,1)S(1)} all-to-all(bf16[16,8,1024]{2,1,0:T(8,128)(2,1)S(1)} %pad_maximum_fusion.3), channel_id=1, replica_groups=mesh['z'=16,'x'=4,'y'=4,'c'=2] {'z'}, dimensions={0} | all-to-all | bytes 524288 | tf_op jit(solution)/shard_map/all_to_all | solution.py:28
  208.2 10.2 %all-to-all-start.10 = ((f32[8,24,128]{2,1,0:T(8,128)}), f32[8,24,128]{2,1,0:T(8,128)S(1)}, u32[]{:S(2)}, u32[]{:S(2)}) async-start(f32[8,24,128]{2,1,0:T(8,128)} %broadcast_in_dim.65), calls=%async_computation.10 | async-start | bytes 196608 | tf_op jit(solution)/shard_map/all_to_all | solution.py:28
  218.9 4.4 %all-to-all-done.10.small_ref = f32[8,24,128]{2,1,0:T(8,128)S(1)} async-done(((f32[8,24,128]{2,1,0:T(8,128)}), f32[8,24,128]{2,1,0:T(8,128)S(1)}, u32[]{:S(2)}, u32[]{:S(2)}) %all-to-all-start.10) | async-done | bytes 98336 | tf_op jit(solution)/shard_map/all_to_all | solution.py:28
  (96 shorter events, 13.7 us)
Async XLA Ops:
  7.2 12.5 %copy-start = (bf16[256,256]{1,0:T(8,128)(2,1)S(1)}, bf16[256,256]{1,0:T(8,128)(2,1)}, u32[]{:S(2)}) copy-start(bf16[256,256]{1,0:T(8,128)(2,1)} %param.14) | copy-start | bytes 393220
  7.2 12.2 %copy-start.11 = (s32[256,1]{0,1:T(1,128)S(1)}, s32[256,1]{0,1:T(1,128)}, u32[]{:S(2)}) copy-start(s32[256,1]{0,1:T(1,128)} %param.15) | copy-start | bytes 3076
  7.2 12.4 %copy-start.13 = (s32[256]{0:T(256)S(1)}, s32[256]{0:T(256)}, u32[]{:S(2)}) copy-start(s32[256]{0:T(256)} %param.16) | copy-start | bytes 3076
  7.2 12.2 %copy-start.6 = (f32[640]{0:T(1024)S(1)}, f32[640]{0:T(1024)}, u32[]{:S(2)}) copy-start(f32[640]{0:T(1024)} %param.20) | copy-start | bytes 7684
  7.2 30.9 %copy-start.7 = (f32[640]{0:T(1024)S(1)}, f32[640]{0:T(1024)}, u32[]{:S(2)}) copy-start(f32[640]{0:T(1024)} %param.21) | copy-start | bytes 7684
  7.2 111.1 %all-gather.2.cloned.1.call-start = ((), (), s32[]{:S(2)}) async-start(), calls=%async_computation.11 | async-start | bytes 6963200 | tf_op jit(solution)/shard_map/all_gather | solution.py:389
  19.3 42.1 %copy-start.8 = (bf16[16,32]{1,0:T(8,128)(2,1)S(1)}, bf16[16,32]{1,0:T(8,128)(2,1)}, u32[]{:S(2)}) copy-start(bf16[16,32]{1,0:T(8,128)(2,1)} %param.17) | copy-start | bytes 3076
  20.7 31.5 %all-to-all-start.1 = ((bf16[64,4,128]{2,1,0:T(4,128)(2,1)}), bf16[64,4,128]{2,1,0:T(4,128)(2,1)S(1)}, u32[]{:S(2)}, u32[]{:S(2)}) async-start(bf16[64,4,128]{2,1,0:T(4,128)(2,1)} %bitcast.2), calls=%async_computation.1 | async-start | bytes 131072 | tf_op jit(solution)/shard_map/all_to_all | solution.py:28
  53.2 17.7 %all-to-all-start.2 = ((bf16[8,256,128]{1,2,0:T(8,128)(2,1)}), bf16[8,256,128]{1,2,0:T(8,128)(2,1)S(1)}, u32[]{:S(2)}, u32[]{:S(2)}) async-start(bf16[8,256,128]{1,2,0:T(8,128)(2,1)} %broadcast_in_dim.57), calls=%async_computation.2 | async-start | bytes 1048576 | tf_op jit(solution)/shard_map/all_to_all | solution.py:28
  71.8 1.6 copy-start.5
  73.4 2.2 copy-start.3
  73.5 2.1 copy-start.4
  73.6 2.0 copy-start.12
  78.7 8.9 %all-to-all-start.3 = ((f32[8,2,256]{2,1,0:T(2,128)}), f32[8,2,256]{2,1,0:T(2,128)S(1)}, u32[]{:S(2)}, u32[]{:S(2)}) async-start(f32[8,2,256]{2,1,0:T(2,128)} %broadcast_in_dim.60), calls=%async_computation.3 | async-start | bytes 32768 | tf_op jit(solution)/shard_map/all_to_all | solution.py:28
  89.2 22.6 %all-to-all-start.4 = ((bf16[4,272,640]{2,1,0:T(8,128)(2,1)}), bf16[4,272,640]{2,1,0:T(8,128)(2,1)}, u32[]{:S(2)}, u32[]{:S(2)}) async-start(bf16[4,272,640]{2,1,0:T(8,128)(2,1)} %broadcast_in_dim.61), calls=%async_computation.4 | async-start | bytes 2785280 | tf_op jit(solution)/shard_map/all_to_all | solution.py:28
  95.4 1.2 copy-start.14
  96.6 18.8 %copy-start.9 = (f32[640]{0:T(1024)S(1)}, f32[640]{0:T(1024)}, u32[]{:S(2)}) copy-start(f32[640]{0:T(1024)} %param.24) | copy-start | bytes 7684
  96.6 19.4 %copy-start.10 = (f32[640]{0:T(1024)S(1)}, f32[640]{0:T(1024)}, u32[]{:S(2)}) copy-start(f32[640]{0:T(1024)} %param.23) | copy-start | bytes 7684
  96.6 21.7 %copy-start.1 = (bf16[256,640]{1,0:T(8,128)(2,1)S(1)}, bf16[256,640]{1,0:T(8,128)(2,1)}, u32[]{:S(2)}) copy-start(bf16[256,640]{1,0:T(8,128)(2,1)} %cot_ref.3) | copy-start | bytes 983044
  111.8 6.5 %collective-permute-start = (bf16[4,272,640]{2,1,0:T(8,128)(2,1)}, bf16[4,272,640]{2,1,0:T(8,128)(2,1)}, u32[]{:S(2)}, u32[]{:S(2)}) collective-permute-start(bf16[4,272,640]{2,1,0:T(8,128)(2,1)} %all-to-all-done.4.own_ref), channel_id=1, source_target_pairs={{0,1},{1,0},{2,3},{3,2},{4,5},{5,4},{6,7},{7,6},{8,9},{9,8},{10,11... | collective-permute-start | bytes 4177928 | tf_op jit(solution)/shard_map/ppermute | solution.py:360
  118.3 13.7 %copy-start.2 = (f32[1,640]{1,0:T(1,128)S(1)}, f32[1,640]{1,0:T(1,128)}, u32[]{:S(2)}) copy-start(f32[1,640]{1,0:T(1,128)} %broadcast_in_dim.51.gain_hbm.gain_ref) | copy-start | bytes 7684
  133.6 5.3 %collective-permute-start.1 = (bf16[4,256,640]{2,1,0:T(8,128)(2,1)S(1)}, bf16[4,256,640]{2,1,0:T(8,128)(2,1)S(1)}, u32[]{:S(2)}, u32[]{:S(2)}) collective-permute-start(bf16[4,256,640]{2,1,0:T(8,128)(2,1)S(1)} %get-tuple-element.42), channel_id=1, source_target_pairs={{0,1},{1,0},{2,3},{3,2},{4,5},{5,4},{6,7},{7,6},{8,9},{9,8},{10,11... | collective-permute-start | bytes 3932168 | tf_op jit(solution)/shard_map/ppermute | solution.py:360
  140.3 21.2 %all-to-all-start.6 = ((bf16[4,256,640]{2,1,0:T(8,128)(2,1)}), bf16[4,256,640]{2,1,0:T(8,128)(2,1)S(1)}, u32[]{:S(2)}, u32[]{:S(2)}) async-start(bf16[4,256,640]{2,1,0:T(8,128)(2,1)} %add_convert_fusion), calls=%async_computation.6 | async-start | bytes 2621440 | tf_op jit(solution)/shard_map/all_to_all | solution.py:28
  165.9 9.5 %all-to-all-start.7 = ((f32[8,24,128]{2,1,0:T(8,128)}), f32[8,24,128]{2,1,0:T(8,128)S(1)}, u32[]{:S(2)}, u32[]{:S(2)}) async-start(f32[8,24,128]{2,1,0:T(8,128)} %get-tuple-element.51), calls=%async_computation.7 | async-start | bytes 196608 | tf_op jit(solution)/shard_map/all_to_all | solution.py:28
  208.2 15.2 %all-to-all-start.10 = ((f32[8,24,128]{2,1,0:T(8,128)}), f32[8,24,128]{2,1,0:T(8,128)S(1)}, u32[]{:S(2)}, u32[]{:S(2)}) async-start(f32[8,24,128]{2,1,0:T(8,128)} %broadcast_in_dim.65), calls=%async_computation.10 | async-start | bytes 196608 | tf_op jit(solution)/shard_map/all_to_all | solution.py:28
Sparse Core Ops, SparseCore 0:
  19.4 93.2 all-gather.1
